TPU v7x, 512 devices: a whole 4x8x8 slice. The times are simulated.
512 devices in a mesh: stream: 8 (over y), span: 16 (over z, core), vert: 4 (over x).
Axes of the slice: x: 4, y: 8, z: 8, core: 2. Of those that a mesh axis runs over, the one named last changes fastest.
Arguments:
- fields: float32 [5, 128, 256, 1024], P(None, 'vert', 'span', 'stream'), may hold values from -6 to 6
- solid_frac: float32 [128, 256, 1024], P('vert', 'span', 'stream'), may hold values from 0 to 1
- panels: float32 [32768, 5, 256], P(('stream', 'span', 'vert')), may hold values from -0.015625 to 0.015625
- panel_owner: int32 [32768, 1], P(('stream', 'span', 'vert')), may hold values from 0 to 63; in each aligned block of 64 rows (0 to 63, 64 to 127, ...) at most 2 rows name the same one
- deck_cells: int32 [4, 16, 8, 2048], P('vert', 'span', 'stream'), may hold values from 0 to 65535
- deck_geom: float32 [4, 16, 8, 3, 2048], P('vert', None, 'stream'), may hold values from -6 to 6
- strip_ids: int32 [4, 16, 8, 2048], P('vert', None, 'stream'), may hold values from 0 to 63, as said below
- mode_shapes: float32 [3, 64, 32], replicated, may hold values from -0.0034179688 to 0.0034179688
Outputs:
- new_fields: float32 [5, 128, 256, 1024], P(None, 'vert', 'span', 'stream')
- modal_force: float32 [32], replicated
Inputs may be any that keep to these rules, and one draw needn't show every extreme that they name: `panel_owner`: tile number s * 4 + v for along-deck tile s and vertical tile v. Among the 64 panels of one device no tile is named more than 2 times; some device names some tile exactly 2 times. `strip_ids`: cells of along-deck tile s belong to strips s * 4 to (s + 1) * 4 - 1.
All inputs are finite; a program needn't handle non-finite values.
Results may differ from a plain program's by a relative error of at most 0.00012.
Values sent between devices are 32-bit elements; how exact they have to be, the bound alone decides.
No kernel may reach another device: no remote copies, remote signals or barrier semaphores. Data moves between devices by JAX's collectives and lax.ppermute only.
A program may use at most 128 MiB of HBM per device.

v0:
```python
import math

import jax
import jax.numpy as jnp
from jax import lax
from jax.sharding import PartitionSpec as P

CAP = 2


time_step = 0.15
viscous = 0.05
heat_diff = 0.03
sound_sq = 1.0
buoyant = 0.5
penalty = 0.5
relax_time = 0.5
relax_depth = 8.0
wave_cols = 16


def extended(block, sides, width):
    for axis, dim in sides:
        count = lax.axis_size(axis)
        forward = [(i, i + 1) for i in range(count - 1)]
        backward = [(target, source) for source, target in forward]
        low = lax.ppermute(
            lax.slice_in_dim(block, block.shape[dim] - width, None, axis=dim), axis, forward
        )
        high = lax.ppermute(lax.slice_in_dim(block, 0, width, axis=dim), axis, backward)
        block = jnp.concatenate([low, block, high], axis=dim)
    return block


def wave_basis(heights, widths, total_z, total_y, spec):
    modes = jnp.arange(spec, dtype=jnp.int32)
    across = (modes % wave_cols)[:, None, None]
    upward = (modes // wave_cols)[:, None, None]
    period = total_y * total_z
    phase = (
        across * widths[None, None, :] * total_z + upward * heights[None, :, None] * total_y
    ) % period
    angle = phase.astype(jnp.float32) * (2.0 * math.pi / period)
    return jnp.concatenate([jnp.cos(angle), jnp.sin(angle)], axis=0)


def relax_weights(positions, limit):
    spots = positions.astype(jnp.float32)
    return jnp.where(positions < limit, jnp.exp(-spots / relax_depth) / relax_time, 0.0)


def rates(padded, solid_frac, relax_rate, target_plane):
    centre = padded[:, 1:-1, 1:-1, 1:-1]
    east_side = padded[:, 1:-1, 1:-1, 2:]
    west_side = padded[:, 1:-1, 1:-1, :-2]
    north_side = padded[:, 1:-1, 2:, 1:-1]
    south_side = padded[:, 1:-1, :-2, 1:-1]
    upper_side = padded[:, 2:, 1:-1, 1:-1]
    lower_side = padded[:, :-2, 1:-1, 1:-1]
    grad_x = 0.5 * (east_side - west_side)
    grad_y = 0.5 * (north_side - south_side)
    grad_z = 0.5 * (upper_side - lower_side)
    laplace = (
        east_side + west_side + north_side + south_side + upper_side + lower_side - 6.0 * centre
    )
    speed_x = centre[0]
    speed_y = centre[1]
    speed_z = centre[2]
    carried = speed_x * grad_x + speed_y * grad_y + speed_z * grad_z
    coeffs = jnp.array([viscous, viscous, viscous, viscous, heat_diff], jnp.float32)[
        :, None, None, None
    ]
    damping = solid_frac / penalty
    nudging = relax_rate[None, None, None, :] * (target_plane[:, :, :, None] - centre)
    common = coeffs * laplace - carried + nudging
    extra_terms = jnp.stack(
        [
            -grad_x[3] - damping * speed_x,
            -grad_y[3] - damping * speed_y,
            -grad_z[3] - damping * speed_z + buoyant * centre[4],
            -sound_sq * (grad_x[0] + grad_y[1] + grad_z[2]),
            jnp.zeros_like(speed_x),
        ]
    )
    return common + extra_terms


def pack_slots(flat_panels, target_tile, chosen, tile_count):
    running = jnp.cumsum(chosen, axis=0) - 1
    slot_rank = jnp.sum(chosen * running, axis=1)
    slot_index = target_tile * CAP + slot_rank
    dispatch = (
        slot_index[None, :] == jnp.arange(tile_count * CAP, dtype=jnp.int32)[:, None]
    ).astype(jnp.float32)
    return jnp.dot(dispatch, flat_panels, precision=lax.Precision.HIGHEST)


def strip_forces(traction, labels, strip_count):
    columns = jnp.arange(strip_count, dtype=jnp.int32)

    def add_row(running, item_pair):
        row_values, row_labels = item_pair
        member = (row_labels[:, None] == columns[None, :]).astype(jnp.float32)
        return (running + jnp.dot(row_values, member, precision=lax.Precision.HIGHEST), None)

    start_value = jnp.zeros((traction.shape[1], strip_count), jnp.float32)
    summed, ignored = lax.scan(add_row, start_value, (traction, labels))
    return summed


def on_device(
    fields, solid_frac, panels, panel_owner, deck_cells, deck_geom, strip_ids, mode_shapes
):
    depth_cells = fields.shape[1]
    span_cells = fields.shape[2]
    wind_cells = fields.shape[3]
    n_span = lax.axis_size("span")
    n_vert = lax.axis_size("vert")
    stream_pos = lax.axis_index("stream")
    span_pos = lax.axis_index("span")
    vert_pos = lax.axis_index("vert")
    tile_count = n_span * n_vert
    held_panels = panels.shape[0]
    spec_cols = panels.shape[2]
    flat_panels = panels.reshape(held_panels, 5 * spec_cols)
    target_tile = panel_owner[:, 0]
    chosen = (target_tile[:, None] == jnp.arange(tile_count, dtype=jnp.int32)[None, :]).astype(
        jnp.int32
    )
    outgoing = pack_slots(flat_panels, target_tile, chosen, tile_count)
    arrived = lax.all_to_all(
        outgoing.reshape(tile_count, CAP * 5 * spec_cols),
        ("span", "vert"),
        split_axis=0,
        concat_axis=0,
        tiled=True,
    )
    coeffs = jnp.sum(arrived.reshape(-1, 5 * spec_cols), axis=0)
    coeffs = coeffs.reshape(5, spec_cols)
    heights = vert_pos * depth_cells + jnp.arange(depth_cells, dtype=jnp.int32)
    widths = span_pos * span_cells + jnp.arange(span_cells, dtype=jnp.int32)
    wave_table = wave_basis(
        heights, widths, depth_cells * n_vert, span_cells * n_span, spec_cols // 2
    )
    wave_table = wave_table.reshape(spec_cols, depth_cells * span_cells)
    partial_value = jnp.dot(coeffs, wave_table, precision=lax.Precision.HIGHEST)
    inflow_plane = lax.psum(partial_value, "stream").reshape(5, depth_cells, span_cells)
    target_plane = inflow_plane + jnp.array([1.0, 0.0, 0.0, 0.0, 0.0], jnp.float32)[:, None, None]
    wind_first = stream_pos * wind_cells
    relax_rate = relax_weights(
        wind_first + jnp.arange(wind_cells, dtype=jnp.int32), wind_cells // 2
    )

    def advance(state):
        padded = extended(state, (("stream", 3), ("span", 2), ("vert", 1)), 1)
        return rates(padded, solid_frac, relax_rate, target_plane)

    first_update = fields + time_step * advance(fields)
    second_rate = advance(first_update)
    new_fields = 0.5 * (fields + first_update + time_step * second_rate)
    pressure = new_fields[3].reshape(-1)
    sampled = pressure[deck_cells[0, 0, 0]]
    strip_count = mode_shapes.shape[1]
    rows_all = lax.all_gather(sampled.reshape(1, 1, 1, -1), "span", axis=1, tiled=True)
    traction = rows_all[0, :, 0][:, None, :] * deck_geom[0, :, 0]
    forces = strip_forces(traction, strip_ids[0, :, 0], strip_count)
    modal_part = jnp.einsum("cj,cjm->m", forces, mode_shapes, precision=lax.Precision.HIGHEST)
    modal_force = lax.psum(modal_part, ("stream", "vert"))
    return (new_fields, modal_force)


def solution(mesh):
    return jax.shard_map(
        on_device,
        mesh=mesh,
        in_specs=(
            P(None, "vert", "span", "stream"),
            P("vert", "span", "stream"),
            P(("stream", "span", "vert"), None, None),
            P(("stream", "span", "vert"), None),
            P("vert", "span", "stream", None),
            P("vert", None, "stream", None, None),
            P("vert", None, "stream", None),
            P(),
        ),
        out_specs=(P(None, "vert", "span", "stream"), P()),
        check_vma=False,
    )
```

profile of v0, /device:TPU:64, one launch (start us, length us, event | category | flops | bytes accessed | tf_op | source)
XLA Modules:
  0.0 263.3 jit_solution(5278629360200519969)
XLA Ops:
  0.6 2.2 fusion.52
  5.3 4.5 %collective-permute-start.1 = (f32[5,32,16,1]{1,2,3,0:T(8,128)S(1)}, f32[5,32,16,1]{1,2,3,0:T(8,128)S(1)}, u32[]{:S(2)}, u32[]{:S(2)}) collective-permute-start(f32[5,32,16,1]{1,2,3,0:T(8,128)S(1)} %copy.56), channel_id=1, source_target_pairs={{0,64},{64,128},{128,192},{192,256},{256,320},{320,384},{384,448},... | collective-permute-start | bytes 30728 | tf_op jit(solution)/shard_map/ppermute | solution.py:27
  12.2 13.3 %all-to-all-start = ((f32[64,1,2560]{2,1,0:T(1,128)}), f32[64,1,2560]{2,1,0:T(1,128)}, u32[]{:S(2)}, u32[]{:S(2)}) async-start(f32[64,1,2560]{2,1,0:T(1,128)} %all_to_all.8), calls=%async_computation | async-start | bytes 1310720 | tf_op jit(solution)/shard_map/all_to_all | solution.py:131
  26.7 1.7 fusion.46
  29.1 1.6 copy.39
  30.7 2.5 pad_maximum_fusion.39
  33.2 2.0 collective-permute-start.2
  35.2 2.3 collective-permute-start.3
  37.5 4.0 %collective-permute-done.2 = f32[5,32,1,130]{3,2,1,0:T(1,128)S(1)} collective-permute-done((f32[5,32,1,130]{3,2,1,0:T(1,128)S(1)}, f32[5,32,1,130]{3,2,1,0:T(1,128)S(1)}, u32[]{:S(2)}, u32[]{:S(2)}) %collective-permute-start.2) | collective-permute-done | bytes 83232 | tf_op jit(solution)/shard_map/ppermute | solution.py:30
  41.5 1.5 collective-permute-done.3
  44.5 4.7 %collective-permute-start.5 = (f32[5,1,18,130]{3,2,1,0:T(8,128)S(1)}, f32[5,1,18,130]{3,2,1,0:T(8,128)S(1)}, u32[]{:S(2)}, u32[]{:S(2)}) collective-permute-start(f32[5,1,18,130]{3,2,1,0:T(8,128)S(1)} %get-tuple-element.71), channel_id=1, source_target_pairs={{0,1},{1,2},{2,3},{4,5},{5,6},{6,7},{8,9},{9,10},{10,11},{12,13},{... | collective-permute-start | bytes 140408 | tf_op jit(solution)/shard_map/ppermute | solution.py:27
  51.7 3.2 %broadcast_multiply_fusion.3 = (f32[5,32,16,128]{3,2,1,0:T(8,128)S(1)}, f32[5,32,16,128]{3,2,1,0:T(8,128)S(1)}) fusion(f32[5,1,18,130]{3,2,1,0:T(8,128)S(1)} %collective-permute-done.4, f32[5,32,1,130]{3,2,1,0:T(1,128)S(1)} %collective-permute-done.2, f32[5,32,16,1]{3,2,1,0:T(8,128)S(1)} %copy.37, f32[5,32,16,128]{3,2,1,0:T(8,128)S(1)} %copy-done.1, ...), kind=kLoop, calls=%fused_computation.50 | loop fusion | flops 5242880 | bytes 4212640 | tf_op jit(solution)/shard_map/mul | solution.py:62
  58.7 2.6 %reduce = f32[64,2560]{1,0:T(8,128)S(1)} reduce(f32[64,1,2560]{2,1,0:T(1,128)} %all-to-all-done, f32[]{:T(128)} %constant.123), dimensions={1}, to_apply=%all_to_all.7.reduce_sub_computation | reduce | bytes 1310724 | tf_op jit(solution)/shard_map/all_to_all | solution.py:131
  63.1 30.8 %psum.14 = f32[5,32,16]{2,1,0:T(8,128)S(1)} all-reduce(f32[5,32,16]{2,1,0:T(8,128)S(1)} %reshape.200), channel_id=1, replica_groups=mesh['stream'=8,'span'=16,'vert'=4] {'stream'}, use_global_device_ids=true, to_apply=%region_3.4 | all-reduce | flops 2560 | bytes 20480 | tf_op jit(solution)/shard_map/psum | solution.py:147
  94.0 7.5 %multiply_add_fusion = f32[5,32,16,128]{3,2,1,0:T(8,128)S(1)} fusion(f32[5,32,16,128]{3,2,1,0:T(8,128)S(1)} %copy-done.1, f32[5,32,16,128]{3,2,1,0:T(8,128)} %broadcast_dynamic-update-slice_fusion.1, f32[5,32,16]{2,1,0:T(8,128)S(1)} %broadcast_add_fusion.1, f32[128]{0:T(128)S(1)} %compare_select_fusion.1, f32[32,16,128]{2,1,0:T(8,128)} %get-tuple-element.87, ...), kind=kLoop, calls=%fused_computation.45 | loop fusion | flops 13434880 | bytes 5009844 | tf_op jit(solution)/shard_map/add | solution.py:158
  101.5 1.9 fusion.51
  103.5 1.9 copy.44
  106.7 1.9 copy.46
  108.5 4.5 %collective-permute-start.7 = (f32[5,32,16,1]{1,2,3,0:T(8,128)S(1)}, f32[5,32,16,1]{1,2,3,0:T(8,128)S(1)}, u32[]{:S(2)}, u32[]{:S(2)}) collective-permute-start(f32[5,32,16,1]{1,2,3,0:T(8,128)S(1)} %copy.46), channel_id=1, source_target_pairs={{0,64},{64,128},{128,192},{192,256},{256,320},{320,384},{384,448},... | collective-permute-start | bytes 30728 | tf_op jit(solution)/shard_map/ppermute | solution.py:27
  113.2 1.6 copy.45
  114.8 1.6 copy.47
  116.4 2.9 %pad_maximum_fusion.36 = (f32[5,32,1,130]{3,2,1,0:T(1,128)S(1)}, f32[5,32,1,130]{3,2,1,0:T(1,128)S(1)}) fusion(f32[5,32,16,1]{3,2,1,0:T(8,128)} %copy.45, f32[5,32,16,128]{3,2,1,0:T(8,128)S(1)} %multiply_add_fusion, f32[5,32,16,1]{3,2,1,0:T(8,128)} %copy.47), kind=kLoop, calls=%fused_computation.118 | loop fusion | flops 83200 | bytes 1497600 | tf_op jit(solution)/shard_map/concatenate | solution.py:31
  119.3 2.1 collective-permute-start.8
  121.4 2.6 collective-permute-start.9
  124.2 3.8 %collective-permute-done.9 = f32[5,32,1,130]{3,2,1,0:T(1,128)S(1)} collective-permute-done((f32[5,32,1,130]{3,2,1,0:T(1,128)S(1)}, f32[5,32,1,130]{3,2,1,0:T(1,128)S(1)}, u32[]{:S(2)}, u32[]{:S(2)}) %collective-permute-start.9) | collective-permute-done | bytes 83232 | tf_op jit(solution)/shard_map/ppermute | solution.py:27
  129.5 5.0 %collective-permute-start.11 = (f32[5,1,18,130]{3,2,1,0:T(8,128)S(1)}, f32[5,1,18,130]{3,2,1,0:T(8,128)S(1)}, u32[]{:S(2)}, u32[]{:S(2)}) collective-permute-start(f32[5,1,18,130]{3,2,1,0:T(8,128)S(1)} %get-tuple-element.69), channel_id=1, source_target_pairs={{0,1},{1,2},{2,3},{4,5},{5,6},{6,7},{8,9},{9,10},{10,11},{12,13},{... | collective-permute-start | bytes 140408 | tf_op jit(solution)/shard_map/ppermute | solution.py:27
  136.9 3.1 %broadcast_multiply_fusion = (f32[5,32,16,128]{3,2,1,0:T(8,128)S(1)}, f32[5,32,16,128]{3,2,1,0:T(8,128)S(1)}) fusion(f32[5,1,18,130]{3,2,1,0:T(8,128)S(1)} %collective-permute-done.10, f32[5,32,1,130]{3,2,1,0:T(1,128)S(1)} %collective-permute-done.8, f32[5,32,16,1]{3,2,1,0:T(8,128)S(1)} %copy-done.4, f32[5,32,16,128]{3,2,1,0:T(8,128)S(1)} %multiply_add_fusion, ...), kind=kLoop, calls=%fused_computation.47 | loop fusion | flops 5242880 | bytes 4212640 | tf_op jit(solution)/shard_map/mul | solution.py:62
  140.4 5.0 %add_multiply_fusion = f32[5,32,16,128]{3,2,1,0:T(8,128)S(1)} fusion(f32[5,32,16,128]{3,2,1,0:T(8,128)S(1)} %broadcast_dynamic-update-slice_fusion, f32[5,32,16,128]{3,2,1,0:T(8,128)S(1)} %multiply_add_fusion, f32[5,32,16,128]{3,2,1,0:T(8,128)S(1)} %copy-done.1, f32[32,16,128]{2,1,0:T(8,128)S(1)} %get-tuple-element.82, ...), kind=kLoop, calls=%fused_computation.44 | loop fusion | flops 14090240 | bytes 6320564 | tf_op jit(solution)/shard_map/mul | solution.py:160
  146.5 11.8 %gather_fusion = f32[2048]{0:T(1024)S(1)} fusion(f32[65536]{0:T(1024)S(1)} %bitcast.150, s32[2048]{0:T(1024)S(1)} %broadcast_clamp_fusion), kind=kCustom, calls=%fused_computation | custom fusion | bytes 24576 | tf_op jit(solution)/shard_map/gather | solution.py:162
  158.2 16.8 %all-gather = f32[32768]{0:T(1024)S(1)} all-gather(f32[2048]{0:T(1024)S(1)} %gather_fusion), channel_id=2, replica_groups=mesh['stream'=8,'span'=16,'vert'=4] {'span'}, dimensions={0}, use_global_device_ids=true | all-gather | bytes 139264 | tf_op jit(solution)/shard_map/all_gather | solution.py:164
  175.2 10.6 %while.11 = (s32[]{:T(128)}, f32[3,64]{1,0:T(4,128)S(1)}, f32[16,3,2048]{2,0,1:T(8,128)S(1)}, s32[16,2048]{1,0:T(8,128)S(1)}, s32[]{:T(128)}, /*index=5*/s32[]{:T(128)}) while((s32[]{:T(128)}, f32[3,64]{1,0:T(4,128)S(1)}, f32[16,3,2048]{2,0,1:T(8,128)S(1)}, s32[16,2048]{1,0:T(8,128)S(1)}, s32[]{:T(128)}, /*index=5*/s32[]{:T(128)}) %tuple.46), condition=%wide.region_5.6_spmd.clone, body=%wide.region_4.5_spmd.clone.sunk | while | flops 4850051 | bytes 99927 | solution.py:107
  186.0 77.3 %psum.15 = f32[32]{0:T(128)} all-reduce(f32[32]{0:T(128)S(1)} %convolution_bitcast_fusion), channel_id=1, replica_groups=mesh['stream'=8,'span'=16,'vert'=4] {'stream','vert'}, use_global_device_ids=true, to_apply=%region_6.7 | all-reduce | flops 32 | bytes 256 | tf_op jit(solution)/shard_map/psum | solution.py:168
  (144 shorter events, 33.0 us)
Async XLA Ops:
  0.6 185.2 %copy-start = (f32[3,64,32]{1,2,0:T(8,128)S(1)}, f32[3,64,32]{1,2,0:T(8,128)}, u32[]{:S(2)}) copy-start(f32[3,64,32]{1,2,0:T(8,128)} %param.20) | copy-start | bytes 73732
  2.8 7.1 %copy-start.14 = (s32[64,1]{0,1:T(1,128)S(1)}, s32[64,1]{0,1:T(1,128)}, u32[]{:S(2)}) copy-start(s32[64,1]{0,1:T(1,128)} %param.16) | copy-start | bytes 772
  2.8 7.4 %copy-start.11 = (f32[64,5,256]{2,0,1:T(8,128)S(1)}, f32[64,5,256]{2,0,1:T(8,128)}, u32[]{:S(2)}) copy-start(f32[64,5,256]{2,0,1:T(8,128)} %param.15) | copy-start | bytes 983044
  3.4 25.0 %collective-permute-start = (f32[5,32,16,1]{1,2,3,0:T(8,128)S(1)}, f32[5,32,16,1]{1,2,3,0:T(8,128)S(1)}, u32[]{:S(2)}, u32[]{:S(2)}) collective-permute-start(f32[5,32,16,1]{1,2,3,0:T(8,128)S(1)} %copy.55), channel_id=1, source_target_pairs={{64,0},{128,64},{192,128},{256,192},{320,256},{384,320},{448,384},... | collective-permute-start | bytes 30728 | tf_op jit(solution)/shard_map/ppermute | solution.py:30
  5.3 23.7 %collective-permute-start.1 = (f32[5,32,16,1]{1,2,3,0:T(8,128)S(1)}, f32[5,32,16,1]{1,2,3,0:T(8,128)S(1)}, u32[]{:S(2)}, u32[]{:S(2)}) collective-permute-start(f32[5,32,16,1]{1,2,3,0:T(8,128)S(1)} %copy.56), channel_id=1, source_target_pairs={{0,64},{64,128},{128,192},{192,256},{256,320},{320,384},{384,448},... | collective-permute-start | bytes 30728 | tf_op jit(solution)/shard_map/ppermute | solution.py:27
  10.7 14.8 %copy-start.1 = (f32[5,32,16,128]{3,2,1,0:T(8,128)S(1)}, f32[5,32,16,128]{3,2,1,0:T(8,128)}, u32[]{:S(2)}) copy-start(f32[5,32,16,128]{3,2,1,0:T(8,128)} %param.13) | copy-start | bytes 3932164
  12.2 14.2 %copy-start.13 = (s32[1,1,1,2048]{3,2,1,0:T(1,128)S(1)}, s32[1,1,1,2048]{3,2,1,0:T(1,128)}, u32[]{:S(2)}) copy-start(s32[1,1,1,2048]{3,2,1,0:T(1,128)} %param.17) | copy-start | bytes 24580
  12.2 46.5 %all-to-all-start = ((f32[64,1,2560]{2,1,0:T(1,128)}), f32[64,1,2560]{2,1,0:T(1,128)}, u32[]{:S(2)}, u32[]{:S(2)}) async-start(f32[64,1,2560]{2,1,0:T(1,128)} %all_to_all.8), calls=%async_computation | async-start | bytes 1310720 | tf_op jit(solution)/shard_map/all_to_all | solution.py:131
  29.1 22.7 %copy-start.2 = (f32[5,32,16,1]{3,2,1,0:T(8,128)}, f32[5,32,16,1]{3,2,1,0:T(8,128)S(1)}, u32[]{:S(2)}) copy-start(f32[5,32,16,1]{3,2,1,0:T(8,128)S(1)} %copy.37) | copy-start | bytes 30724
  30.7 12.4 %copy-start.3 = (f32[5,32,16,1]{3,2,1,0:T(8,128)S(1)}, f32[5,32,16,1]{3,2,1,0:T(8,128)}, u32[]{:S(2)}) copy-start(f32[5,32,16,1]{3,2,1,0:T(8,128)} %copy.39) | copy-start | bytes 30724
  33.2 8.4 %collective-permute-start.2 = (f32[5,32,1,130]{3,2,1,0:T(1,128)S(1)}, f32[5,32,1,130]{3,2,1,0:T(1,128)S(1)}, u32[]{:S(2)}, u32[]{:S(2)}) collective-permute-start(f32[5,32,1,130]{3,2,1,0:T(1,128)S(1)} %get-tuple-element.80), channel_id=1, source_target_pairs={{4,0},{8,4},{12,8},{16,12},{20,16},{24,20},{28,24},{32,28},{36,32}... | collective-permute-start | bytes 249608 | tf_op jit(solution)/shard_map/ppermute | solution.py:30
  35.2 7.9 %collective-permute-start.3 = (f32[5,32,1,130]{3,2,1,0:T(1,128)S(1)}, f32[5,32,1,130]{3,2,1,0:T(1,128)S(1)}, u32[]{:S(2)}, u32[]{:S(2)}) collective-permute-start(f32[5,32,1,130]{3,2,1,0:T(1,128)S(1)} %get-tuple-element.79), channel_id=1, source_target_pairs={{0,4},{4,8},{8,12},{12,16},{16,20},{20,24},{24,28},{28,32},{32,36}... | collective-permute-start | bytes 249608 | tf_op jit(solution)/shard_map/ppermute | solution.py:27
  43.2 7.3 %collective-permute-start.4 = (f32[5,1,18,130]{3,2,1,0:T(8,128)S(1)}, f32[5,1,18,130]{3,2,1,0:T(8,128)S(1)}, u32[]{:S(2)}, u32[]{:S(2)}) collective-permute-start(f32[5,1,18,130]{3,2,1,0:T(8,128)S(1)} %get-tuple-element.72), channel_id=1, source_target_pairs={{1,0},{2,1},{3,2},{5,4},{6,5},{7,6},{9,8},{10,9},{11,10},{13,12},{... | collective-permute-start | bytes 140408 | tf_op jit(solution)/shard_map/ppermute | solution.py:30
  44.5 7.2 %collective-permute-start.5 = (f32[5,1,18,130]{3,2,1,0:T(8,128)S(1)}, f32[5,1,18,130]{3,2,1,0:T(8,128)S(1)}, u32[]{:S(2)}, u32[]{:S(2)}) collective-permute-start(f32[5,1,18,130]{3,2,1,0:T(8,128)S(1)} %get-tuple-element.71), channel_id=1, source_target_pairs={{0,1},{1,2},{2,3},{4,5},{5,6},{6,7},{8,9},{9,10},{10,11},{12,13},{... | collective-permute-start | bytes 140408 | tf_op jit(solution)/shard_map/ppermute | solution.py:27
  50.4 4.5 %copy-start.6 = (f32[32,16,128]{2,1,0:T(8,128)S(1)}, f32[32,16,128]{2,1,0:T(8,128)}, u32[]{:S(2)}) copy-start(f32[32,16,128]{2,1,0:T(8,128)} %param.14) | copy-start | bytes 786436
  50.5 4.4 %copy-start.8 = (f32[5,1,18,130]{3,2,1,0:T(8,128)}, f32[5,1,18,130]{3,2,1,0:T(8,128)S(1)}, u32[]{:S(2)}) copy-start(f32[5,1,18,130]{3,2,1,0:T(8,128)S(1)} %collective-permute-done.4) | copy-start | bytes 140404
  51.7 3.2 %copy-start.9 = (f32[5,1,18,130]{3,2,1,0:T(8,128)}, f32[5,1,18,130]{3,2,1,0:T(8,128)S(1)}, u32[]{:S(2)}) copy-start(f32[5,1,18,130]{3,2,1,0:T(8,128)S(1)} %collective-permute-done.5) | copy-start | bytes 140404
  61.3 32.6 %copy-start.16 = (f32[5]{0:T(128)S(1)}, f32[5]{0:T(128)}, u32[]{:S(2)}) copy-start(f32[5]{0:T(128)} %constant.116.clone) | copy-start | bytes 64
  61.4 32.6 %copy-start.15 = (f32[5]{0:T(128)S(1)}, f32[5]{0:T(128)}, u32[]{:S(2)}) copy-start(f32[5]{0:T(128)} %constant.117.clone) | copy-start | bytes 64
  103.5 9.7 %copy-start.12 = (s32[1,16,1,2048]{3,2,1,0:T(1,128)S(1)}, s32[1,16,1,2048]{3,2,1,0:T(1,128)}, u32[]{:S(2)}) copy-start(s32[1,16,1,2048]{3,2,1,0:T(1,128)} %param.19) | copy-start | bytes 393220
  105.4 7.8 %collective-permute-start.6 = (f32[5,32,16,1]{1,2,3,0:T(8,128)S(1)}, f32[5,32,16,1]{1,2,3,0:T(8,128)S(1)}, u32[]{:S(2)}, u32[]{:S(2)}) collective-permute-start(f32[5,32,16,1]{1,2,3,0:T(8,128)S(1)} %copy.44), channel_id=1, source_target_pairs={{64,0},{128,64},{192,128},{256,192},{320,256},{384,320},{448,384},... | collective-permute-start | bytes 30728 | tf_op jit(solution)/shard_map/ppermute | solution.py:30
  108.5 6.3 %collective-permute-start.7 = (f32[5,32,16,1]{1,2,3,0:T(8,128)S(1)}, f32[5,32,16,1]{1,2,3,0:T(8,128)S(1)}, u32[]{:S(2)}, u32[]{:S(2)}) collective-permute-start(f32[5,32,16,1]{1,2,3,0:T(8,128)S(1)} %copy.46), channel_id=1, source_target_pairs={{0,64},{64,128},{128,192},{192,256},{256,320},{320,384},{384,448},... | collective-permute-start | bytes 30728 | tf_op jit(solution)/shard_map/ppermute | solution.py:27
  116.4 11.6 %copy-start.5 = (f32[5,32,16,1]{3,2,1,0:T(8,128)S(1)}, f32[5,32,16,1]{3,2,1,0:T(8,128)}, u32[]{:S(2)}) copy-start(f32[5,32,16,1]{3,2,1,0:T(8,128)} %copy.47) | copy-start | bytes 30724
  119.3 8.7 %copy-start.4 = (f32[5,32,16,1]{3,2,1,0:T(8,128)S(1)}, f32[5,32,16,1]{3,2,1,0:T(8,128)}, u32[]{:S(2)}) copy-start(f32[5,32,16,1]{3,2,1,0:T(8,128)} %copy.45) | copy-start | bytes 30724
  119.3 4.9 %collective-permute-start.8 = (f32[5,32,1,130]{3,2,1,0:T(1,128)S(1)}, f32[5,32,1,130]{3,2,1,0:T(1,128)S(1)}, u32[]{:S(2)}, u32[]{:S(2)}) collective-permute-start(f32[5,32,1,130]{3,2,1,0:T(1,128)S(1)} %get-tuple-element.76), channel_id=1, source_target_pairs={{4,0},{8,4},{12,8},{16,12},{20,16},{24,20},{28,24},{32,28},{36,32}... | collective-permute-start | bytes 249608 | tf_op jit(solution)/shard_map/ppermute | solution.py:30
  121.4 6.6 %collective-permute-start.9 = (f32[5,32,1,130]{3,2,1,0:T(1,128)S(1)}, f32[5,32,1,130]{3,2,1,0:T(1,128)S(1)}, u32[]{:S(2)}, u32[]{:S(2)}) collective-permute-start(f32[5,32,1,130]{3,2,1,0:T(1,128)S(1)} %get-tuple-element.75), channel_id=1, source_target_pairs={{0,4},{4,8},{8,12},{12,16},{16,20},{20,24},{24,28},{28,32},{32,36}... | collective-permute-start | bytes 249608 | tf_op jit(solution)/shard_map/ppermute | solution.py:27
  128.2 7.4 %collective-permute-start.10 = (f32[5,1,18,130]{3,2,1,0:T(8,128)S(1)}, f32[5,1,18,130]{3,2,1,0:T(8,128)S(1)}, u32[]{:S(2)}, u32[]{:S(2)}) collective-permute-start(f32[5,1,18,130]{3,2,1,0:T(8,128)S(1)} %get-tuple-element.70), channel_id=1, source_target_pairs={{1,0},{2,1},{3,2},{5,4},{6,5},{7,6},{9,8},{10,9},{11,10},{13,12},{... | collective-permute-start | bytes 140408 | tf_op jit(solution)/shard_map/ppermute | solution.py:30
  129.5 7.4 %collective-permute-start.11 = (f32[5,1,18,130]{3,2,1,0:T(8,128)S(1)}, f32[5,1,18,130]{3,2,1,0:T(8,128)S(1)}, u32[]{:S(2)}, u32[]{:S(2)}) collective-permute-start(f32[5,1,18,130]{3,2,1,0:T(8,128)S(1)} %get-tuple-element.69), channel_id=1, source_target_pairs={{0,1},{1,2},{2,3},{4,5},{5,6},{6,7},{8,9},{9,10},{10,11},{12,13},{... | collective-permute-start | bytes 140408 | tf_op jit(solution)/shard_map/ppermute | solution.py:27
  145.4 1.1 copy-start.7
  146.4 28.6 %copy-start.10 = (f32[1,16,1,3,2048]{4,2,3,1,0:T(1,128)S(1)}, f32[1,16,1,3,2048]{4,2,3,1,0:T(1,128)}, u32[]{:S(2)}) copy-start(f32[1,16,1,3,2048]{4,2,3,1,0:T(1,128)} %param.18) | copy-start | bytes 1179652
where the time goes:
time: 264 us; the launch traced here: 263 us
  blocking collectives  125 us (47%)
  starting transfers between devices  46.3 us (18%)
  other arithmetic  36.1 us (14%)
  local copies, waits for them, and re-layouts  30.7 us (12%)
  waiting for transfers between devices  12.1 us (5%)
  matrix products  11.3 us (4%)
    psum x1, blocking collectives, on_device(): modal_force = lax.psum(modal_part, ('stream', 'vert'))  77.3 us
    psum x1, blocking collectives, on_device(): lax.psum(partial_value, 'stream').reshape(5, depth_cells, span_cells)  30.8 us
    ppermute x6, starting transfers between devices, extended(): lax.ppermute(lax.slice_in_dim(block, block.shape[dim] - width, None, axis...  23.8 us
    all_gather x1, blocking collectives, on_device(): lax.all_gather(sampled.reshape(1, 1, 1, -1), 'span', axis=1, tiled=True)  16.8 us
    all_to_all x1, starting transfers between devices, on_device(): lax.all_to_all(outgoing.reshape(tile_count, CAP * 5 * spec_cols), ('span'...  13.3 us
    gather x1, local copies, waits for them, and re-layouts, on_device(): sampled = pressure[deck_cells[0, 0, 0]]  11.8 us
    dot_general x16, matrix products, add_row(): jnp.dot(row_values, member, precision=lax.Precision.HIGHEST)  9.31 us
    ppermute x6, starting transfers between devices, extended(): lax.ppermute(lax.slice_in_dim(block, 0, width, axis=dim), axis, backward)  9.23 us
  transfers between devices with their start and end apart: 13, of which 7 were waited for; matrix products, arithmetic and copies ran while one was open for 8% of the time, Pallas kernels for 0%

commit v1 on v0

v1 whole, which is shorter than its diff:
```python
import math

import jax
import jax.numpy as jnp
import numpy as np
from jax import lax
from jax.experimental import pallas as pl
from jax.experimental.pallas import tpu as pltpu
from jax.sharding import PartitionSpec as P

time_step = 0.15
viscous = 0.05
heat_diff = 0.03
sound_sq = 1.0
buoyant = 0.5
penalty = 0.5
relax_time = 0.5
relax_depth = 8.0
wave_cols = 16

HI = lax.Precision.HIGHEST
NF = 5
ROWS = 16


def mdot(a, b, dims):
    return lax.dot_general(
        a, b, (dims, ((), ())), precision=HI, preferred_element_type=jnp.float32
    )


def wave_tables(cz, cy, n_span, n_vert, spec):
    modes = np.arange(spec)
    across = (modes % wave_cols).astype(np.float64)
    upward = (modes // wave_cols).astype(np.float64)
    ny, nz = cy * n_span, cz * n_vert

    def basis(z, y):
        turn = across[None] * y[:, None] / ny + upward[None] * z[:, None] / nz
        angle = 2.0 * math.pi * turn
        return np.concatenate([np.cos(angle), np.sin(angle)], axis=1)

    z, y = np.arange(cz, dtype=np.float64), np.arange(cy, dtype=np.float64)
    plane = basis(np.repeat(z, cy), np.tile(y, cz)).astype(np.float32)
    edges = np.zeros((2 * spec, 128), np.float64)
    at = 0
    for part in (
        basis(z, 0 * z + cy - 1),
        basis(z, 0 * z),
        basis(0 * y + cz - 1, y),
        basis(0 * y, y),
    ):
        edges[:, at : at + part.shape[0]] = part.T
        at += part.shape[0]
    s, v = np.repeat(np.arange(n_span), n_vert), np.tile(np.arange(n_vert), n_span)
    turn = basis(1.0 * v * cz, 1.0 * s * cy).astype(np.float32)
    return plane, edges.astype(np.float32), turn


def sum_panels(n_vert, panels, owner, turn, edge_table, out):
    tiles = turn.shape[0]
    spec = turn.shape[1] // 2
    held = owner.shape[0]
    named = (owner[...] == lax.broadcasted_iota(jnp.int32, (held, tiles), 1)).astype(jnp.float32)
    cos_t, sin_t = turn[:, :spec], turn[:, spec:]
    lane = lax.broadcasted_iota(jnp.int32, (tiles, 128), 1)
    for f in range(NF):
        total = mdot(named, panels[:, f, :], ((0,), (0,)))
        c, s = total[:, :spec], total[:, spec:]
        c2 = c * cos_t + s * sin_t
        s2 = s * cos_t - c * sin_t
        out[pl.ds(f, tiles, stride=ROWS), :] = c2
        out[pl.ds(8 + f, tiles, stride=ROWS), :] = s2
        e = mdot(c2, edge_table[:spec, :], ((1,), (0,))) + mdot(
            s2, edge_table[spec:, :], ((1,), (0,))
        )
        row = jnp.where(
            lane < 32,
            jnp.roll(e, n_vert, 0),
            jnp.where(
                lane < 64,
                jnp.roll(e, -n_vert, 0),
                jnp.where(lane < 80, jnp.roll(e, 1, 0), jnp.roll(e, -1, 0)),
            ),
        )
        at = 5 + f if f < 3 else 10 + f
        out[pl.ds(at, tiles, stride=ROWS), :] = row
    out[pl.ds(15, tiles, stride=ROWS), :] = jnp.zeros((tiles, 128), jnp.float32)


def sum_sources(got, out):
    tiles = got.shape[0]
    total = jnp.sum(got[...], axis=0)
    for i in range(out.shape[0]):
        out[i] = total


def lane_ids(shape):
    return lax.broadcasted_iota(jnp.int32, shape, len(shape) - 1)


def packed_x(acc, v, z):
    lane = lane_ids((8, 128))
    for h in range(2):
        k = 2 * z + h
        acc = jnp.where((lane >> 1) == k, pltpu.roll(v[8 * h : 8 * h + 8], 2 * k + 1, 1), acc)
    return acc


def pack_faces(fields, xf, ylo, yhi, zlo, zhi):
    cz = fields.shape[1]

    def body(z, accs):
        return tuple(packed_x(accs[f], fields[f, z], z) for f in range(NF))

    zero = jnp.zeros((8, 128), jnp.float32)
    accs = lax.fori_loop(0, cz, body, (zero,) * NF, unroll=4)
    for f in range(NF):
        xf[f] = accs[f]
    store_faces(fields, ylo, yhi, zlo, zhi)


def store_faces(state, ylo, yhi, zlo, zhi):
    cz, cy = state.shape[1], state.shape[2]
    for f in range(NF):
        ylo[f] = state[f, :, 0, :]
        yhi[f] = state[f, :, cy - 1, :]
        zlo[f] = state[f, 0]
        zhi[f] = state[f, cz - 1]


def ghosts_x(xw, xe):
    lane = lane_ids((8, 128))
    return [jnp.where((lane & 1) == 0, xw[f], pltpu.roll(xe[f], 126, 1)) for f in range(NF)]


def slab_rates(q, xg, damp, relax, z):
    lane = lane_ids((16, 128))
    cs, gx, gy, gz, lap = [], [], [], [], []
    for f in range(NF):
        c = q[f, z + 1, 8:24, :]
        up, down = q[f, z + 2, 8:24, :], q[f, z, 8:24, :]
        north, south = q[f, z + 1, 9:25, :], q[f, z + 1, 7:23, :]
        side = jnp.concatenate(
            [
                pltpu.roll(xg[f], (128 - 4 * z) & 127, 1),
                pltpu.roll(xg[f], (126 - 4 * z) & 127, 1),
            ],
            axis=0,
        )
        west = jnp.where(lane == 0, side, pltpu.roll(c, 1, 1))
        east = jnp.where(lane == 127, side, pltpu.roll(c, 127, 1))
        cs.append(c)
        gx.append(0.5 * (east - west))
        gy.append(0.5 * (north - south))
        gz.append(0.5 * (up - down))
        lap.append(east + west + north + south + up + down - 6.0 * c)
    u, v, w = cs[0], cs[1], cs[2]
    out = []
    for f in range(NF):
        nu = heat_diff if f == 4 else viscous
        r = nu * lap[f] - (u * gx[f] + v * gy[f] + w * gz[f]) - relax * cs[f]
        if f == 0:
            r = r - gx[3] - damp * u
        elif f == 1:
            r = r - gy[3] - damp * v
        elif f == 2:
            r = r - gz[3] - damp * w + buoyant * cs[4]
        elif f == 3:
            r = r - sound_sq * (gx[0] + gy[1] + gz[2])
        out.append(r)
    return cs, out


def first_step(fields, solid, xw, xe, ys, yn, zd, zu, relax, base, xf, ylo, yhi, zlo, zhi, q):
    cz = fields.shape[1]
    for f in range(NF):
        q[f, 1 : cz + 1, 7, :] = ys[f]
        q[f, 1 : cz + 1, 24, :] = yn[f]
        q[f, 0, 8:24, :] = zd[f]
        q[f, cz + 1, 8:24, :] = zu[f]

    def fill(z, carry):
        for f in range(NF):
            q[f, z + 1, 8:24, :] = fields[f, z]
        return carry

    lax.fori_loop(0, cz, fill, 0, unroll=4)
    xg = ghosts_x(xw, xe)
    relax_row = relax[...]

    def body(z, accs):
        damp = solid[z] * (1.0 / penalty)
        cs, rs = slab_rates(q, xg, damp, relax_row, z)
        new = []
        for f in range(NF):
            b = cs[f] + time_step * rs[f]
            base[f, z] = b
            new.append(packed_x(accs[f], b, z))
        return tuple(new)

    zero = jnp.zeros((8, 128), jnp.float32)
    accs = lax.fori_loop(0, cz, body, (zero,) * NF)
    for f in range(NF):
        xf[f] = accs[f]
    store_faces(base, ylo, yhi, zlo, zhi)


def second_step(
    flags,
    coeffs,
    plane_table,
    fields,
    base,
    solid,
    xw,
    xe,
    ys,
    yn,
    zd,
    zu,
    relax,
    cells,
    geom,
    strips,
    shapes,
    out,
    modal,
    q,
    target,
    geom_v,
    strips_v,
    sems,
):
    cz, cy = fields.shape[1], fields.shape[2]
    spec = plane_table.shape[1] // 2
    span_pos = flags[0]
    get_geom = pltpu.make_async_copy(geom.at[0, span_pos, 0], geom_v, sems.at[0])
    get_strips = pltpu.make_async_copy(strips.at[0, span_pos], strips_v, sems.at[1])
    get_geom.start()
    get_strips.start()
    chunk = coeffs[0]
    for i in range(1, coeffs.shape[0]):
        chunk = chunk + coeffs[i]
    low, high = chunk[0:8], chunk[8:16]
    one = jnp.where(lane_ids((1, 8)) == 0, 1.0, 0.0)
    target[...] = (
        mdot(plane_table[:, :spec], low, ((1,), (1,)))
        + mdot(plane_table[:, spec:], high, ((1,), (1,)))
        + one
    )
    n_edge = 2 * cz + 2 * cy
    pick = (
        lax.broadcasted_iota(jnp.int32, (n_edge, 128), 0) == lane_ids((n_edge, 128))
    ).astype(jnp.float32)
    e_low = mdot(pick, low, ((1,), (1,)))
    e_high = mdot(pick, high, ((1,), (1,)))
    relax_row = relax[...]
    push = time_step * relax_row
    for f in range(NF):
        col = e_low[:, 5 + f : 6 + f] if f < 3 else e_high[:, 2 + f : 3 + f]
        if f == 0:
            col = col + 1.0
        col = col * push

        def masked(part, flag):
            return jnp.where(flags[flag] > 0, part, 0.0)

        q[f, 1 : cz + 1, 7, :] = ys[f] + masked(col[0:cz], 1)
        q[f, 1 : cz + 1, 24, :] = yn[f] + masked(col[cz : 2 * cz], 2)
        q[f, 0, 8:24, :] = zd[f] + masked(col[2 * cz : 2 * cz + cy], 3)
        q[f, cz + 1, 8:24, :] = zu[f] + masked(col[2 * cz + cy :], 4)

    def fill(z, carry):
        t = target[pl.ds(pl.multiple_of(z * cy, cy), cy), :]
        for f in range(NF):
            q[f, z + 1, 8:24, :] = base[f, z] + push * t[:, f : f + 1]
        return carry

    lax.fori_loop(0, cz, fill, 0, unroll=2)
    xg = ghosts_x(xw, xe)

    def body(z, carry):
        damp = solid[z] * (1.0 / penalty)
        t = target[pl.ds(pl.multiple_of(z * cy, cy), cy), :]
        cs, rs = slab_rates(q, xg, damp, relax_row, z)
        for f in range(NF):
            r = rs[f] + relax_row * t[:, f : f + 1]
            out[f, z] = 0.5 * (fields[f, z] + cs[f] + time_step * r)
        return carry

    lax.fori_loop(0, cz, body, 0)

    pressure = jnp.reshape(out[3], (cz * cy, 128))
    p_hi = pressure.astype(jnp.bfloat16)
    rest = pressure - p_hi.astype(jnp.float32)
    p_mid = rest.astype(jnp.bfloat16)
    p_lo = (rest - p_mid.astype(jnp.float32)).astype(jnp.bfloat16)
    get_geom.wait()
    get_strips.wait()
    count = cells.shape[1]
    step = 512
    forces = jnp.zeros((8, shapes.shape[1]), jnp.float32)
    for at in range(0, count, step):
        where = cells[:, at : at + step]
        rows = lax.broadcasted_iota(jnp.int32, (cz * cy, step), 0)
        hit = jnp.where(rows == (where >> 7), 1.0, 0.0).astype(jnp.bfloat16)
        picked = jnp.zeros((128, step), jnp.float32)
        for part in (p_hi, p_mid, p_lo):
            picked = picked + lax.dot_general(
                part, hit, (((0,), (0,)), ((), ())), preferred_element_type=jnp.float32
            )
        lanes = lax.broadcasted_iota(jnp.int32, (128, step), 0)
        sample = jnp.sum(jnp.where(lanes == (where & 127), picked, 0.0), axis=0, keepdims=True)
        traction = sample * geom_v[:, at : at + step]
        traction = jnp.concatenate(
            [traction, jnp.zeros((8 - traction.shape[0], step), jnp.float32)], axis=0
        )
        strip = lax.broadcasted_iota(jnp.int32, (shapes.shape[1], step), 0)
        member = jnp.where(strip == strips_v[:, at : at + step], 1.0, 0.0)
        forces = forces + mdot(traction, member, ((1,), (1,)))
    total = jnp.zeros((1, shapes.shape[2]), jnp.float32)
    for c in range(shapes.shape[0]):
        total = total + mdot(forces[c : c + 1], shapes[c], ((1,), (0,)))
    total = jnp.concatenate(
        [total, jnp.zeros((1, 128 - shapes.shape[2]), jnp.float32)], axis=1
    )
    modal[...] = jnp.broadcast_to(total, modal.shape)


def f32(*shape):
    return jax.ShapeDtypeStruct(shape, jnp.float32)


VM = pl.BlockSpec(memory_space=pltpu.VMEM)
SM = pl.BlockSpec(memory_space=pltpu.SMEM)
AN = pl.BlockSpec(memory_space=pl.ANY)
BIG = pltpu.CompilerParams(vmem_limit_bytes=40 * 1024 * 1024)


def swap_faces(faces):
    xf, ylo, yhi, zlo, zhi = faces

    def moved(block, axis, up):
        count = lax.axis_size(axis)
        pairs = [(i, i + 1) for i in range(count - 1)]
        if not up:
            pairs = [(b, a) for a, b in pairs]
        return lax.ppermute(block, axis, pairs)

    return (
        moved(xf, "stream", True),
        moved(xf, "stream", False),
        moved(yhi, "span", True),
        moved(ylo, "span", False),
        moved(zhi, "vert", True),
        moved(zlo, "vert", False),
    )


def on_device(
    fields, solid_frac, panels, panel_owner, deck_cells, deck_geom, strip_ids, mode_shapes
):
    cz, cy, cx = fields.shape[1:]
    n_stream = lax.axis_size("stream")
    n_span = lax.axis_size("span")
    n_vert = lax.axis_size("vert")
    stream_pos = lax.axis_index("stream")
    span_pos = lax.axis_index("span")
    vert_pos = lax.axis_index("vert")
    tiles = n_span * n_vert
    spec = panels.shape[2] // 2
    plane, edges, turn = wave_tables(cz, cy, n_span, n_vert, spec)
    spots = np.arange(cx)
    relax_np = np.where(spots < cx // 2, np.exp(-spots / relax_depth) / relax_time, 0.0)
    relax = jnp.where(stream_pos == 0, jnp.asarray(relax_np, jnp.float32), 0.0).reshape(1, cx)
    flags = jnp.stack(
        [
            span_pos,
            (span_pos > 0).astype(jnp.int32),
            (span_pos < n_span - 1).astype(jnp.int32),
            (vert_pos > 0).astype(jnp.int32),
            (vert_pos < n_vert - 1).astype(jnp.int32),
        ]
    ).astype(jnp.int32)

    def panel_kernel(*refs):
        sum_panels(n_vert, *refs)

    sent = pl.pallas_call(
        panel_kernel,
        out_shape=f32(tiles * ROWS, 128),
        in_specs=[VM] * 4,
        out_specs=VM,
        compiler_params=BIG,
        name="panel_sums",
    )(panels, panel_owner, jnp.asarray(turn), jnp.asarray(edges))
    got = lax.all_to_all(
        sent.reshape(tiles, ROWS, 128), ("span", "vert"), 0, 0, tiled=True
    )
    face_shapes = (
        f32(NF, 8, 128),
        f32(NF, cz, cx),
        f32(NF, cz, cx),
        f32(NF, cy, cx),
        f32(NF, cy, cx),
    )
    faces = pl.pallas_call(
        pack_faces,
        out_shape=face_shapes,
        in_specs=[VM],
        out_specs=(VM,) * 5,
        compiler_params=BIG,
        name="pack_faces",
    )(fields)
    ghosts = swap_faces(faces)
    scratch = pltpu.VMEM((NF, cz + 2, 32, cx), jnp.float32)
    base, *faces = pl.pallas_call(
        first_step,
        out_shape=(f32(NF, cz, cy, cx),) + face_shapes,
        in_specs=[VM] * 9,
        out_specs=(VM,) * 6,
        scratch_shapes=[scratch],
        compiler_params=BIG,
        name="first_step",
    )(fields, solid_frac, *ghosts, relax)
    ghosts = swap_faces(faces)
    summed = pl.pallas_call(
        sum_sources,
        out_shape=f32(n_stream, ROWS, 128),
        in_specs=[VM],
        out_specs=VM,
        compiler_params=BIG,
        name="sum_sources",
    )(got)
    coeffs = lax.all_to_all(summed, "stream", 0, 0, tiled=True)
    deck = deck_cells.shape[3]
    new_fields, modal = pl.pallas_call(
        second_step,
        out_shape=(f32(NF, cz, cy, cx), f32(tiles, 128)),
        in_specs=[SM] + [VM] * 13 + [AN, AN, VM],
        out_specs=(VM, VM),
        scratch_shapes=[
            scratch,
            pltpu.VMEM((cz * cy, 8), jnp.float32),
            pltpu.VMEM((3, deck), jnp.float32),
            pltpu.VMEM((1, deck), jnp.int32),
            pltpu.SemaphoreType.DMA((2,)),
        ],
        compiler_params=BIG,
        name="second_step",
    )(
        flags,
        coeffs,
        jnp.asarray(plane),
        fields,
        base,
        solid_frac,
        *ghosts,
        relax,
        deck_cells.reshape(1, deck),
        deck_geom,
        strip_ids,
        mode_shapes,
    )
    part = lax.all_to_all(modal, ("span", "vert"), 0, 0, tiled=True)
    part = jnp.broadcast_to(jnp.sum(part, axis=0, keepdims=True), (n_stream, 128))
    part = lax.all_to_all(part, "stream", 0, 0, tiled=True)
    modal_force = jnp.sum(part, axis=0)[: mode_shapes.shape[2]]
    return (new_fields, modal_force)


def solution(mesh):
    return jax.shard_map(
        on_device,
        mesh=mesh,
        in_specs=(
            P(None, "vert", "span", "stream"),
            P("vert", "span", "stream"),
            P(("stream", "span", "vert"), None, None),
            P(("stream", "span", "vert"), None),
            P("vert", "span", "stream", None),
            P("vert", None, "stream", None, None),
            P("vert", None, "stream", None),
            P(),
        ),
        out_specs=(P(None, "vert", "span", "stream"), P()),
        check_vma=False,
    )
```

time: 264 us -> 130 us (0.49)
  the two profiles are of different devices: /device:TPU:64 before, /device:TPU:1 now
where the time goes in v1:
time: 130 us; the launch traced here: 129 us
  starting transfers between devices  54.8 us (42%)
  blocking collectives  35.8 us (28%)
  Pallas kernels  22.1 us (17%)
  local copies, waits for them, and re-layouts  11.2 us (9%)
  waiting for transfers between devices  3.84 us (3%)
    ppermute x12, starting transfers between devices, moved(): return lax.ppermute(block, axis, pairs)  33 us
    all_to_all x1, blocking collectives, on_device(): part = lax.all_to_all(modal, ('span', 'vert'), 0, 0, tiled=True)  21 us
    all_to_all x1, starting transfers between devices, on_device(): lax.all_to_all(sent.reshape(tiles, ROWS, 128), ('span', 'vert'), 0, 0, ti...  15 us
    all_to_all x1, blocking collectives, on_device(): part = lax.all_to_all(part, 'stream', 0, 0, tiled=True)  14.8 us
    unnamed x34, local copies, waits for them, and re-layouts  11.1 us
    pallas_call x1, Pallas kernels, on_device(): pl.pallas_call(second_step, out_shape=(f32(NF, cz, cy, cx), f32(tiles, 12...  10.8 us
    pallas_call x1, Pallas kernels, on_device(): pl.pallas_call(first_step, out_shape=(f32(NF, cz, cy, cx),) + face_shapes...  7.11 us
    all_to_all x1, starting transfers between devices, on_device(): coeffs = lax.all_to_all(summed, 'stream', 0, 0, tiled=True)  6.82 us
  transfers between devices with their start and end apart: 14, of which 2 were waited for; matrix products, arithmetic and copies ran while one was open for 1% of the time, Pallas kernels for 7%

profile of v1, /device:TPU:1, one launch (start us, length us, event | category | flops | bytes accessed | tf_op | source)
XLA Modules:
  0.0 129.3 jit_solution(15735967191745761235)
XLA Ops:
  0.6 0.7 copy.29.refs_1_
  1.4 1.2 copy.28.refs_0_
  2.6 0.9 copy-done.4
  3.5 0.8 copy-done.5
  4.3 2.5 %panel_sums.1 = f32[1024,128]{1,0:T(8,128)} custom-call(f32[64,5,256]{2,1,0:T(8,128)S(1)} %copy.28.refs_0_, s32[64,1]{1,0:T(8,128)S(1)} %copy.29.refs_1_, f32[64,256]{1,0:T(8,128)S(1)} %copy-done.5, f32[256,128]{1,0:T(8,128)S(1)} %copy-done.4), custom_call_target="tpu_custom_call" | custom-call | tf_op jit(solution)/shard_map/panel_sums/pallas_call | solution.py:390
  6.9 15.0 %all-to-all-start = ((f32[64,16,128]{2,1,0:T(8,128)}), f32[64,16,128]{2,1,0:T(8,128)S(1)}, u32[]{:S(2)}, u32[]{:S(2)}) async-start(f32[64,16,128]{2,1,0:T(8,128)} %bitcast.5), calls=%async_computation | async-start | bytes 1048576 | tf_op jit(solution)/shard_map/all_to_all | solution.py:398
  21.8 1.0 pack_faces.1
  22.8 1.3 collective-permute-start.1
  24.1 4.0 %collective-permute-start = (f32[5,8,128]{2,1,0:T(8,128)S(1)}, f32[5,8,128]{2,1,0:T(8,128)S(1)}, u32[]{:S(2)}, u32[]{:S(2)}) collective-permute-start(f32[5,8,128]{2,1,0:T(8,128)S(1)} %get-tuple-element.15), channel_id=1, source_target_pairs={{0,64},{64,128},{128,192},{192,256},{256,320},{320,384},{384,448},... | collective-permute-start | bytes 61448 | tf_op jit(solution)/shard_map/ppermute | solution.py:349
  28.1 3.3 %collective-permute-start.4 = (f32[5,16,128]{2,1,0:T(8,128)S(1)}, f32[5,16,128]{2,1,0:T(8,128)S(1)}, u32[]{:S(2)}, u32[]{:S(2)}) collective-permute-start(f32[5,16,128]{2,1,0:T(8,128)S(1)} %get-tuple-element.18), channel_id=1, source_target_pairs={{0,1},{1,2},{2,3},{4,5},{5,6},{6,7},{8,9},{9,10},{10,11},{12,13},{... | collective-permute-start | bytes 122888 | tf_op jit(solution)/shard_map/ppermute | solution.py:349
  31.4 1.3 collective-permute-start.5
  32.7 4.2 %collective-permute-start.2 = (f32[5,32,128]{2,1,0:T(8,128)S(1)}, f32[5,32,128]{2,1,0:T(8,128)S(1)}, u32[]{:S(2)}, u32[]{:S(2)}) collective-permute-start(f32[5,32,128]{2,1,0:T(8,128)S(1)} %get-tuple-element.16), channel_id=1, source_target_pairs={{0,4},{4,8},{8,12},{12,16},{16,20},{20,24},{24,28},{28,32},{32,36}... | collective-permute-start | bytes 245768 | tf_op jit(solution)/shard_map/ppermute | solution.py:349
  36.9 2.2 %all-to-all-done.got = f32[64,16,128]{2,1,0:T(8,128)S(1)} async-done(((f32[64,16,128]{2,1,0:T(8,128)}), f32[64,16,128]{2,1,0:T(8,128)S(1)}, u32[]{:S(2)}, u32[]{:S(2)}) %all-to-all-start) | async-done | bytes 524320 | tf_op jit(solution)/shard_map/all_to_all | solution.py:398
  39.8 6.8 %all-to-all-start.1 = ((f32[8,16,128]{2,1,0:T(8,128)}), f32[8,16,128]{2,1,0:T(8,128)}, u32[]{:S(2)}, u32[]{:S(2)}) async-start(f32[8,16,128]{2,1,0:T(8,128)} %sum_sources.1), calls=%async_computation.1 | async-start | bytes 131072 | tf_op jit(solution)/shard_map/all_to_all | solution.py:436
  46.6 4.0 %collective-permute-start.3 = (f32[5,32,128]{2,1,0:T(8,128)S(1)}, f32[5,32,128]{2,1,0:T(8,128)S(1)}, u32[]{:S(2)}, u32[]{:S(2)}) collective-permute-start(f32[5,32,128]{2,1,0:T(8,128)S(1)} %get-tuple-element.17), channel_id=1, source_target_pairs={{4,0},{8,4},{12,8},{16,12},{20,16},{24,20},{28,24},{32,28},{36,32}... | collective-permute-start | bytes 245768 | tf_op jit(solution)/shard_map/ppermute | solution.py:349
  51.9 1.6 %collective-permute-done.3.yn = f32[5,32,128]{2,1,0:T(8,128)S(1)} collective-permute-done((f32[5,32,128]{2,1,0:T(8,128)S(1)}, f32[5,32,128]{2,1,0:T(8,128)S(1)}, u32[]{:S(2)}, u32[]{:S(2)}) %collective-permute-start.3) | collective-permute-done | bytes 81952 | tf_op jit(solution)/shard_map/ppermute | solution.py:349
  53.5 0.8 copy-done.7
  54.3 0.7 copy-done.11
  55.0 7.1 %first_step.1 = (f32[5,32,16,128]{3,2,1,0:T(8,128)S(1)}, f32[5,8,128]{2,1,0:T(8,128)}, f32[5,32,128]{2,1,0:T(8,128)}, f32[5,32,128]{2,1,0:T(8,128)}, f32[5,16,128]{2,1,0:T(8,128)}, /*index=5*/f32[5,16,128]{2,1,0:T(8,128)}) custom-call(f32[5,32,16,128]{3,2,1,0:T(8,128)S(1)} %copy-done, f32[32,16,128]{2,1,0:T(8,128)S(1)} %copy-done.1, ...), custom_call_target="tpu_custom_call" | custom-call | tf_op jit(solution)/shard_map/first_step/pallas_call | solution.py:418
  62.1 1.9 %collective-permute-start.8 = (f32[5,32,128]{2,1,0:T(8,128)}, f32[5,32,128]{2,1,0:T(8,128)}, u32[]{:S(2)}, u32[]{:S(2)}) collective-permute-start(f32[5,32,128]{2,1,0:T(8,128)} %get-tuple-element.22), channel_id=1, source_target_pairs={{0,4},{4,8},{8,12},{12,16},{16,20},{20,24},{24,28},{28,32},{32,36}... | collective-permute-start | bytes 245768 | tf_op jit(solution)/shard_map/ppermute | solution.py:349
  64.1 3.0 %collective-permute-start.9 = (f32[5,32,128]{2,1,0:T(8,128)}, f32[5,32,128]{2,1,0:T(8,128)}, u32[]{:S(2)}, u32[]{:S(2)}) collective-permute-start(f32[5,32,128]{2,1,0:T(8,128)} %get-tuple-element.23), channel_id=1, source_target_pairs={{4,0},{8,4},{12,8},{16,12},{20,16},{24,20},{28,24},{32,28},{36,32}... | collective-permute-start | bytes 245768 | tf_op jit(solution)/shard_map/ppermute | solution.py:349
  67.1 1.3 collective-permute-start.7
  68.4 2.6 %collective-permute-start.10 = (f32[5,16,128]{2,1,0:T(8,128)}, f32[5,16,128]{2,1,0:T(8,128)S(1)}, u32[]{:S(2)}, u32[]{:S(2)}) collective-permute-start(f32[5,16,128]{2,1,0:T(8,128)} %get-tuple-element.24), channel_id=1, source_target_pairs={{0,1},{1,2},{2,3},{4,5},{5,6},{6,7},{8,9},{9,10},{10,11},{12,13},{... | collective-permute-start | bytes 122888 | tf_op jit(solution)/shard_map/ppermute | solution.py:349
  71.0 1.3 collective-permute-start.11
  72.3 4.9 %collective-permute-start.6 = (f32[5,8,128]{2,1,0:T(8,128)}, f32[5,8,128]{2,1,0:T(8,128)}, u32[]{:S(2)}, u32[]{:S(2)}) collective-permute-start(f32[5,8,128]{2,1,0:T(8,128)} %get-tuple-element.21), channel_id=1, source_target_pairs={{0,64},{64,128},{128,192},{192,256},{256,320},{320,384},{384,448},... | collective-permute-start | bytes 61448 | tf_op jit(solution)/shard_map/ppermute | solution.py:349
  77.3 1.2 copy.30.geom
  78.7 1.0 copy-done.2
  79.7 0.9 copy-done.3
  80.6 0.7 copy-done.9
  82.0 10.8 %second_step.1 = (f32[5,32,16,128]{3,2,1,0:T(8,128)}, f32[64,128]{1,0:T(8,128)S(1)}) custom-call(s32[5]{0:T(128)S(1)} %stack.39.flags, f32[8,16,128]{2,1,0:T(8,128)} %all-to-all-done.1.coeffs, f32[512,256]{1,0:T(8,128)S(1)} %copy-done.2, f32[5,32,16,128]{3,2,1,0:T(8,128)S(1)} %copy-done, f32[5,32,16,128]{3,2,1,0:T(8,128)S(1)} %get-tuple-element.20.base, ...), custom_call_target="tpu_custom_call" | custom-call | tf_op jit(solution)/shard_map/second_step/pallas_call | solution.py:438
  92.9 21.0 %all_to_all.25 = f32[64,1,128]{2,1,0:T(1,128)S(1)} all-to-all(f32[64,1,128]{2,1,0:T(1,128)S(1)} %bitcast.14), channel_id=1, replica_groups=mesh['stream'=8,'span'=16,'vert'=4] {'span','vert'}, dimensions={0} | all-to-all | bytes 65536 | tf_op jit(solution)/shard_map/all_to_all | solution.py:466
  114.0 14.8 %all_to_all.26 = f32[8,1,128]{2,1,0:T(1,128)S(1)} all-to-all(f32[8,1,128]{2,1,0:T(1,128)S(1)} %broadcast_in_dim.11), channel_id=1, replica_groups=mesh['stream'=8,'span'=16,'vert'=4] {'stream'}, dimensions={0} | all-to-all | bytes 8192 | tf_op jit(solution)/shard_map/all_to_all | solution.py:468
  (42 shorter events, 3.5 us)
Async XLA Ops:
  2.6 0.9 copy-start.4
  3.5 0.8 copy-start.5
  4.3 17.5 %copy-start = (f32[5,32,16,128]{3,2,1,0:T(8,128)S(1)}, f32[5,32,16,128]{3,2,1,0:T(8,128)}, u32[]{:S(2)}) copy-start(f32[5,32,16,128]{3,2,1,0:T(8,128)} %fields.5) | copy-start | bytes 3932164
  6.9 43.8 %copy-start.14 = (f32[128]{0:T(128)S(1)}, f32[128]{0:T(128)}, u32[]{:S(2)}) copy-start(f32[128]{0:T(128)} %constant.31.clone) | copy-start | bytes 1540
  6.9 46.7 %copy-start.1 = (f32[32,16,128]{2,1,0:T(8,128)S(1)}, f32[32,16,128]{2,1,0:T(8,128)}, u32[]{:S(2)}) copy-start(f32[32,16,128]{2,1,0:T(8,128)} %solid.3) | copy-start | bytes 786436
  6.9 32.2 %all-to-all-start = ((f32[64,16,128]{2,1,0:T(8,128)}), f32[64,16,128]{2,1,0:T(8,128)S(1)}, u32[]{:S(2)}, u32[]{:S(2)}) async-start(f32[64,16,128]{2,1,0:T(8,128)} %bitcast.5), calls=%async_computation | async-start | bytes 1048576 | tf_op jit(solution)/shard_map/all_to_all | solution.py:398
  22.8 23.8 %collective-permute-start.1 = (f32[5,8,128]{2,1,0:T(8,128)S(1)}, f32[5,8,128]{2,1,0:T(8,128)S(1)}, u32[]{:S(2)}, u32[]{:S(2)}) collective-permute-start(f32[5,8,128]{2,1,0:T(8,128)S(1)} %get-tuple-element.15), channel_id=1, source_target_pairs={{64,0},{128,64},{192,128},{256,192},{320,256},{384,320},{448,384},... | collective-permute-start | bytes 61448 | tf_op jit(solution)/shard_map/ppermute | solution.py:349
  24.1 26.5 %collective-permute-start = (f32[5,8,128]{2,1,0:T(8,128)S(1)}, f32[5,8,128]{2,1,0:T(8,128)S(1)}, u32[]{:S(2)}, u32[]{:S(2)}) collective-permute-start(f32[5,8,128]{2,1,0:T(8,128)S(1)} %get-tuple-element.15), channel_id=1, source_target_pairs={{0,64},{64,128},{128,192},{192,256},{256,320},{320,384},{384,448},... | collective-permute-start | bytes 61448 | tf_op jit(solution)/shard_map/ppermute | solution.py:349
  28.1 23.2 %collective-permute-start.4 = (f32[5,16,128]{2,1,0:T(8,128)S(1)}, f32[5,16,128]{2,1,0:T(8,128)S(1)}, u32[]{:S(2)}, u32[]{:S(2)}) collective-permute-start(f32[5,16,128]{2,1,0:T(8,128)S(1)} %get-tuple-element.18), channel_id=1, source_target_pairs={{0,1},{1,2},{2,3},{4,5},{5,6},{6,7},{8,9},{9,10},{10,11},{12,13},{... | collective-permute-start | bytes 122888 | tf_op jit(solution)/shard_map/ppermute | solution.py:349
  31.4 19.9 %collective-permute-start.5 = (f32[5,16,128]{2,1,0:T(8,128)S(1)}, f32[5,16,128]{2,1,0:T(8,128)S(1)}, u32[]{:S(2)}, u32[]{:S(2)}) collective-permute-start(f32[5,16,128]{2,1,0:T(8,128)S(1)} %get-tuple-element.19), channel_id=1, source_target_pairs={{1,0},{2,1},{3,2},{5,4},{6,5},{7,6},{9,8},{10,9},{11,10},{13,12},{... | collective-permute-start | bytes 122888 | tf_op jit(solution)/shard_map/ppermute | solution.py:349
  32.7 19.2 %collective-permute-start.2 = (f32[5,32,128]{2,1,0:T(8,128)S(1)}, f32[5,32,128]{2,1,0:T(8,128)S(1)}, u32[]{:S(2)}, u32[]{:S(2)}) collective-permute-start(f32[5,32,128]{2,1,0:T(8,128)S(1)} %get-tuple-element.16), channel_id=1, source_target_pairs={{0,4},{4,8},{8,12},{12,16},{16,20},{20,24},{24,28},{28,32},{32,36}... | collective-permute-start | bytes 245768 | tf_op jit(solution)/shard_map/ppermute | solution.py:349
  36.9 40.3 %copy-start.13 = (f32[3,64,32]{1,2,0:T(8,128)S(1)}, f32[3,64,32]{1,2,0:T(8,128)}, u32[]{:S(2)}) copy-start(f32[3,64,32]{1,2,0:T(8,128)} %param.19) | copy-start | bytes 73732
  39.8 38.9 %all-to-all-start.1 = ((f32[8,16,128]{2,1,0:T(8,128)}), f32[8,16,128]{2,1,0:T(8,128)}, u32[]{:S(2)}, u32[]{:S(2)}) async-start(f32[8,16,128]{2,1,0:T(8,128)} %sum_sources.1), calls=%async_computation.1 | async-start | bytes 131072 | tf_op jit(solution)/shard_map/all_to_all | solution.py:436
  46.6 6.9 %collective-permute-start.3 = (f32[5,32,128]{2,1,0:T(8,128)S(1)}, f32[5,32,128]{2,1,0:T(8,128)S(1)}, u32[]{:S(2)}, u32[]{:S(2)}) collective-permute-start(f32[5,32,128]{2,1,0:T(8,128)S(1)} %get-tuple-element.17), channel_id=1, source_target_pairs={{4,0},{8,4},{12,8},{16,12},{20,16},{24,20},{28,24},{32,28},{36,32}... | collective-permute-start | bytes 245768 | tf_op jit(solution)/shard_map/ppermute | solution.py:349
  50.7 0.6 copy-start.10
  51.3 0.6 copy-start.6
  53.5 0.8 copy-start.7
  54.3 0.7 copy-start.11
  62.1 16.5 %collective-permute-start.8 = (f32[5,32,128]{2,1,0:T(8,128)}, f32[5,32,128]{2,1,0:T(8,128)}, u32[]{:S(2)}, u32[]{:S(2)}) collective-permute-start(f32[5,32,128]{2,1,0:T(8,128)} %get-tuple-element.22), channel_id=1, source_target_pairs={{0,4},{4,8},{8,12},{12,16},{16,20},{20,24},{24,28},{28,32},{32,36}... | collective-permute-start | bytes 245768 | tf_op jit(solution)/shard_map/ppermute | solution.py:349
  64.1 14.6 %collective-permute-start.9 = (f32[5,32,128]{2,1,0:T(8,128)}, f32[5,32,128]{2,1,0:T(8,128)}, u32[]{:S(2)}, u32[]{:S(2)}) collective-permute-start(f32[5,32,128]{2,1,0:T(8,128)} %get-tuple-element.23), channel_id=1, source_target_pairs={{4,0},{8,4},{12,8},{16,12},{20,16},{24,20},{28,24},{32,28},{36,32}... | collective-permute-start | bytes 245768 | tf_op jit(solution)/shard_map/ppermute | solution.py:349
  67.1 5.2 %collective-permute-start.7 = (f32[5,8,128]{2,1,0:T(8,128)}, f32[5,8,128]{2,1,0:T(8,128)S(1)}, u32[]{:S(2)}, u32[]{:S(2)}) collective-permute-start(f32[5,8,128]{2,1,0:T(8,128)} %get-tuple-element.21), channel_id=1, source_target_pairs={{64,0},{128,64},{192,128},{256,192},{320,256},{384,320},{448,384},... | collective-permute-start | bytes 61448 | tf_op jit(solution)/shard_map/ppermute | solution.py:349
  68.4 10.2 %collective-permute-start.10 = (f32[5,16,128]{2,1,0:T(8,128)}, f32[5,16,128]{2,1,0:T(8,128)S(1)}, u32[]{:S(2)}, u32[]{:S(2)}) collective-permute-start(f32[5,16,128]{2,1,0:T(8,128)} %get-tuple-element.24), channel_id=1, source_target_pairs={{0,1},{1,2},{2,3},{4,5},{5,6},{6,7},{8,9},{9,10},{10,11},{12,13},{... | collective-permute-start | bytes 122888 | tf_op jit(solution)/shard_map/ppermute | solution.py:349
  71.0 7.6 %collective-permute-start.11 = (f32[5,16,128]{2,1,0:T(8,128)}, f32[5,16,128]{2,1,0:T(8,128)}, u32[]{:S(2)}, u32[]{:S(2)}) collective-permute-start(f32[5,16,128]{2,1,0:T(8,128)} %get-tuple-element.25), channel_id=1, source_target_pairs={{1,0},{2,1},{3,2},{5,4},{6,5},{7,6},{9,8},{10,9},{11,10},{13,12},{... | collective-permute-start | bytes 122888 | tf_op jit(solution)/shard_map/ppermute | solution.py:349
  72.3 4.9 %copy-start.8 = (f32[5,8,128]{2,1,0:T(8,128)}, f32[5,8,128]{2,1,0:T(8,128)S(1)}, u32[]{:S(2)}) copy-start(f32[5,8,128]{2,1,0:T(8,128)S(1)} %collective-permute-done.7.xe) | copy-start | bytes 61444
  72.3 6.3 %collective-permute-start.6 = (f32[5,8,128]{2,1,0:T(8,128)}, f32[5,8,128]{2,1,0:T(8,128)}, u32[]{:S(2)}, u32[]{:S(2)}) collective-permute-start(f32[5,8,128]{2,1,0:T(8,128)} %get-tuple-element.21), channel_id=1, source_target_pairs={{0,64},{64,128},{128,192},{192,256},{256,320},{320,384},{384,448},... | collective-permute-start | bytes 61448 | tf_op jit(solution)/shard_map/ppermute | solution.py:349
  78.7 1.0 copy-start.2
  79.7 0.9 copy-start.3
  80.6 0.7 copy-start.9
  81.3 0.7 copy-start.12

commit v2 on v1

v2 whole, which is shorter than its diff:
```python
import math

import jax
import jax.numpy as jnp
import numpy as np
from jax import lax
from jax.experimental import pallas as pl
from jax.experimental.pallas import tpu as pltpu
from jax.sharding import PartitionSpec as P

time_step = 0.15
viscous = 0.05
heat_diff = 0.03
sound_sq = 1.0
buoyant = 0.5
penalty = 0.5
relax_time = 0.5
relax_depth = 8.0
wave_cols = 16

HI = lax.Precision.HIGHEST
NF = 5
ROWS = 16


def mdot(a, b, dims):
    return lax.dot_general(
        a, b, (dims, ((), ())), precision=HI, preferred_element_type=jnp.float32
    )


def wave_tables(cz, cy, n_span, n_vert, spec):
    modes = np.arange(spec)
    across = (modes % wave_cols).astype(np.float64)
    upward = (modes // wave_cols).astype(np.float64)
    ny, nz = cy * n_span, cz * n_vert

    def basis(z, y):
        turn = across[None] * y[:, None] / ny + upward[None] * z[:, None] / nz
        angle = 2.0 * math.pi * turn
        return np.concatenate([np.cos(angle), np.sin(angle)], axis=1)

    z, y = np.arange(cz, dtype=np.float64), np.arange(cy, dtype=np.float64)
    plane = basis(np.repeat(z, cy), np.tile(y, cz)).astype(np.float32)
    edges = np.zeros((2 * spec, 128), np.float64)
    at = 0
    for part in (
        basis(z, 0 * z + cy - 1),
        basis(z, 0 * z),
        basis(0 * y + cz - 1, y),
        basis(0 * y, y),
    ):
        edges[:, at : at + part.shape[0]] = part.T
        at += part.shape[0]
    s, v = np.repeat(np.arange(n_span), n_vert), np.tile(np.arange(n_vert), n_span)
    turn = basis(1.0 * v * cz, 1.0 * s * cy).astype(np.float32)
    return plane, edges.astype(np.float32), turn


def sum_panels(panels, owner, turn, edge_table, out):
    n_vert = lax.axis_size("vert")
    tiles = turn.shape[0]
    spec = turn.shape[1] // 2
    held = owner.shape[1]
    named = (owner[...] == lax.broadcasted_iota(jnp.int32, (tiles, held), 0)).astype(jnp.float32)
    cos_t, sin_t = turn[:, :spec], turn[:, spec:]
    lane = lax.broadcasted_iota(jnp.int32, (tiles, 128), 1)
    for f in range(NF):
        total = mdot(named, panels[f], ((1,), (0,)))
        c, s = total[:, :spec], total[:, spec:]
        c2 = c * cos_t + s * sin_t
        s2 = s * cos_t - c * sin_t
        out[pl.ds(f, tiles, stride=ROWS), :] = c2
        out[pl.ds(8 + f, tiles, stride=ROWS), :] = s2
        e = mdot(c2, edge_table[:spec, :], ((1,), (0,))) + mdot(
            s2, edge_table[spec:, :], ((1,), (0,))
        )
        row = jnp.where(
            lane < 32,
            jnp.roll(e, n_vert, 0),
            jnp.where(
                lane < 64,
                jnp.roll(e, -n_vert, 0),
                jnp.where(lane < 80, jnp.roll(e, 1, 0), jnp.roll(e, -1, 0)),
            ),
        )
        at = 5 + f if f < 3 else 10 + f
        out[pl.ds(at, tiles, stride=ROWS), :] = row
    out[pl.ds(15, tiles, stride=ROWS), :] = jnp.zeros((tiles, 128), jnp.float32)


def lane_ids(shape):
    return lax.broadcasted_iota(jnp.int32, shape, len(shape) - 1)


INNER = 8


def packed_x(acc, v, zi):
    lane = lane_ids((8, 128))
    for h in range(2):
        k = 2 * zi + h
        acc = jnp.where((lane >> 1) == k, pltpu.roll(v[8 * h : 8 * h + 8], 2 * k + 1, 1), acc)
    return acc


def placed(whole, part, zo):
    width = 4 * INNER
    lane = lane_ids((8, 128))
    return jnp.where(lane // width == zo, pltpu.roll(part, zo * width, 1), whole)


def face_choice(axis):
    return lax.rem(lax.axis_index(axis), 2) == 0


def store_faces(state, ye, yo, ze, zo):
    cz, cy = state.shape[1], state.shape[2]
    y_low, z_low = face_choice("span"), face_choice("vert")
    for f in range(NF):
        low, high = state[f, :, 0, :], state[f, :, cy - 1, :]
        ye[f] = jnp.where(y_low, high, low)
        yo[f] = jnp.where(y_low, low, high)
        low, high = state[f, 0], state[f, cz - 1]
        ze[f] = jnp.where(z_low, high, low)
        zo[f] = jnp.where(z_low, low, high)


def pack_faces(fields, xf, ye, yo, ze, zo):
    cz = fields.shape[1]
    zero = jnp.zeros((8, 128), jnp.float32)

    def body(g, accs):
        new = []
        for f in range(NF):
            part = zero
            for i in range(INNER):
                part = packed_x(part, fields[f, g * INNER + i], i)
            new.append(placed(accs[f], part, g))
        return tuple(new)

    accs = lax.fori_loop(0, cz // INNER, body, (zero,) * NF)
    for f in range(NF):
        xf[f] = accs[f]
    store_faces(fields, ye, yo, ze, zo)


def fill_ghosts(q, ye, yo, ze, zo, extra=None):
    cz = q.shape[1] - 2
    y_low, z_low = face_choice("span"), face_choice("vert")
    for f in range(NF):
        south = jnp.where(y_low, yo[f], ye[f])
        north = jnp.where(y_low, ye[f], yo[f])
        down = jnp.where(z_low, zo[f], ze[f])
        up = jnp.where(z_low, ze[f], zo[f])
        if extra is not None:
            es, en, ed, eu = extra(f)
            south, north, down, up = south + es, north + en, down + ed, up + eu
        q[f, 1 : cz + 1, 7, :] = south
        q[f, 1 : cz + 1, 24, :] = north
        q[f, 0, 8:24, :] = down
        q[f, cz + 1, 8:24, :] = up


def ghosts_x(west, east):
    lane = lane_ids((8, 128))
    return [jnp.where((lane & 1) == 0, west[f], pltpu.roll(east[f], 126, 1)) for f in range(NF)]


def slab_rates(q, xg, damp2, decay, z, zi):
    lane = lane_ids((16, 128))
    first, last = lane == 0, lane == 127
    cs, dx, dy, dz, rs = [], [], [], [], []
    for f in range(NF):
        c = q[f, z + 1, 8:24, :]
        up, down = q[f, z + 2, 8:24, :], q[f, z, 8:24, :]
        north, south = q[f, z + 1, 9:25, :], q[f, z + 1, 7:23, :]
        side = jnp.concatenate(
            [
                pltpu.roll(xg[f], (128 - 4 * zi) % 128, 1),
                pltpu.roll(xg[f], (126 - 4 * zi) % 128, 1),
            ],
            axis=0,
        )
        west = jnp.where(first, side, pltpu.roll(c, 1, 1))
        east = jnp.where(last, side, pltpu.roll(c, 127, 1))
        nu = heat_diff if f == 4 else viscous
        around = (east + west) + (north + south) + (up + down)
        cs.append(c)
        dx.append(east - west)
        dy.append(north - south)
        dz.append(up - down)
        rs.append(nu * around - decay[f == 4] * c)
    hu, hv, hw = 0.5 * cs[0], 0.5 * cs[1], 0.5 * cs[2]
    out = []
    for f in range(NF):
        r = rs[f] - (hu * dx[f] + hv * dy[f] + hw * dz[f])
        if f == 0:
            r = r - 0.5 * dx[3] - damp2 * hu
        elif f == 1:
            r = r - 0.5 * dy[3] - damp2 * hv
        elif f == 2:
            r = r - 0.5 * dz[3] - damp2 * hw + buoyant * cs[4]
        elif f == 3:
            r = r - (0.5 * sound_sq) * (dx[0] + dy[1] + dz[2])
        out.append(r)
    return cs, out


def relax_weights(cx):
    lane = lane_ids((1, cx))
    weight = jnp.exp(lane.astype(jnp.float32) * (-1.0 / relax_depth)) / relax_time
    return jnp.where((lax.axis_index("stream") == 0) & (lane < cx // 2), weight, 0.0)


def first_step(got, fields, solid, xe, xo, ye, yo, ze, zo, base, carry_out, ye1, yo1, ze1, zo1, q):
    cz = fields.shape[1]
    fill_ghosts(q, ye, yo, ze, zo)

    def fill(z, carry):
        for f in range(NF):
            q[f, z + 1, 8:24, :] = fields[f, z]
        return carry

    lax.fori_loop(0, cz, fill, 0, unroll=4)
    x_low = face_choice("stream")
    xg = ghosts_x(
        [jnp.where(x_low, xo[f], xe[f]) for f in range(NF)],
        [jnp.where(x_low, xe[f], xo[f]) for f in range(NF)],
    )
    relax = relax_weights(fields.shape[3])
    decay = (6.0 * viscous + relax, 6.0 * heat_diff + relax)
    zero = jnp.zeros((8, 128), jnp.float32)

    def body(g, accs):
        turned = [pltpu.roll(xg[f], (128 - 4 * INNER * g) & 127, 1) for f in range(NF)]
        parts = [zero] * NF
        for i in range(INNER):
            z = g * INNER + i
            damp2 = solid[z] * (2.0 / penalty)
            cs, rs = slab_rates(q, turned, damp2, decay, z, i)
            for f in range(NF):
                b = cs[f] + time_step * rs[f]
                base[f, z] = b
                parts[f] = packed_x(parts[f], b, i)
        return tuple(placed(accs[f], parts[f], g) for f in range(NF))

    accs = lax.fori_loop(0, cz // INNER, body, (zero,) * NF)
    total = got[0:ROWS]
    for i in range(1, got.shape[0] // ROWS):
        total = total + got[ROWS * i : ROWS * i + ROWS]
    for i in range(carry_out.shape[0]):
        carry_out[i, 0:ROWS] = total
        for f in range(NF):
            carry_out[i, ROWS + 8 * f : ROWS + 8 * f + 8] = accs[f]
    store_faces(base, ye1, yo1, ze1, zo1)


def second_step(
    carried,
    plane_table,
    fields,
    base,
    solid,
    ye,
    yo,
    ze,
    zo,
    cells,
    geom,
    strips,
    shapes,
    out,
    modal,
    q,
    target,
    geom_v,
    strips_v,
    sems,
):
    cz, cy, cx = fields.shape[1:]
    spec = plane_table.shape[1] // 2
    n_stream = carried.shape[0]
    span_pos = lax.axis_index("span")
    vert_pos = lax.axis_index("vert")
    stream_pos = lax.axis_index("stream")
    get_geom = pltpu.make_async_copy(geom.at[0, span_pos], geom_v, sems.at[0])
    get_strips = pltpu.make_async_copy(strips.at[0, span_pos], strips_v, sems.at[1])
    get_geom.start()
    get_strips.start()
    low, high = carried[0, 0:8], carried[0, 8:16]
    for i in range(1, n_stream):
        low = low + carried[i, 0:8]
        high = high + carried[i, 8:16]
    one = jnp.where(lane_ids((1, 8)) == 0, 1.0, 0.0)
    target[...] = (
        mdot(plane_table[:, :spec], low, ((1,), (1,)))
        + mdot(plane_table[:, spec:], high, ((1,), (1,)))
        + one
    )
    n_edge = 2 * cz + 2 * cy
    pick = (
        lax.broadcasted_iota(jnp.int32, (n_edge, 128), 0) == lane_ids((n_edge, 128))
    ).astype(jnp.float32)
    e_low = mdot(pick, low, ((1,), (1,)))
    e_high = mdot(pick, high, ((1,), (1,)))
    relax = relax_weights(cx)
    decay = (6.0 * viscous + relax, 6.0 * heat_diff + relax)
    push = time_step * relax

    def edge_push(f):
        col = e_low[:, 5 + f : 6 + f] if f < 3 else e_high[:, 2 + f : 3 + f]
        if f == 0:
            col = col + 1.0
        col = col * push
        return (
            jnp.where(span_pos > 0, col[0:cz], 0.0),
            jnp.where(span_pos < lax.axis_size("span") - 1, col[cz : 2 * cz], 0.0),
            jnp.where(vert_pos > 0, col[2 * cz : 2 * cz + cy], 0.0),
            jnp.where(vert_pos < lax.axis_size("vert") - 1, col[2 * cz + cy :], 0.0),
        )

    fill_ghosts(q, ye, yo, ze, zo, edge_push)

    def fill(g, carry):
        for i in range(4):
            z = g * 4 + i
            t = target[pl.ds(pl.multiple_of(z * cy, cy), cy), :]
            for f in range(NF):
                pushed = push * t[:, f : f + 1]
                q[f, z + 1, 8:24, :] = base[f, z] + pushed
                out[f, z] = fields[f, z] + pushed
        return carry

    lax.fori_loop(0, cz // 4, fill, 0)
    west_at = jnp.maximum(stream_pos - 1, 0)
    east_at = jnp.minimum(stream_pos + 1, n_stream - 1)
    west, east = [], []
    for f in range(NF):
        rows = slice(ROWS + 8 * f, ROWS + 8 * f + 8)
        west.append(jnp.where(stream_pos > 0, carried[west_at, rows], 0.0))
        east.append(jnp.where(stream_pos < n_stream - 1, carried[east_at, rows], 0.0))
    xg = ghosts_x(west, east)

    def body(g, carry):
        turned = [pltpu.roll(xg[f], (128 - 4 * INNER * g) & 127, 1) for f in range(NF)]
        for i in range(INNER):
            z = g * INNER + i
            damp2 = solid[z] * (2.0 / penalty)
            cs, rs = slab_rates(q, turned, damp2, decay, z, i)
            for f in range(NF):
                out[f, z] = 0.5 * (out[f, z] + cs[f] + time_step * rs[f])
        return carry

    lax.fori_loop(0, cz // INNER, body, 0)

    pressure = jnp.transpose(jnp.reshape(out[3], (cz * cy, cx)))
    p_hi = pressure.astype(jnp.bfloat16)
    p_lo = (pressure - p_hi.astype(jnp.float32)).astype(jnp.bfloat16)
    parts = jnp.concatenate([p_hi, p_lo], axis=0)
    get_geom.wait()
    get_strips.wait()
    count = cells.shape[1]
    step = 512
    n_comp = geom_v.shape[0]
    forces = jnp.zeros((8, shapes.shape[2]), jnp.float32)
    for at in range(0, count, step):
        where = cells[:, at : at + step]
        rows = lax.broadcasted_iota(jnp.int32, (cz * cy, step), 0)
        hit = jnp.where(rows == (where >> 7), 1.0, 0.0).astype(jnp.bfloat16)
        picked = lax.dot_general(
            parts, hit, (((1,), (0,)), ((), ())), preferred_element_type=jnp.float32
        )
        picked = picked[:cx] + picked[cx:]
        lanes = lax.broadcasted_iota(jnp.int32, (cx, step), 0)
        sample = jnp.sum(jnp.where(lanes == (where & 127), picked, 0.0), axis=0, keepdims=True)
        traction = jnp.concatenate(
            [sample * geom_v[c, :, at : at + step] for c in range(n_comp)]
            + [jnp.zeros((8 - n_comp, step), jnp.float32)],
            axis=0,
        )
        strip = lax.broadcasted_iota(jnp.int32, (shapes.shape[2], step), 0)
        member = jnp.where(strip == strips_v[:, at : at + step], 1.0, 0.0)
        forces = forces + mdot(traction, member, ((1,), (1,)))
    total = jnp.zeros((1, shapes.shape[1]), jnp.float32)
    for c in range(n_comp):
        total = total + mdot(forces[c : c + 1], shapes[c], ((1,), (1,)))
    total = jnp.concatenate(
        [total, jnp.zeros((1, 128 - shapes.shape[1]), jnp.float32)], axis=1
    )
    modal[...] = jnp.broadcast_to(total, modal.shape)


def f32(*shape):
    return jax.ShapeDtypeStruct(shape, jnp.float32)


VM = pl.BlockSpec(memory_space=pltpu.VMEM)
AN = pl.BlockSpec(memory_space=pl.ANY)
BIG = pltpu.CompilerParams(vmem_limit_bytes=16 * 1024 * 1024)


def swapped(block, axis, odd):
    pairs = []
    for i in range(odd, lax.axis_size(axis) - 1, 2):
        pairs += [(i, i + 1), (i + 1, i)]
    return lax.ppermute(block, axis, pairs)


def on_device(
    fields, solid_frac, panels, panel_owner, deck_cells, deck_geom, strip_ids, mode_shapes
):
    cz, cy, cx = fields.shape[1:]
    n_stream = lax.axis_size("stream")
    n_span = lax.axis_size("span")
    n_vert = lax.axis_size("vert")
    tiles = n_span * n_vert
    spec = panels.shape[2] // 2
    plane, edges, turn = wave_tables(cz, cy, n_span, n_vert, spec)
    sent = pl.pallas_call(
        sum_panels,
        out_shape=f32(tiles * ROWS, 128),
        compiler_params=BIG,
        name="panel_sums",
    )(
        panels.transpose(1, 0, 2),
        panel_owner.reshape(1, -1),
        jnp.asarray(turn),
        jnp.asarray(edges),
    )
    got = lax.all_to_all(
        sent.reshape(tiles, ROWS, 128), ("span", "vert"), 0, 0, tiled=True
    ).reshape(tiles * ROWS, 128)
    yz_shapes = (f32(NF, cz, cx), f32(NF, cz, cx), f32(NF, cy, cx), f32(NF, cy, cx))

    def swap_yz(ye, yo, ze, zo):
        return (
            swapped(ye, "span", 0),
            swapped(yo, "span", 1),
            swapped(ze, "vert", 0),
            swapped(zo, "vert", 1),
        )

    xf, *faces = pl.pallas_call(
        pack_faces,
        out_shape=(f32(NF, 8, 128),) + yz_shapes,
        in_specs=[VM],
        out_specs=(VM,) * 5,
        compiler_params=BIG,
        name="pack_faces",
    )(fields)
    ghosts = (swapped(xf, "stream", 0), swapped(xf, "stream", 1)) + swap_yz(*faces)
    scratch = pltpu.VMEM((NF, cz + 2, 32, cx), jnp.float32)
    base, carry, *faces = pl.pallas_call(
        first_step,
        out_shape=(f32(NF, cz, cy, cx), f32(n_stream, ROWS + 8 * NF, 128)) + yz_shapes,
        in_specs=[VM] * 9,
        out_specs=(VM,) * 6,
        scratch_shapes=[scratch],
        compiler_params=BIG,
        name="first_step",
    )(got, fields, solid_frac, *ghosts)
    carried = lax.all_to_all(carry, "stream", 0, 0, tiled=True)
    ghosts = swap_yz(*faces)
    deck = deck_cells.shape[3]
    new_fields, modal = pl.pallas_call(
        second_step,
        out_shape=(f32(NF, cz, cy, cx), f32(tiles, 128)),
        in_specs=[VM] * 10 + [AN, AN, VM],
        out_specs=(VM, VM),
        scratch_shapes=[
            scratch,
            pltpu.VMEM((cz * cy, 8), jnp.float32),
            pltpu.VMEM((3, 1, deck), jnp.float32),
            pltpu.VMEM((1, deck), jnp.int32),
            pltpu.SemaphoreType.DMA((2,)),
        ],
        compiler_params=BIG,
        name="second_step",
    )(
        carried,
        jnp.asarray(plane),
        fields,
        base,
        solid_frac,
        *ghosts,
        deck_cells.reshape(1, deck),
        deck_geom.transpose(0, 1, 3, 2, 4),
        strip_ids,
        mode_shapes.transpose(0, 2, 1),
    )
    part = lax.all_to_all(modal, ("span", "vert"), 0, 0, tiled=True)
    part = jnp.broadcast_to(jnp.sum(part, axis=0, keepdims=True), (n_stream, 128))
    part = lax.all_to_all(part, "stream", 0, 0, tiled=True)
    modal_force = jnp.sum(part, axis=0)[: mode_shapes.shape[2]]
    return (new_fields, modal_force)


def solution(mesh):
    return jax.shard_map(
        on_device,
        mesh=mesh,
        in_specs=(
            P(None, "vert", "span", "stream"),
            P("vert", "span", "stream"),
            P(("stream", "span", "vert"), None, None),
            P(("stream", "span", "vert"), None),
            P("vert", "span", "stream", None),
            P("vert", None, "stream", None, None),
            P("vert", None, "stream", None),
            P(),
        ),
        out_specs=(P(None, "vert", "span", "stream"), P()),
        check_vma=False,
    )
```

time: 130 us -> 120 us (0.923)
  Pallas kernels: 22.1 us -> 13.7 us
  local copies, waits for them, and re-layouts: 11.2 us -> 17.9 us
  starting transfers between devices: 54.8 us -> 49.1 us
  blocking collectives: 35.8 us -> 34.1 us
  waiting for transfers between devices: 3.84 us -> 2.2 us
    unnamed x34 -> x56, local copies, waits for them, and re-layouts: 11.1 us -> 17.9 us
    ppermute x12 -> x10, starting transfers between devices: 33 us -> 27.9 us  [swapped(): return lax.ppermute(block, axis, pairs)]
    pallas_call x4 -> x3, Pallas kernels: 11.3 us -> 6.99 us  [the longest x1 3.57 us: on_device(): pl.pallas_call(first_step, out_shape=(f32(NF, cz, cy, cx), f32(n_stream,...]
    pallas_call x1, Pallas kernels: 10.8 us -> 6.72 us  [on_device(): pl.pallas_call(second_step, out_shape=(f32(NF, cz, cy, cx), f32(tiles, 12...]
    all_to_all x1, waiting for transfers between devices: 2.18 us -> 0.01 us  [on_device(): lax.all_to_all(sent.reshape(tiles, ROWS, 128), ('span', 'vert'), 0, 0, ti...]
    all_to_all x1, blocking collectives: 14.8 us -> 13.2 us  [on_device(): part = lax.all_to_all(part, 'stream', 0, 0, tiled=True)]
  transfers between devices with their start and end apart: 14 -> 12, of which waited for: 2 -> 2; matrix products, arithmetic and copies ran while one was open for 1% -> 0% of each run, Pallas kernels for 7% -> 1%
where the time goes in v2:
time: 120 us; the launch traced here: 118 us
  starting transfers between devices  49.1 us (41%)
  blocking collectives  34.1 us (28%)
  local copies, waits for them, and re-layouts  17.9 us (15%)
  Pallas kernels  13.7 us (11%)
  waiting for transfers between devices  2.2 us (2%)
    ppermute x10, starting transfers between devices, swapped(): return lax.ppermute(block, axis, pairs)  27.9 us
    all_to_all x1, blocking collectives, on_device(): part = lax.all_to_all(modal, ('span', 'vert'), 0, 0, tiled=True)  20.8 us
    unnamed x56, local copies, waits for them, and re-layouts  17.9 us
    all_to_all x1, starting transfers between devices, on_device(): lax.all_to_all(sent.reshape(tiles, ROWS, 128), ('span', 'vert'), 0, 0, ti...  15 us
    all_to_all x1, blocking collectives, on_device(): part = lax.all_to_all(part, 'stream', 0, 0, tiled=True)  13.2 us
    pallas_call x1, Pallas kernels, on_device(): pl.pallas_call(second_step, out_shape=(f32(NF, cz, cy, cx), f32(tiles, 12...  6.72 us
    all_to_all x1, starting transfers between devices, on_device(): carried = lax.all_to_all(carry, 'stream', 0, 0, tiled=True)  6.21 us
    pallas_call x1, Pallas kernels, on_device(): pl.pallas_call(first_step, out_shape=(f32(NF, cz, cy, cx), f32(n_stream,...  3.57 us
  transfers between devices with their start and end apart: 12, of which 2 were waited for; matrix products, arithmetic and copies ran while one was open for 0% of the time, Pallas kernels for 1%

profile of v2, /device:TPU:1, one launch (start us, length us, event | category | flops | bytes accessed | tf_op | source)
XLA Modules:
  0.0 118.4 jit_solution(11181616934954408514)
XLA Ops:
  0.6 1.1 copy-done.4
  1.7 0.9 copy-done.7
  2.6 0.8 copy-done.12
  4.1 2.4 %panel_sums.1 = f32[1024,128]{1,0:T(8,128)} custom-call(f32[5,64,256]{2,1,0:T(8,128)S(1)} %bitcast.14, s32[1,64]{1,0:T(1,128)S(1)} %bitcast.18, f32[64,256]{1,0:T(8,128)S(1)} %copy-done.12, f32[256,128]{1,0:T(8,128)S(1)} %copy-done.7), custom_call_target="tpu_custom_call" | custom-call | tf_op jit(solution)/shard_map/panel_sums/pallas_call | solution.py:420
  6.5 15.0 %all-to-all-start = ((f32[64,16,128]{2,1,0:T(8,128)}), f32[64,16,128]{2,1,0:T(8,128)S(1)}, u32[]{:S(2)}, u32[]{:S(2)}) async-start(f32[64,16,128]{2,1,0:T(8,128)} %bitcast.2), calls=%async_computation | async-start | bytes 1048576 | tf_op jit(solution)/shard_map/all_to_all | solution.py:431
  21.5 1.0 pack_faces.1
  22.5 2.4 %collective-permute-start.2 = (f32[5,32,128]{2,1,0:T(8,128)S(1)}, f32[5,32,128]{2,1,0:T(8,128)S(1)}, u32[]{:S(2)}, u32[]{:S(2)}) collective-permute-start(f32[5,32,128]{2,1,0:T(8,128)S(1)} %get-tuple-element.16), channel_id=1, source_target_pairs={{0,4},{4,0},{8,12},{12,8},{16,20},{20,16},{24,28},{28,24},{32,36},... | collective-permute-start | bytes 245768 | tf_op jit(solution)/shard_map/ppermute | solution.py:407
  24.9 3.2 %collective-permute-start.3 = (f32[5,32,128]{2,1,0:T(8,128)S(1)}, f32[5,32,128]{2,1,0:T(8,128)S(1)}, u32[]{:S(2)}, u32[]{:S(2)}) collective-permute-start(f32[5,32,128]{2,1,0:T(8,128)S(1)} %get-tuple-element.17), channel_id=1, source_target_pairs={{4,8},{8,4},{12,16},{16,12},{20,24},{24,20},{28,32},{32,28},{36,40... | collective-permute-start | bytes 245768 | tf_op jit(solution)/shard_map/ppermute | solution.py:407
  28.8 3.1 %collective-permute-start.4 = (f32[5,16,128]{2,1,0:T(8,128)S(1)}, f32[5,16,128]{2,1,0:T(8,128)S(1)}, u32[]{:S(2)}, u32[]{:S(2)}) collective-permute-start(f32[5,16,128]{2,1,0:T(8,128)S(1)} %get-tuple-element.18), channel_id=1, source_target_pairs={{0,1},{1,0},{2,3},{3,2},{4,5},{5,4},{6,7},{7,6},{8,9},{9,8},{10,11... | collective-permute-start | bytes 122888 | tf_op jit(solution)/shard_map/ppermute | solution.py:407
  31.9 0.7 collective-permute-start.5
  33.2 5.7 %collective-permute-start = (f32[5,8,128]{2,1,0:T(8,128)S(1)}, f32[5,8,128]{2,1,0:T(8,128)S(1)}, u32[]{:S(2)}, u32[]{:S(2)}) collective-permute-start(f32[5,8,128]{2,1,0:T(8,128)S(1)} %get-tuple-element.15), channel_id=1, source_target_pairs={{0,64},{64,0},{128,192},{192,128},{256,320},{320,256},{384,448},{4... | collective-permute-start | bytes 61448 | tf_op jit(solution)/shard_map/ppermute | solution.py:407
  38.9 1.3 %collective-permute-done.xe = f32[5,8,128]{2,1,0:T(8,128)S(1)} collective-permute-done((f32[5,8,128]{2,1,0:T(8,128)S(1)}, f32[5,8,128]{2,1,0:T(8,128)S(1)}, u32[]{:S(2)}, u32[]{:S(2)}) %collective-permute-start) | collective-permute-done | bytes 20512 | tf_op jit(solution)/shard_map/ppermute | solution.py:407
  43.3 0.9 copy-done.9
  44.2 0.9 copy-done.11
  45.1 0.8 copy-done.15
  45.8 0.8 copy-done.17
  46.6 0.7 copy-done.19
  47.4 0.7 copy-done.21
  48.1 3.6 %first_step.1 = (f32[5,32,16,128]{3,2,1,0:T(8,128)S(1)}, f32[8,56,128]{2,1,0:T(8,128)S(1)}, f32[5,32,128]{2,1,0:T(8,128)S(1)}, f32[5,32,128]{2,1,0:T(8,128)S(1)}...) custom-call(f32[1024,128]{1,0:T(8,128)S(1)} %bitcast.12, f32[5,32,16,128]{3,2,1,0:T(8,128)S(1)} %copy-done, ...), custom_call_target="tpu_custom_call" | custom-call | tf_op jit(solution)/shard_map/first_step/pallas_call | solution.py:454
  51.7 0.7 copy-done.5
  54.8 6.2 %all-to-all-start.1 = ((f32[8,56,128]{2,1,0:T(8,128)}), f32[8,56,128]{2,1,0:T(8,128)S(1)}, u32[]{:S(2)}, u32[]{:S(2)}) async-start(f32[8,56,128]{2,1,0:T(8,128)} %copy-done.5), calls=%async_computation.1 | async-start | bytes 458752 | tf_op jit(solution)/shard_map/all_to_all | solution.py:463
  61.0 1.9 %collective-permute-start.6 = (f32[5,32,128]{2,1,0:T(8,128)}, f32[5,32,128]{2,1,0:T(8,128)S(1)}, u32[]{:S(2)}, u32[]{:S(2)}) collective-permute-start(f32[5,32,128]{2,1,0:T(8,128)} %copy-done.25), channel_id=1, source_target_pairs={{0,4},{4,0},{8,12},{12,8},{16,20},{20,16},{24,28},{28,24},{32,36},... | collective-permute-start | bytes 245768 | tf_op jit(solution)/shard_map/ppermute | solution.py:407
  63.0 4.3 %collective-permute-start.7 = (f32[5,32,128]{2,1,0:T(8,128)}, f32[5,32,128]{2,1,0:T(8,128)S(1)}, u32[]{:S(2)}, u32[]{:S(2)}) collective-permute-start(f32[5,32,128]{2,1,0:T(8,128)} %copy-done.24), channel_id=1, source_target_pairs={{4,8},{8,4},{12,16},{16,12},{20,24},{24,20},{28,32},{32,28},{36,40... | collective-permute-start | bytes 245768 | tf_op jit(solution)/shard_map/ppermute | solution.py:407
  67.3 5.2 %collective-permute-start.8 = (f32[5,16,128]{2,1,0:T(8,128)}, f32[5,16,128]{2,1,0:T(8,128)S(1)}, u32[]{:S(2)}, u32[]{:S(2)}) collective-permute-start(f32[5,16,128]{2,1,0:T(8,128)} %copy-done.27), channel_id=1, source_target_pairs={{0,1},{1,0},{2,3},{3,2},{4,5},{5,4},{6,7},{7,6},{8,9},{9,8},{10,11... | collective-permute-start | bytes 122888 | tf_op jit(solution)/shard_map/ppermute | solution.py:407
  72.5 0.7 collective-permute-start.9
  73.2 0.9 collective-permute-done.8.ze
  74.2 1.0 copy-done.2
  75.2 1.0 copy-done.3
  76.2 0.8 copy-done.13
  77.0 6.7 %second_step.1 = (f32[5,32,16,128]{3,2,1,0:T(8,128)}, f32[64,128]{1,0:T(8,128)S(1)}) custom-call(f32[8,56,128]{2,1,0:T(8,128)S(1)} %all-to-all-done.1.carried, f32[512,256]{1,0:T(8,128)S(1)} %copy-done.2, f32[5,32,16,128]{3,2,1,0:T(8,128)S(1)} %copy-done, f32[5,32,16,128]{3,2,1,0:T(8,128)S(1)} %get-tuple-element.21.base, f32[32,16,128]{2,1,0:T(8,128)S(1)} %copy-done.1, ...), custom_call_target="tpu_custom_call" | custom-call | tf_op jit(solution)/shard_map/second_step/pallas_call | solution.py:466
  83.7 20.8 %all_to_all.25 = f32[64,1,128]{2,1,0:T(1,128)S(1)} all-to-all(f32[64,1,128]{2,1,0:T(1,128)S(1)} %bitcast.16), channel_id=1, replica_groups=mesh['stream'=8,'span'=16,'vert'=4] {'span','vert'}, dimensions={0} | all-to-all | bytes 65536 | tf_op jit(solution)/shard_map/all_to_all | solution.py:492
  104.7 13.2 %all_to_all.26 = f32[8,1,128]{2,1,0:T(1,128)S(1)} all-to-all(f32[8,1,128]{2,1,0:T(1,128)S(1)} %broadcast_in_dim.2), channel_id=1, replica_groups=mesh['stream'=8,'span'=16,'vert'=4] {'stream'}, dimensions={0} | all-to-all | bytes 8192 | tf_op jit(solution)/shard_map/all_to_all | solution.py:494
  (57 shorter events, 8.1 us)
Async XLA Ops:
  0.6 20.9 %copy-start = (f32[5,32,16,128]{3,2,1,0:T(8,128)S(1)}, f32[5,32,16,128]{3,2,1,0:T(8,128)}, u32[]{:S(2)}) copy-start(f32[5,32,16,128]{3,2,1,0:T(8,128)} %fields.5) | copy-start | bytes 3932164
  0.6 1.1 copy-start.4
  1.7 0.9 copy-start.7
  2.6 0.8 copy-start.12
  3.5 0.7 copy-start.23
  6.5 36.8 %copy-start.1 = (f32[32,16,128]{2,1,0:T(8,128)S(1)}, f32[32,16,128]{2,1,0:T(8,128)}, u32[]{:S(2)}) copy-start(f32[32,16,128]{2,1,0:T(8,128)} %solid.3) | copy-start | bytes 786436
  6.5 36.8 %all-to-all-start = ((f32[64,16,128]{2,1,0:T(8,128)}), f32[64,16,128]{2,1,0:T(8,128)S(1)}, u32[]{:S(2)}, u32[]{:S(2)}) async-start(f32[64,16,128]{2,1,0:T(8,128)} %bitcast.2), calls=%async_computation | async-start | bytes 1048576 | tf_op jit(solution)/shard_map/all_to_all | solution.py:431
  22.5 19.5 %collective-permute-start.2 = (f32[5,32,128]{2,1,0:T(8,128)S(1)}, f32[5,32,128]{2,1,0:T(8,128)S(1)}, u32[]{:S(2)}, u32[]{:S(2)}) collective-permute-start(f32[5,32,128]{2,1,0:T(8,128)S(1)} %get-tuple-element.16), channel_id=1, source_target_pairs={{0,4},{4,0},{8,12},{12,8},{16,20},{20,16},{24,28},{28,24},{32,36},... | collective-permute-start | bytes 245768 | tf_op jit(solution)/shard_map/ppermute | solution.py:407
  24.9 17.8 %collective-permute-start.3 = (f32[5,32,128]{2,1,0:T(8,128)S(1)}, f32[5,32,128]{2,1,0:T(8,128)S(1)}, u32[]{:S(2)}, u32[]{:S(2)}) collective-permute-start(f32[5,32,128]{2,1,0:T(8,128)S(1)} %get-tuple-element.17), channel_id=1, source_target_pairs={{4,8},{8,4},{12,16},{16,12},{20,24},{24,20},{28,32},{32,28},{36,40... | collective-permute-start | bytes 245768 | tf_op jit(solution)/shard_map/ppermute | solution.py:407
  28.1 4.4 %collective-permute-start.1 = (f32[5,8,128]{2,1,0:T(8,128)S(1)}, f32[5,8,128]{2,1,0:T(8,128)S(1)}, u32[]{:S(2)}, u32[]{:S(2)}) collective-permute-start(f32[5,8,128]{2,1,0:T(8,128)S(1)} %get-tuple-element.15), channel_id=1, source_target_pairs={{64,128},{128,64},{192,256},{256,192},{320,384},{384,320},{65,129}... | collective-permute-start | bytes 61448 | tf_op jit(solution)/shard_map/ppermute | solution.py:407
  28.8 12.0 %collective-permute-start.4 = (f32[5,16,128]{2,1,0:T(8,128)S(1)}, f32[5,16,128]{2,1,0:T(8,128)S(1)}, u32[]{:S(2)}, u32[]{:S(2)}) collective-permute-start(f32[5,16,128]{2,1,0:T(8,128)S(1)} %get-tuple-element.18), channel_id=1, source_target_pairs={{0,1},{1,0},{2,3},{3,2},{4,5},{5,4},{6,7},{7,6},{8,9},{9,8},{10,11... | collective-permute-start | bytes 122888 | tf_op jit(solution)/shard_map/ppermute | solution.py:407
  31.9 9.5 %collective-permute-start.5 = (f32[5,16,128]{2,1,0:T(8,128)S(1)}, f32[5,16,128]{2,1,0:T(8,128)S(1)}, u32[]{:S(2)}, u32[]{:S(2)}) collective-permute-start(f32[5,16,128]{2,1,0:T(8,128)S(1)} %get-tuple-element.19), channel_id=1, source_target_pairs={{1,2},{2,1},{5,6},{6,5},{9,10},{10,9},{13,14},{14,13},{17,18},{18,... | collective-permute-start | bytes 122888 | tf_op jit(solution)/shard_map/ppermute | solution.py:407
  33.2 7.0 %collective-permute-start = (f32[5,8,128]{2,1,0:T(8,128)S(1)}, f32[5,8,128]{2,1,0:T(8,128)S(1)}, u32[]{:S(2)}, u32[]{:S(2)}) collective-permute-start(f32[5,8,128]{2,1,0:T(8,128)S(1)} %get-tuple-element.15), channel_id=1, source_target_pairs={{0,64},{64,0},{128,192},{192,128},{256,320},{320,256},{384,448},{4... | collective-permute-start | bytes 61448 | tf_op jit(solution)/shard_map/ppermute | solution.py:407
  42.7 0.6 copy-start.10
  43.3 0.9 copy-start.9
  44.2 0.9 copy-start.11
  45.1 0.8 copy-start.15
  45.8 0.8 copy-start.17
  46.6 0.7 copy-start.19
  47.4 0.7 copy-start.21
  48.1 26.1 %copy-start.6 = (s32[1,16,1,2048]{3,2,1,0:T(1,128)S(1)}, s32[1,16,1,2048]{3,2,1,0:T(1,128)}, u32[]{:S(2)}) copy-start(s32[1,16,1,2048]{3,2,1,0:T(1,128)} %strips.1) | copy-start | bytes 393220
  48.1 26.1 %copy-start.22 = (s32[1,1,1,2048]{3,2,1,0:T(1,128)S(1)}, s32[1,1,1,2048]{3,2,1,0:T(1,128)}, u32[]{:S(2)}) copy-start(s32[1,1,1,2048]{3,2,1,0:T(1,128)} %param.15) | copy-start | bytes 24580
  51.7 0.7 copy-start.5
  53.0 0.6 copy-start.25
  54.8 19.3 %all-to-all-start.1 = ((f32[8,56,128]{2,1,0:T(8,128)}), f32[8,56,128]{2,1,0:T(8,128)S(1)}, u32[]{:S(2)}, u32[]{:S(2)}) async-start(f32[8,56,128]{2,1,0:T(8,128)} %copy-done.5), calls=%async_computation.1 | async-start | bytes 458752 | tf_op jit(solution)/shard_map/all_to_all | solution.py:463
  61.0 13.1 %collective-permute-start.6 = (f32[5,32,128]{2,1,0:T(8,128)}, f32[5,32,128]{2,1,0:T(8,128)S(1)}, u32[]{:S(2)}, u32[]{:S(2)}) collective-permute-start(f32[5,32,128]{2,1,0:T(8,128)} %copy-done.25), channel_id=1, source_target_pairs={{0,4},{4,0},{8,12},{12,8},{16,20},{20,16},{24,28},{28,24},{32,36},... | collective-permute-start | bytes 245768 | tf_op jit(solution)/shard_map/ppermute | solution.py:407
  63.0 11.2 %collective-permute-start.7 = (f32[5,32,128]{2,1,0:T(8,128)}, f32[5,32,128]{2,1,0:T(8,128)S(1)}, u32[]{:S(2)}, u32[]{:S(2)}) collective-permute-start(f32[5,32,128]{2,1,0:T(8,128)} %copy-done.24), channel_id=1, source_target_pairs={{4,8},{8,4},{12,16},{16,12},{20,24},{24,20},{28,32},{32,28},{36,40... | collective-permute-start | bytes 245768 | tf_op jit(solution)/shard_map/ppermute | solution.py:407
  67.3 6.8 %collective-permute-start.8 = (f32[5,16,128]{2,1,0:T(8,128)}, f32[5,16,128]{2,1,0:T(8,128)S(1)}, u32[]{:S(2)}, u32[]{:S(2)}) collective-permute-start(f32[5,16,128]{2,1,0:T(8,128)} %copy-done.27), channel_id=1, source_target_pairs={{0,1},{1,0},{2,3},{3,2},{4,5},{5,4},{6,7},{7,6},{8,9},{9,8},{10,11... | collective-permute-start | bytes 122888 | tf_op jit(solution)/shard_map/ppermute | solution.py:407
  72.5 1.6 %collective-permute-start.9 = (f32[5,16,128]{2,1,0:T(8,128)}, f32[5,16,128]{2,1,0:T(8,128)S(1)}, u32[]{:S(2)}, u32[]{:S(2)}) collective-permute-start(f32[5,16,128]{2,1,0:T(8,128)} %copy-done.26), channel_id=1, source_target_pairs={{1,2},{2,1},{5,6},{6,5},{9,10},{10,9},{13,14},{14,13},{17,18},{18,... | collective-permute-start | bytes 122888 | tf_op jit(solution)/shard_map/ppermute | solution.py:407
  74.2 1.0 copy-start.2
  75.2 1.0 copy-start.3
  76.2 0.8 copy-start.13
  (8 other events, 4.9 us)

commit v3 on v2

--- a/solution.py
+++ b/solution.py
@@ -57,7 +57,25 @@
     return plane, edges.astype(np.float32), turn
 
 
-def sum_panels(panels, owner, turn, edge_table, out):
+def fetch(sources, targets, sems, at=0):
+    copies = [
+        pltpu.make_async_copy(a, b, sems.at[at + i])
+        for i, (a, b) in enumerate(zip(sources, targets))
+    ]
+    for c in copies:
+        c.start()
+    return copies
+
+
+def wait_all(copies):
+    for c in copies:
+        c.wait()
+
+
+def sum_panels(panels_h, owner_h, turn_h, edge_h, out, panels, owner, turn, edge_table, sems):
+    wait_all(
+        fetch((panels_h, owner_h, turn_h, edge_h), (panels, owner, turn, edge_table), sems)
+    )
     n_vert = lax.axis_size("vert")
     tiles = turn.shape[0]
     spec = turn.shape[1] // 2
@@ -213,9 +231,14 @@
     return jnp.where((lax.axis_index("stream") == 0) & (lane < cx // 2), weight, 0.0)
 
 
-def first_step(got, fields, solid, xe, xo, ye, yo, ze, zo, base, carry_out, ye1, yo1, ze1, zo1, q):
+def first_step(*refs):
+    fields, solid = refs[:2]
+    arrived, base, sent = refs[2:9], refs[9], refs[10:15]
+    q, kept, leaving, sems = refs[15], refs[16:23], refs[23:28], refs[28]
+    got, xe, xo, ye, yo, ze, zo = kept
+    carry_out, ye1, yo1, ze1, zo1 = leaving
     cz = fields.shape[1]
-    fill_ghosts(q, ye, yo, ze, zo)
+    coming = fetch(arrived, kept, sems)
 
     def fill(z, carry):
         for f in range(NF):
@@ -223,6 +246,8 @@
         return carry
 
     lax.fori_loop(0, cz, fill, 0, unroll=4)
+    wait_all(coming)
+    fill_ghosts(q, ye, yo, ze, zo)
     x_low = face_choice("stream")
     xg = ghosts_x(
         [jnp.where(x_low, xo[f], xe[f]) for f in range(NF)],
@@ -254,40 +279,32 @@
         for f in range(NF):
             carry_out[i, ROWS + 8 * f : ROWS + 8 * f + 8] = accs[f]
     store_faces(base, ye1, yo1, ze1, zo1)
-
-
-def second_step(
-    carried,
-    plane_table,
-    fields,
-    base,
-    solid,
-    ye,
-    yo,
-    ze,
-    zo,
-    cells,
-    geom,
-    strips,
-    shapes,
-    out,
-    modal,
-    q,
-    target,
-    geom_v,
-    strips_v,
-    sems,
-):
+    wait_all(fetch(leaving, sent, sems))
+
+
+def second_step(*refs):
+    fields, base, solid = refs[:3]
+    arrived, late = refs[3:9], refs[9:13]
+    out, modal, q, target = refs[13:17]
+    kept, late_kept, sems = refs[17:23], refs[23:27], refs[27]
+    carried, plane_table, ye, yo, ze, zo = kept
+    cells, geom_v, strips_v, shapes = late_kept
     cz, cy, cx = fields.shape[1:]
     spec = plane_table.shape[1] // 2
     n_stream = carried.shape[0]
     span_pos = lax.axis_index("span")
     vert_pos = lax.axis_index("vert")
     stream_pos = lax.axis_index("stream")
-    get_geom = pltpu.make_async_copy(geom.at[0, span_pos], geom_v, sems.at[0])
-    get_strips = pltpu.make_async_copy(strips.at[0, span_pos], strips_v, sems.at[1])
-    get_geom.start()
-    get_strips.start()
+    coming = fetch(arrived, kept, sems)
+    cells_h, geom_h, strips_h, shapes_h = late
+    rest = fetch(
+        (cells_h, geom_h.at[0, span_pos], strips_h.at[0, span_pos], shapes_h),
+        late_kept,
+        sems,
+        len(coming),
+    )
+
+    wait_all(coming)
     low, high = carried[0, 0:8], carried[0, 8:16]
     for i in range(1, n_stream):
         low = low + carried[i, 0:8]
@@ -322,7 +339,7 @@
 
     fill_ghosts(q, ye, yo, ze, zo, edge_push)
 
-    def fill(g, carry):
+    def pushing(g, carry):
         for i in range(4):
             z = g * 4 + i
             t = target[pl.ds(pl.multiple_of(z * cy, cy), cy), :]
@@ -332,7 +349,7 @@
                 out[f, z] = fields[f, z] + pushed
         return carry
 
-    lax.fori_loop(0, cz // 4, fill, 0)
+    lax.fori_loop(0, cz // 4, pushing, 0)
     west_at = jnp.maximum(stream_pos - 1, 0)
     east_at = jnp.minimum(stream_pos + 1, n_stream - 1)
     west, east = [], []
@@ -358,8 +375,7 @@
     p_hi = pressure.astype(jnp.bfloat16)
     p_lo = (pressure - p_hi.astype(jnp.float32)).astype(jnp.bfloat16)
     parts = jnp.concatenate([p_hi, p_lo], axis=0)
-    get_geom.wait()
-    get_strips.wait()
+    wait_all(rest)
     count = cells.shape[1]
     step = 512
     n_comp = geom_v.shape[0]
@@ -396,8 +412,15 @@
 
 
 VM = pl.BlockSpec(memory_space=pltpu.VMEM)
-AN = pl.BlockSpec(memory_space=pl.ANY)
-BIG = pltpu.CompilerParams(vmem_limit_bytes=16 * 1024 * 1024)
+HB = pl.BlockSpec(memory_space=pltpu.HBM)
+
+
+def room(mib):
+    return pltpu.CompilerParams(vmem_limit_bytes=mib * 1024 * 1024)
+
+
+def buffers(arrays):
+    return [pltpu.VMEM(x.shape, x.dtype) for x in arrays]
 
 
 def swapped(block, axis, odd):
@@ -417,17 +440,21 @@
     tiles = n_span * n_vert
     spec = panels.shape[2] // 2
     plane, edges, turn = wave_tables(cz, cy, n_span, n_vert, spec)
-    sent = pl.pallas_call(
-        sum_panels,
-        out_shape=f32(tiles * ROWS, 128),
-        compiler_params=BIG,
-        name="panel_sums",
-    )(
+    operands = (
         panels.transpose(1, 0, 2),
         panel_owner.reshape(1, -1),
         jnp.asarray(turn),
         jnp.asarray(edges),
     )
+    sent = pl.pallas_call(
+        sum_panels,
+        out_shape=f32(tiles * ROWS, 128),
+        in_specs=[HB] * 4,
+        out_specs=VM,
+        scratch_shapes=buffers(operands) + [pltpu.SemaphoreType.DMA((4,))],
+        compiler_params=room(60),
+        name="panel_sums",
+    )(*operands)
     got = lax.all_to_all(
         sent.reshape(tiles, ROWS, 128), ("span", "vert"), 0, 0, tiled=True
     ).reshape(tiles * ROWS, 128)
@@ -446,48 +473,51 @@
         out_shape=(f32(NF, 8, 128),) + yz_shapes,
         in_specs=[VM],
         out_specs=(VM,) * 5,
-        compiler_params=BIG,
+        compiler_params=room(52),
         name="pack_faces",
     )(fields)
     ghosts = (swapped(xf, "stream", 0), swapped(xf, "stream", 1)) + swap_yz(*faces)
     scratch = pltpu.VMEM((NF, cz + 2, 32, cx), jnp.float32)
+    arrived = (got,) + ghosts
+    leaving = (f32(n_stream, ROWS + 8 * NF, 128),) + yz_shapes
     base, carry, *faces = pl.pallas_call(
         first_step,
-        out_shape=(f32(NF, cz, cy, cx), f32(n_stream, ROWS + 8 * NF, 128)) + yz_shapes,
-        in_specs=[VM] * 9,
-        out_specs=(VM,) * 6,
-        scratch_shapes=[scratch],
-        compiler_params=BIG,
+        out_shape=(f32(NF, cz, cy, cx),) + leaving,
+        in_specs=[VM] * 2 + [HB] * 7,
+        out_specs=(VM,) + (HB,) * 5,
+        scratch_shapes=[scratch]
+        + buffers(arrived)
+        + buffers(leaving)
+        + [pltpu.SemaphoreType.DMA((7,))],
+        compiler_params=room(52),
         name="first_step",
-    )(got, fields, solid_frac, *ghosts)
+    )(fields, solid_frac, *arrived)
     carried = lax.all_to_all(carry, "stream", 0, 0, tiled=True)
     ghosts = swap_yz(*faces)
     deck = deck_cells.shape[3]
+    arrived = (carried, jnp.asarray(plane)) + ghosts
+    cells = deck_cells.reshape(1, deck)
+    shapes = mode_shapes.transpose(0, 2, 1)
     new_fields, modal = pl.pallas_call(
         second_step,
         out_shape=(f32(NF, cz, cy, cx), f32(tiles, 128)),
-        in_specs=[VM] * 10 + [AN, AN, VM],
+        in_specs=[VM] * 3 + [HB] * 10,
         out_specs=(VM, VM),
-        scratch_shapes=[
-            scratch,
-            pltpu.VMEM((cz * cy, 8), jnp.float32),
-            pltpu.VMEM((3, 1, deck), jnp.float32),
-            pltpu.VMEM((1, deck), jnp.int32),
-            pltpu.SemaphoreType.DMA((2,)),
-        ],
-        compiler_params=BIG,
+        scratch_shapes=[scratch, pltpu.VMEM((cz * cy, 8), jnp.float32)]
+        + buffers(arrived)
+        + buffers((cells, f32(3, 1, deck), strip_ids[0, 0], shapes))
+        + [pltpu.SemaphoreType.DMA((10,))],
+        compiler_params=room(52),
         name="second_step",
     )(
-        carried,
-        jnp.asarray(plane),
         fields,
         base,
         solid_frac,
-        *ghosts,
-        deck_cells.reshape(1, deck),
+        *arrived,
+        cells,
         deck_geom.transpose(0, 1, 3, 2, 4),
         strip_ids,
-        mode_shapes.transpose(0, 2, 1),
+        shapes,
     )
     part = lax.all_to_all(modal, ("span", "vert"), 0, 0, tiled=True)
     part = jnp.broadcast_to(jnp.sum(part, axis=0, keepdims=True), (n_stream, 128))

time: 120 us -> 108 us (0.900)
  local copies, waits for them, and re-layouts: 17.9 us -> 0.05 us
  Pallas kernels: 13.7 us -> 20.2 us
    unnamed x56 -> x14, local copies, waits for them, and re-layouts: 17.9 us -> 0.04 us
    pallas_call x2, Pallas kernels: 5.97 us -> 10.7 us  [the longest x1 7.1 us: on_device(): pl.pallas_call(first_step, out_shape=(f32(NF, cz, cy, cx),) + leaving, in...]
    pallas_call x1, Pallas kernels: 6.72 us -> 8.45 us  [on_device(): pl.pallas_call(second_step, out_shape=(f32(NF, cz, cy, cx), f32(tiles, 12...]
where the time goes in v3:
time: 108 us; the launch traced here: 107 us
  starting transfers between devices  48.9 us (45%)
  blocking collectives  34.1 us (32%)
  Pallas kernels  20.2 us (19%)
  waiting for transfers between devices  2.18 us (2%)
    ppermute x10, starting transfers between devices, swapped(): return lax.ppermute(block, axis, pairs)  27.9 us
    all_to_all x1, blocking collectives, on_device(): part = lax.all_to_all(modal, ('span', 'vert'), 0, 0, tiled=True)  20.8 us
    all_to_all x1, starting transfers between devices, on_device(): lax.all_to_all(sent.reshape(tiles, ROWS, 128), ('span', 'vert'), 0, 0, ti...  15 us
    all_to_all x1, blocking collectives, on_device(): part = lax.all_to_all(part, 'stream', 0, 0, tiled=True)  13.2 us
    pallas_call x1, Pallas kernels, on_device(): pl.pallas_call(second_step, out_shape=(f32(NF, cz, cy, cx), f32(tiles, 12...  8.45 us
    pallas_call x1, Pallas kernels, on_device(): pl.pallas_call(first_step, out_shape=(f32(NF, cz, cy, cx),) + leaving, in...  7.1 us
    all_to_all x1, starting transfers between devices, on_device(): carried = lax.all_to_all(carry, 'stream', 0, 0, tiled=True)  6.02 us
    pallas_call x1, Pallas kernels, on_device(): pl.pallas_call(sum_panels, out_shape=f32(tiles * ROWS, 128), in_specs=[HB...  3.59 us
  transfers between devices with their start and end apart: 12, of which 2 were waited for; matrix products, arithmetic and copies ran while one was open for 0% of the time, Pallas kernels for 1%

profile of v3, /device:TPU:1, one launch (start us, length us, event | category | flops | bytes accessed | tf_op | source)
XLA Modules:
  0.0 106.9 jit_solution(4115547645897475318)
XLA Ops:
  0.6 0.0 copy-start
  0.6 3.6 %panel_sums.1 = f32[1024,128]{1,0:T(8,128)} custom-call(f32[5,64,256]{2,1,0:T(8,128)} %bitcast.18, s32[1,64]{1,0:T(1,128)} %bitcast.20, f32[64,256]{1,0:T(8,128)} %constant.8.clone.turn_h, f32[256,128]{1,0:T(8,128)} %constant.9.clone.edge_h), custom_call_target="tpu_custom_call" | custom-call | tf_op jit(solution)/shard_map/panel_sums/pallas_call | solution.py:449
  4.2 0.0 copy-start.1
  4.3 15.0 %all-to-all-start = ((f32[64,16,128]{2,1,0:T(8,128)}), f32[64,16,128]{2,1,0:T(8,128)S(1)}, u32[]{:S(2)}, u32[]{:S(2)}) async-start(f32[64,16,128]{2,1,0:T(8,128)} %bitcast.17), calls=%async_computation | async-start | bytes 1048576 | tf_op jit(solution)/shard_map/all_to_all | solution.py:458
  19.3 1.0 pack_faces.1
  20.3 2.4 %collective-permute-start.2 = (f32[5,32,128]{2,1,0:T(8,128)S(1)}, f32[5,32,128]{2,1,0:T(8,128)S(1)}, u32[]{:S(2)}, u32[]{:S(2)}) collective-permute-start(f32[5,32,128]{2,1,0:T(8,128)S(1)} %get-tuple-element.16), channel_id=1, source_target_pairs={{0,4},{4,0},{8,12},{12,8},{16,20},{20,16},{24,28},{28,24},{32,36},... | collective-permute-start | bytes 245768 | tf_op jit(solution)/shard_map/ppermute | solution.py:430
  22.6 3.2 %collective-permute-start.3 = (f32[5,32,128]{2,1,0:T(8,128)S(1)}, f32[5,32,128]{2,1,0:T(8,128)S(1)}, u32[]{:S(2)}, u32[]{:S(2)}) collective-permute-start(f32[5,32,128]{2,1,0:T(8,128)S(1)} %get-tuple-element.17), channel_id=1, source_target_pairs={{4,8},{8,4},{12,16},{16,12},{20,24},{24,20},{28,32},{32,28},{36,40... | collective-permute-start | bytes 245768 | tf_op jit(solution)/shard_map/ppermute | solution.py:430
  25.9 0.7 collective-permute-start.1
  26.6 3.1 %collective-permute-start.4 = (f32[5,16,128]{2,1,0:T(8,128)S(1)}, f32[5,16,128]{2,1,0:T(8,128)S(1)}, u32[]{:S(2)}, u32[]{:S(2)}) collective-permute-start(f32[5,16,128]{2,1,0:T(8,128)S(1)} %get-tuple-element.18), channel_id=1, source_target_pairs={{0,1},{1,0},{2,3},{3,2},{4,5},{5,4},{6,7},{7,6},{8,9},{9,8},{10,11... | collective-permute-start | bytes 122888 | tf_op jit(solution)/shard_map/ppermute | solution.py:430
  29.7 0.7 collective-permute-start.5
  30.3 0.0 collective-permute-done.1.refs_4_
  30.3 5.7 %collective-permute-start = (f32[5,8,128]{2,1,0:T(8,128)S(1)}, f32[5,8,128]{2,1,0:T(8,128)S(1)}, u32[]{:S(2)}, u32[]{:S(2)}) collective-permute-start(f32[5,8,128]{2,1,0:T(8,128)S(1)} %get-tuple-element.15), channel_id=1, source_target_pairs={{0,64},{64,0},{128,192},{192,128},{256,320},{320,256},{384,448},{4... | collective-permute-start | bytes 61448 | tf_op jit(solution)/shard_map/ppermute | solution.py:430
  36.1 1.5 %collective-permute-done.refs_3_ = f32[5,8,128]{2,1,0:T(8,128)S(1)} collective-permute-done((f32[5,8,128]{2,1,0:T(8,128)S(1)}, f32[5,8,128]{2,1,0:T(8,128)S(1)}, u32[]{:S(2)}, u32[]{:S(2)}) %collective-permute-start) | collective-permute-done | bytes 20512 | tf_op jit(solution)/shard_map/ppermute | solution.py:430
  37.6 0.0 collective-permute-done.3.refs_6_
  37.6 0.0 copy-start.2
  37.6 0.0 copy-start.3
  37.6 0.0 copy-start.4
  37.6 0.0 copy-start.5
  37.6 0.0 copy-start.6
  37.7 7.1 %first_step.1 = (f32[5,32,16,128]{3,2,1,0:T(8,128)}, f32[8,56,128]{2,1,0:T(8,128)}, f32[5,32,128]{2,1,0:T(8,128)S(1)}, f32[5,32,128]{2,1,0:T(8,128)S(1)}, f32[5,...) custom-call(f32[5,32,16,128]{3,2,1,0:T(8,128)} %refs_0_.3, f32[32,16,128]{2,1,0:T(8,128)S(1)} %copy-done.1, ...), custom_call_target="tpu_custom_call" | custom-call | tf_op jit(solution)/shard_map/first_step/pallas_call | solution.py:483
  44.8 6.0 %all-to-all-start.1 = ((f32[8,56,128]{2,1,0:T(8,128)}), f32[8,56,128]{2,1,0:T(8,128)S(1)}, u32[]{:S(2)}, u32[]{:S(2)}) async-start(f32[8,56,128]{2,1,0:T(8,128)} %get-tuple-element.21), calls=%async_computation.1 | async-start | bytes 458752 | tf_op jit(solution)/shard_map/all_to_all | solution.py:495
  50.8 3.7 %collective-permute-start.6 = (f32[5,32,128]{2,1,0:T(8,128)S(1)}, f32[5,32,128]{2,1,0:T(8,128)S(1)}, u32[]{:S(2)}, u32[]{:S(2)}) collective-permute-start(f32[5,32,128]{2,1,0:T(8,128)S(1)} %get-tuple-element.22), channel_id=1, source_target_pairs={{0,4},{4,0},{8,12},{12,8},{16,20},{20,16},{24,28},{28,24},{32,36},... | collective-permute-start | bytes 245768 | tf_op jit(solution)/shard_map/ppermute | solution.py:430
  54.5 2.5 %collective-permute-start.7 = (f32[5,32,128]{2,1,0:T(8,128)S(1)}, f32[5,32,128]{2,1,0:T(8,128)S(1)}, u32[]{:S(2)}, u32[]{:S(2)}) collective-permute-start(f32[5,32,128]{2,1,0:T(8,128)S(1)} %get-tuple-element.23), channel_id=1, source_target_pairs={{4,8},{8,4},{12,16},{16,12},{20,24},{24,20},{28,32},{32,28},{36,40... | collective-permute-start | bytes 245768 | tf_op jit(solution)/shard_map/ppermute | solution.py:430
  57.0 5.3 %collective-permute-start.8 = (f32[5,16,128]{2,1,0:T(8,128)S(1)}, f32[5,16,128]{2,1,0:T(8,128)S(1)}, u32[]{:S(2)}, u32[]{:S(2)}) collective-permute-start(f32[5,16,128]{2,1,0:T(8,128)S(1)} %get-tuple-element.24), channel_id=1, source_target_pairs={{0,1},{1,0},{2,3},{3,2},{4,5},{5,4},{6,7},{7,6},{8,9},{9,8},{10,11... | collective-permute-start | bytes 122888 | tf_op jit(solution)/shard_map/ppermute | solution.py:430
  62.3 0.7 collective-permute-start.9
  63.0 0.7 collective-permute-done.8.refs_7_
  63.7 0.0 collective-permute-done.9.refs_8_
  63.8 8.5 %second_step.1 = (f32[5,32,16,128]{3,2,1,0:T(8,128)}, f32[64,128]{1,0:T(8,128)S(1)}) custom-call(f32[5,32,16,128]{3,2,1,0:T(8,128)} %refs_0_.3, f32[5,32,16,128]{3,2,1,0:T(8,128)} %get-tuple-element.20.refs_1_, f32[32,16,128]{2,1,0:T(8,128)S(1)} %copy-done.1, f32[8,56,128]{2,1,0:T(8,128)S(1)} %all-to-all-done.1.refs_3_, f32[512,256]{1,0:T(8,128)S(1)} %copy-done.2, ...), custom_call_target="tpu_custom_call" | custom-call | tf_op jit(solution)/shard_map/second_step/pallas_call | solution.py:501
  72.2 20.8 %all_to_all.25 = f32[64,1,128]{2,1,0:T(1,128)S(1)} all-to-all(f32[64,1,128]{2,1,0:T(1,128)S(1)} %bitcast.15), channel_id=1, replica_groups=mesh['stream'=8,'span'=16,'vert'=4] {'span','vert'}, dimensions={0} | all-to-all | bytes 65536 | tf_op jit(solution)/shard_map/all_to_all | solution.py:522
  93.1 0.1 reduce_sum.18
  93.1 13.2 %all_to_all.26 = f32[8,1,128]{2,1,0:T(1,128)S(1)} all-to-all(f32[8,1,128]{2,1,0:T(1,128)S(1)} %broadcast_in_dim.2), channel_id=1, replica_groups=mesh['stream'=8,'span'=16,'vert'=4] {'stream'}, dimensions={0} | all-to-all | bytes 8192 | tf_op jit(solution)/shard_map/all_to_all | solution.py:524
  106.4 0.5 reduce_sum.19
  (15 shorter events, 0.0 us)
Async XLA Ops:
  0.6 18.6 %copy-start = (f32[5,32,16,128]{3,2,1,0:T(8,128)S(1)}, f32[5,32,16,128]{3,2,1,0:T(8,128)}, u32[]{:S(2)}) copy-start(f32[5,32,16,128]{3,2,1,0:T(8,128)} %refs_0_.3) | copy-start | bytes 3932164
  4.2 33.3 %copy-start.1 = (f32[32,16,128]{2,1,0:T(8,128)S(1)}, f32[32,16,128]{2,1,0:T(8,128)}, u32[]{:S(2)}) copy-start(f32[32,16,128]{2,1,0:T(8,128)} %refs_2_.1) | copy-start | bytes 786436
  4.3 33.3 %all-to-all-start = ((f32[64,16,128]{2,1,0:T(8,128)}), f32[64,16,128]{2,1,0:T(8,128)S(1)}, u32[]{:S(2)}, u32[]{:S(2)}) async-start(f32[64,16,128]{2,1,0:T(8,128)} %bitcast.17), calls=%async_computation | async-start | bytes 1048576 | tf_op jit(solution)/shard_map/all_to_all | solution.py:458
  20.3 17.3 %collective-permute-start.2 = (f32[5,32,128]{2,1,0:T(8,128)S(1)}, f32[5,32,128]{2,1,0:T(8,128)S(1)}, u32[]{:S(2)}, u32[]{:S(2)}) collective-permute-start(f32[5,32,128]{2,1,0:T(8,128)S(1)} %get-tuple-element.16), channel_id=1, source_target_pairs={{0,4},{4,0},{8,12},{12,8},{16,20},{20,16},{24,28},{28,24},{32,36},... | collective-permute-start | bytes 245768 | tf_op jit(solution)/shard_map/ppermute | solution.py:430
  22.6 14.9 %collective-permute-start.3 = (f32[5,32,128]{2,1,0:T(8,128)S(1)}, f32[5,32,128]{2,1,0:T(8,128)S(1)}, u32[]{:S(2)}, u32[]{:S(2)}) collective-permute-start(f32[5,32,128]{2,1,0:T(8,128)S(1)} %get-tuple-element.17), channel_id=1, source_target_pairs={{4,8},{8,4},{12,16},{16,12},{20,24},{24,20},{28,32},{32,28},{36,40... | collective-permute-start | bytes 245768 | tf_op jit(solution)/shard_map/ppermute | solution.py:430
  25.9 4.4 %collective-permute-start.1 = (f32[5,8,128]{2,1,0:T(8,128)S(1)}, f32[5,8,128]{2,1,0:T(8,128)S(1)}, u32[]{:S(2)}, u32[]{:S(2)}) collective-permute-start(f32[5,8,128]{2,1,0:T(8,128)S(1)} %get-tuple-element.15), channel_id=1, source_target_pairs={{64,128},{128,64},{192,256},{256,192},{320,384},{384,320},{65,129}... | collective-permute-start | bytes 61448 | tf_op jit(solution)/shard_map/ppermute | solution.py:430
  26.6 11.0 %collective-permute-start.4 = (f32[5,16,128]{2,1,0:T(8,128)S(1)}, f32[5,16,128]{2,1,0:T(8,128)S(1)}, u32[]{:S(2)}, u32[]{:S(2)}) collective-permute-start(f32[5,16,128]{2,1,0:T(8,128)S(1)} %get-tuple-element.18), channel_id=1, source_target_pairs={{0,1},{1,0},{2,3},{3,2},{4,5},{5,4},{6,7},{7,6},{8,9},{9,8},{10,11... | collective-permute-start | bytes 122888 | tf_op jit(solution)/shard_map/ppermute | solution.py:430
  29.7 7.9 %collective-permute-start.5 = (f32[5,16,128]{2,1,0:T(8,128)S(1)}, f32[5,16,128]{2,1,0:T(8,128)S(1)}, u32[]{:S(2)}, u32[]{:S(2)}) collective-permute-start(f32[5,16,128]{2,1,0:T(8,128)S(1)} %get-tuple-element.19), channel_id=1, source_target_pairs={{1,2},{2,1},{5,6},{6,5},{9,10},{10,9},{13,14},{14,13},{17,18},{18,... | collective-permute-start | bytes 122888 | tf_op jit(solution)/shard_map/ppermute | solution.py:430
  30.3 7.2 %collective-permute-start = (f32[5,8,128]{2,1,0:T(8,128)S(1)}, f32[5,8,128]{2,1,0:T(8,128)S(1)}, u32[]{:S(2)}, u32[]{:S(2)}) collective-permute-start(f32[5,8,128]{2,1,0:T(8,128)S(1)} %get-tuple-element.15), channel_id=1, source_target_pairs={{0,64},{64,0},{128,192},{192,128},{256,320},{320,256},{384,448},{4... | collective-permute-start | bytes 61448 | tf_op jit(solution)/shard_map/ppermute | solution.py:430
  37.6 26.1 %copy-start.2 = (f32[512,256]{1,0:T(8,128)S(1)}, f32[512,256]{1,0:T(8,128)}, u32[]{:S(2)}) copy-start(f32[512,256]{1,0:T(8,128)} %constant.10.clone.refs_4_) | copy-start | bytes 1572868
  37.6 26.1 %copy-start.3 = (f32[1,16,1,3,2048]{4,2,3,1,0:T(1,128)S(1)}, f32[1,16,1,3,2048]{4,2,3,1,0:T(1,128)}, u32[]{:S(2)}) copy-start(f32[1,16,1,3,2048]{4,2,3,1,0:T(1,128)} %param.16) | copy-start | bytes 1179652
  37.6 26.1 %copy-start.4 = (s32[1,16,1,2048]{3,2,1,0:T(1,128)S(1)}, s32[1,16,1,2048]{3,2,1,0:T(1,128)}, u32[]{:S(2)}) copy-start(s32[1,16,1,2048]{3,2,1,0:T(1,128)} %refs_11_.1) | copy-start | bytes 393220
  37.6 26.1 %copy-start.5 = (f32[3,64,32]{1,2,0:T(8,128)S(1)}, f32[3,64,32]{1,2,0:T(8,128)}, u32[]{:S(2)}) copy-start(f32[3,64,32]{1,2,0:T(8,128)} %param.18) | copy-start | bytes 73732
  37.6 26.1 %copy-start.6 = (s32[1,1,1,2048]{3,2,1,0:T(1,128)S(1)}, s32[1,1,1,2048]{3,2,1,0:T(1,128)}, u32[]{:S(2)}) copy-start(s32[1,1,1,2048]{3,2,1,0:T(1,128)} %param.15) | copy-start | bytes 24580
  44.8 18.9 %all-to-all-start.1 = ((f32[8,56,128]{2,1,0:T(8,128)}), f32[8,56,128]{2,1,0:T(8,128)S(1)}, u32[]{:S(2)}, u32[]{:S(2)}) async-start(f32[8,56,128]{2,1,0:T(8,128)} %get-tuple-element.21), calls=%async_computation.1 | async-start | bytes 458752 | tf_op jit(solution)/shard_map/all_to_all | solution.py:495
  50.8 12.9 %collective-permute-start.6 = (f32[5,32,128]{2,1,0:T(8,128)S(1)}, f32[5,32,128]{2,1,0:T(8,128)S(1)}, u32[]{:S(2)}, u32[]{:S(2)}) collective-permute-start(f32[5,32,128]{2,1,0:T(8,128)S(1)} %get-tuple-element.22), channel_id=1, source_target_pairs={{0,4},{4,0},{8,12},{12,8},{16,20},{20,16},{24,28},{28,24},{32,36},... | collective-permute-start | bytes 245768 | tf_op jit(solution)/shard_map/ppermute | solution.py:430
  54.5 9.2 %collective-permute-start.7 = (f32[5,32,128]{2,1,0:T(8,128)S(1)}, f32[5,32,128]{2,1,0:T(8,128)S(1)}, u32[]{:S(2)}, u32[]{:S(2)}) collective-permute-start(f32[5,32,128]{2,1,0:T(8,128)S(1)} %get-tuple-element.23), channel_id=1, source_target_pairs={{4,8},{8,4},{12,16},{16,12},{20,24},{24,20},{28,32},{32,28},{36,40... | collective-permute-start | bytes 245768 | tf_op jit(solution)/shard_map/ppermute | solution.py:430
  57.0 6.6 %collective-permute-start.8 = (f32[5,16,128]{2,1,0:T(8,128)S(1)}, f32[5,16,128]{2,1,0:T(8,128)S(1)}, u32[]{:S(2)}, u32[]{:S(2)}) collective-permute-start(f32[5,16,128]{2,1,0:T(8,128)S(1)} %get-tuple-element.24), channel_id=1, source_target_pairs={{0,1},{1,0},{2,3},{3,2},{4,5},{5,4},{6,7},{7,6},{8,9},{9,8},{10,11... | collective-permute-start | bytes 122888 | tf_op jit(solution)/shard_map/ppermute | solution.py:430
  62.3 1.4 %collective-permute-start.9 = (f32[5,16,128]{2,1,0:T(8,128)S(1)}, f32[5,16,128]{2,1,0:T(8,128)S(1)}, u32[]{:S(2)}, u32[]{:S(2)}) collective-permute-start(f32[5,16,128]{2,1,0:T(8,128)S(1)} %get-tuple-element.25), channel_id=1, source_target_pairs={{1,2},{2,1},{5,6},{6,5},{9,10},{10,9},{13,14},{14,13},{17,18},{18,... | collective-permute-start | bytes 122888 | tf_op jit(solution)/shard_map/ppermute | solution.py:430

commit v4 on v3

--- a/solution.py
+++ b/solution.py
@@ -2,6 +2,7 @@
 
 import jax
 import jax.numpy as jnp
+import ml_dtypes
 import numpy as np
 from jax import lax
 from jax.experimental import pallas as pl
@@ -27,6 +28,20 @@
     return lax.dot_general(
         a, b, (dims, ((), ())), precision=HI, preferred_element_type=jnp.float32
     )
+
+
+def split_np(a):
+    hi = a.astype(ml_dtypes.bfloat16)
+    return hi, (a - hi.astype(np.float32)).astype(ml_dtypes.bfloat16)
+
+
+def split(a):
+    hi = a.astype(jnp.bfloat16)
+    return hi, (a - hi.astype(jnp.float32)).astype(jnp.bfloat16)
+
+
+def bdot(a, b, dims):
+    return lax.dot_general(a, b, (dims, ((), ())), preferred_element_type=jnp.float32)
 
 
 def wave_tables(cz, cy, n_span, n_vert, spec):
@@ -54,7 +69,11 @@
         at += part.shape[0]
     s, v = np.repeat(np.arange(n_span), n_vert), np.tile(np.arange(n_vert), n_span)
     turn = basis(1.0 * v * cz, 1.0 * s * cy).astype(np.float32)
-    return plane, edges.astype(np.float32), turn
+    hi, lo = split_np(plane)
+    plane = np.concatenate([hi, lo, hi], axis=1)
+    hi, lo = split_np(edges.astype(np.float32))
+    edges = np.concatenate([hi, lo, hi], axis=0)
+    return plane, edges, turn
 
 
 def fetch(sources, targets, sems, at=0):
@@ -80,19 +99,25 @@
     tiles = turn.shape[0]
     spec = turn.shape[1] // 2
     held = owner.shape[1]
-    named = (owner[...] == lax.broadcasted_iota(jnp.int32, (tiles, held), 0)).astype(jnp.float32)
+    named = jnp.where(
+        owner[...] == lax.broadcasted_iota(jnp.int32, (tiles, held), 0), 1.0, 0.0
+    ).astype(jnp.bfloat16)
+    named = jnp.concatenate([named, named], axis=1)
     cos_t, sin_t = turn[:, :spec], turn[:, spec:]
-    lane = lax.broadcasted_iota(jnp.int32, (tiles, 128), 1)
-    for f in range(NF):
-        total = mdot(named, panels[f], ((1,), (0,)))
+    turned = []
+    for f in range(NF):
+        total = bdot(named, jnp.concatenate(split(panels[f]), axis=0), ((1,), (0,)))
         c, s = total[:, :spec], total[:, spec:]
         c2 = c * cos_t + s * sin_t
         s2 = s * cos_t - c * sin_t
         out[pl.ds(f, tiles, stride=ROWS), :] = c2
         out[pl.ds(8 + f, tiles, stride=ROWS), :] = s2
-        e = mdot(c2, edge_table[:spec, :], ((1,), (0,))) + mdot(
-            s2, edge_table[spec:, :], ((1,), (0,))
-        )
+        turned.append(jnp.concatenate([c2, s2], axis=1))
+    hi, lo = split(jnp.concatenate(turned, axis=0))
+    edge = bdot(jnp.concatenate([hi, hi, lo], axis=1), edge_table[...], ((1,), (0,)))
+    lane = lax.broadcasted_iota(jnp.int32, (tiles, 128), 1)
+    for f in range(NF):
+        e = edge[f * tiles : (f + 1) * tiles]
         row = jnp.where(
             lane < 32,
             jnp.roll(e, n_vert, 0),
@@ -233,8 +258,8 @@
 
 def first_step(*refs):
     fields, solid = refs[:2]
-    arrived, base, sent = refs[2:9], refs[9], refs[10:15]
-    q, kept, leaving, sems = refs[15], refs[16:23], refs[23:28], refs[28]
+    arrived, base_out, sent = refs[2:9], refs[9], refs[10:15]
+    q, kept, leaving, base, sems, base_sems = refs[15], refs[16:23], refs[23:28], *refs[28:31]
     got, xe, xo, ye, yo, ze, zo = kept
     carry_out, ye1, yo1, ze1, zo1 = leaving
     cz = fields.shape[1]
@@ -246,7 +271,7 @@
         return carry
 
     lax.fori_loop(0, cz, fill, 0, unroll=4)
-    wait_all(coming)
+    wait_all(coming[1:])
     fill_ghosts(q, ye, yo, ze, zo)
     x_low = face_choice("stream")
     xg = ghosts_x(
@@ -268,9 +293,14 @@
                 b = cs[f] + time_step * rs[f]
                 base[f, z] = b
                 parts[f] = packed_x(parts[f], b, i)
+        chunk = pl.ds(pl.multiple_of(g * INNER, INNER), INNER)
+        pltpu.make_async_copy(base.at[:, chunk], base_out.at[:, chunk], base_sems.at[g]).start()
         return tuple(placed(accs[f], parts[f], g) for f in range(NF))
 
     accs = lax.fori_loop(0, cz // INNER, body, (zero,) * NF)
+    store_faces(base, ye1, yo1, ze1, zo1)
+    going = fetch(leaving[1:], sent[1:], sems, 1)
+    coming[0].wait()
     total = got[0:ROWS]
     for i in range(1, got.shape[0] // ROWS):
         total = total + got[ROWS * i : ROWS * i + ROWS]
@@ -278,24 +308,27 @@
         carry_out[i, 0:ROWS] = total
         for f in range(NF):
             carry_out[i, ROWS + 8 * f : ROWS + 8 * f + 8] = accs[f]
-    store_faces(base, ye1, yo1, ze1, zo1)
-    wait_all(fetch(leaving, sent, sems))
+    wait_all(going + fetch(leaving[:1], sent[:1], sems))
+    for g in range(cz // INNER):
+        chunk = pl.ds(g * INNER, INNER)
+        pltpu.make_async_copy(base.at[:, chunk], base_out.at[:, chunk], base_sems.at[g]).wait()
 
 
 def second_step(*refs):
-    fields, base, solid = refs[:3]
+    fields, solid, base = refs[:3]
     arrived, late = refs[3:9], refs[9:13]
-    out, modal, q, target = refs[13:17]
-    kept, late_kept, sems = refs[17:23], refs[23:27], refs[27]
+    out_h, modal, q, target = refs[13:17]
+    kept, late_kept, out, sems, out_sems = refs[17:23], refs[23:27], *refs[27:30]
     carried, plane_table, ye, yo, ze, zo = kept
     cells, geom_v, strips_v, shapes = late_kept
     cz, cy, cx = fields.shape[1:]
-    spec = plane_table.shape[1] // 2
     n_stream = carried.shape[0]
     span_pos = lax.axis_index("span")
     vert_pos = lax.axis_index("vert")
     stream_pos = lax.axis_index("stream")
     coming = fetch(arrived, kept, sems)
+    get_base = pltpu.make_async_copy(base, q.at[:, 1 : cz + 1, 8:24, :], out_sems.at[0])
+    get_base.start()
     cells_h, geom_h, strips_h, shapes_h = late
     rest = fetch(
         (cells_h, geom_h.at[0, span_pos], strips_h.at[0, span_pos], shapes_h),
@@ -304,23 +337,23 @@
         len(coming),
     )
 
-    wait_all(coming)
+    wait_all(coming[:2])
     low, high = carried[0, 0:8], carried[0, 8:16]
     for i in range(1, n_stream):
         low = low + carried[i, 0:8]
         high = high + carried[i, 8:16]
     one = jnp.where(lane_ids((1, 8)) == 0, 1.0, 0.0)
+    hi, lo = split(jnp.concatenate([low, high], axis=1))
     target[...] = (
-        mdot(plane_table[:, :spec], low, ((1,), (1,)))
-        + mdot(plane_table[:, spec:], high, ((1,), (1,)))
-        + one
+        bdot(plane_table[...], jnp.concatenate([hi, hi, lo], axis=1), ((1,), (1,))) + one
     )
     n_edge = 2 * cz + 2 * cy
     pick = (
         lax.broadcasted_iota(jnp.int32, (n_edge, 128), 0) == lane_ids((n_edge, 128))
-    ).astype(jnp.float32)
-    e_low = mdot(pick, low, ((1,), (1,)))
-    e_high = mdot(pick, high, ((1,), (1,)))
+    ).astype(jnp.bfloat16)
+    pick = jnp.concatenate([pick, pick], axis=1)
+    e_low = bdot(pick, jnp.concatenate(split(low), axis=1), ((1,), (1,)))
+    e_high = bdot(pick, jnp.concatenate(split(high), axis=1), ((1,), (1,)))
     relax = relax_weights(cx)
     decay = (6.0 * viscous + relax, 6.0 * heat_diff + relax)
     push = time_step * relax
@@ -337,7 +370,9 @@
             jnp.where(vert_pos < lax.axis_size("vert") - 1, col[2 * cz + cy :], 0.0),
         )
 
+    wait_all(coming[2:])
     fill_ghosts(q, ye, yo, ze, zo, edge_push)
+    get_base.wait()
 
     def pushing(g, carry):
         for i in range(4):
@@ -345,7 +380,7 @@
             t = target[pl.ds(pl.multiple_of(z * cy, cy), cy), :]
             for f in range(NF):
                 pushed = push * t[:, f : f + 1]
-                q[f, z + 1, 8:24, :] = base[f, z] + pushed
+                q[f, z + 1, 8:24, :] = q[f, z + 1, 8:24, :] + pushed
                 out[f, z] = fields[f, z] + pushed
         return carry
 
@@ -367,6 +402,8 @@
             cs, rs = slab_rates(q, turned, damp2, decay, z, i)
             for f in range(NF):
                 out[f, z] = 0.5 * (out[f, z] + cs[f] + time_step * rs[f])
+        chunk = pl.ds(pl.multiple_of(g * INNER, INNER), INNER)
+        pltpu.make_async_copy(out.at[:, chunk], out_h.at[:, chunk], out_sems.at[g + 1]).start()
         return carry
 
     lax.fori_loop(0, cz // INNER, body, 0)
@@ -379,14 +416,13 @@
     count = cells.shape[1]
     step = 512
     n_comp = geom_v.shape[0]
-    forces = jnp.zeros((8, shapes.shape[2]), jnp.float32)
+    own = shapes.shape[2] // lax.axis_size("span")
+    sums = [jnp.zeros((8, 128), jnp.float32)] * own
     for at in range(0, count, step):
         where = cells[:, at : at + step]
         rows = lax.broadcasted_iota(jnp.int32, (cz * cy, step), 0)
         hit = jnp.where(rows == (where >> 7), 1.0, 0.0).astype(jnp.bfloat16)
-        picked = lax.dot_general(
-            parts, hit, (((1,), (0,)), ((), ())), preferred_element_type=jnp.float32
-        )
+        picked = bdot(parts, hit, ((1,), (0,)))
         picked = picked[:cx] + picked[cx:]
         lanes = lax.broadcasted_iota(jnp.int32, (cx, step), 0)
         sample = jnp.sum(jnp.where(lanes == (where & 127), picked, 0.0), axis=0, keepdims=True)
@@ -395,16 +431,27 @@
             + [jnp.zeros((8 - n_comp, step), jnp.float32)],
             axis=0,
         )
-        strip = lax.broadcasted_iota(jnp.int32, (shapes.shape[2], step), 0)
-        member = jnp.where(strip == strips_v[:, at : at + step], 1.0, 0.0)
-        forces = forces + mdot(traction, member, ((1,), (1,)))
-    total = jnp.zeros((1, shapes.shape[1]), jnp.float32)
+        strip = strips_v[:, at : at + step] - span_pos * own
+        for j in range(own):
+            mine = jnp.where(strip == j, traction, 0.0)
+            for k in range(0, step, 128):
+                sums[j] = sums[j] + mine[:, k : k + 128]
+    lane = lane_ids((8, shapes.shape[2]))
+    spread = jnp.zeros((8, shapes.shape[2]), jnp.float32)
+    for j in range(own):
+        force = jnp.sum(sums[j], axis=1, keepdims=True)
+        spread = jnp.where(lane == span_pos * own + j, force, spread)
+    total = jnp.zeros(shapes.shape[1:], jnp.float32)
     for c in range(n_comp):
-        total = total + mdot(forces[c : c + 1], shapes[c], ((1,), (1,)))
+        total = total + shapes[c] * spread[c : c + 1]
+    total = mdot(jnp.ones((8, shapes.shape[2]), jnp.float32), total, ((1,), (1,)))[0:1]
     total = jnp.concatenate(
         [total, jnp.zeros((1, 128 - shapes.shape[1]), jnp.float32)], axis=1
     )
     modal[...] = jnp.broadcast_to(total, modal.shape)
+    for g in range(cz // INNER):
+        chunk = pl.ds(g * INNER, INNER)
+        pltpu.make_async_copy(out.at[:, chunk], out_h.at[:, chunk], out_sems.at[g + 1]).wait()
 
 
 def f32(*shape):
@@ -484,11 +531,12 @@
         first_step,
         out_shape=(f32(NF, cz, cy, cx),) + leaving,
         in_specs=[VM] * 2 + [HB] * 7,
-        out_specs=(VM,) + (HB,) * 5,
+        out_specs=(HB,) * 6,
         scratch_shapes=[scratch]
         + buffers(arrived)
         + buffers(leaving)
-        + [pltpu.SemaphoreType.DMA((7,))],
+        + [pltpu.VMEM((NF, cz, cy, cx), jnp.float32)]
+        + [pltpu.SemaphoreType.DMA((7,)), pltpu.SemaphoreType.DMA((cz // INNER,))],
         compiler_params=room(52),
         name="first_step",
     )(fields, solid_frac, *arrived)
@@ -501,18 +549,19 @@
     new_fields, modal = pl.pallas_call(
         second_step,
         out_shape=(f32(NF, cz, cy, cx), f32(tiles, 128)),
-        in_specs=[VM] * 3 + [HB] * 10,
-        out_specs=(VM, VM),
+        in_specs=[VM] * 2 + [HB] * 11,
+        out_specs=(HB, VM),
         scratch_shapes=[scratch, pltpu.VMEM((cz * cy, 8), jnp.float32)]
         + buffers(arrived)
         + buffers((cells, f32(3, 1, deck), strip_ids[0, 0], shapes))
-        + [pltpu.SemaphoreType.DMA((10,))],
+        + [pltpu.VMEM((NF, cz, cy, cx), jnp.float32)]
+        + [pltpu.SemaphoreType.DMA((10,)), pltpu.SemaphoreType.DMA((cz // INNER + 1,))],
         compiler_params=room(52),
         name="second_step",
     )(
         fields,
+        solid_frac,
         base,
-        solid_frac,
         *arrived,
         cells,
         deck_geom.transpose(0, 1, 3, 2, 4),

time: 108 us -> 105 us (0.972)
  Pallas kernels: 20.2 us -> 17.9 us
where the time goes in v4:
time: 105 us
  starting transfers between devices  48.9 us (47%)
  blocking collectives  34.1 us (32%)
  Pallas kernels  17.9 us (17%)
  waiting for transfers between devices  2.18 us (2%)
    ppermute x10, starting transfers between devices, swapped(): return lax.ppermute(block, axis, pairs)  27.9 us
    all_to_all x1, blocking collectives, on_device(): part = lax.all_to_all(modal, ('span', 'vert'), 0, 0, tiled=True)  20.8 us
    all_to_all x1, starting transfers between devices, on_device(): lax.all_to_all(sent.reshape(tiles, ROWS, 128), ('span', 'vert'), 0, 0, ti...  15 us
    all_to_all x1, blocking collectives, on_device(): part = lax.all_to_all(part, 'stream', 0, 0, tiled=True)  13.2 us
    pallas_call x1, Pallas kernels, on_device(): pl.pallas_call(second_step, out_shape=(f32(NF, cz, cy, cx), f32(tiles, 12...  7.81 us
    pallas_call x1, Pallas kernels, on_device(): pl.pallas_call(first_step, out_shape=(f32(NF, cz, cy, cx),) + leaving, in...  6.45 us
    all_to_all x1, starting transfers between devices, on_device(): carried = lax.all_to_all(carry, 'stream', 0, 0, tiled=True)  6.02 us
    pallas_call x1, Pallas kernels, on_device(): pl.pallas_call(sum_panels, out_shape=f32(tiles * ROWS, 128), in_specs=[HB...  2.59 us
  transfers between devices with their start and end apart: 12, of which 2 were waited for; matrix products, arithmetic and copies ran while one was open for 0% of the time, Pallas kernels for 1%

profile of v4, /device:TPU:1, one launch (start us, length us, event | category | flops | bytes accessed | tf_op | source)
XLA Modules:
  0.0 104.6 jit_solution(4302506446572023864)
XLA Ops:
  0.6 0.0 copy-start
  0.6 2.6 %panel_sums.1 = f32[1024,128]{1,0:T(8,128)} custom-call(f32[5,64,256]{2,1,0:T(8,128)} %bitcast.18, s32[1,64]{1,0:T(1,128)} %bitcast.20, f32[64,256]{1,0:T(8,128)} %constant.8.clone.turn_h, bf16[768,128]{1,0:T(8,128)(2,1)} %constant.9.clone.edge_h), custom_call_target="tpu_custom_call" | custom-call | tf_op jit(solution)/shard_map/panel_sums/pallas_call | solution.py:496
  3.2 0.0 copy-start.1
  3.2 15.0 %all-to-all-start = ((f32[64,16,128]{2,1,0:T(8,128)}), f32[64,16,128]{2,1,0:T(8,128)S(1)}, u32[]{:S(2)}, u32[]{:S(2)}) async-start(f32[64,16,128]{2,1,0:T(8,128)} %bitcast.17), calls=%async_computation | async-start | bytes 1048576 | tf_op jit(solution)/shard_map/all_to_all | solution.py:505
  18.2 1.0 pack_faces.1
  19.3 2.4 %collective-permute-start.2 = (f32[5,32,128]{2,1,0:T(8,128)S(1)}, f32[5,32,128]{2,1,0:T(8,128)S(1)}, u32[]{:S(2)}, u32[]{:S(2)}) collective-permute-start(f32[5,32,128]{2,1,0:T(8,128)S(1)} %get-tuple-element.16), channel_id=1, source_target_pairs={{0,4},{4,0},{8,12},{12,8},{16,20},{20,16},{24,28},{28,24},{32,36},... | collective-permute-start | bytes 245768 | tf_op jit(solution)/shard_map/ppermute | solution.py:477
  21.6 3.2 %collective-permute-start.3 = (f32[5,32,128]{2,1,0:T(8,128)S(1)}, f32[5,32,128]{2,1,0:T(8,128)S(1)}, u32[]{:S(2)}, u32[]{:S(2)}) collective-permute-start(f32[5,32,128]{2,1,0:T(8,128)S(1)} %get-tuple-element.17), channel_id=1, source_target_pairs={{4,8},{8,4},{12,16},{16,12},{20,24},{24,20},{28,32},{32,28},{36,40... | collective-permute-start | bytes 245768 | tf_op jit(solution)/shard_map/ppermute | solution.py:477
  24.9 0.7 collective-permute-start.1
  25.6 3.1 %collective-permute-start.4 = (f32[5,16,128]{2,1,0:T(8,128)S(1)}, f32[5,16,128]{2,1,0:T(8,128)S(1)}, u32[]{:S(2)}, u32[]{:S(2)}) collective-permute-start(f32[5,16,128]{2,1,0:T(8,128)S(1)} %get-tuple-element.18), channel_id=1, source_target_pairs={{0,1},{1,0},{2,3},{3,2},{4,5},{5,4},{6,7},{7,6},{8,9},{9,8},{10,11... | collective-permute-start | bytes 122888 | tf_op jit(solution)/shard_map/ppermute | solution.py:477
  28.7 0.7 collective-permute-start.5
  29.3 0.0 collective-permute-done.1.refs_4_
  29.3 5.7 %collective-permute-start = (f32[5,8,128]{2,1,0:T(8,128)S(1)}, f32[5,8,128]{2,1,0:T(8,128)S(1)}, u32[]{:S(2)}, u32[]{:S(2)}) collective-permute-start(f32[5,8,128]{2,1,0:T(8,128)S(1)} %get-tuple-element.15), channel_id=1, source_target_pairs={{0,64},{64,0},{128,192},{192,128},{256,320},{320,256},{384,448},{4... | collective-permute-start | bytes 61448 | tf_op jit(solution)/shard_map/ppermute | solution.py:477
  35.1 1.5 %collective-permute-done.refs_3_ = f32[5,8,128]{2,1,0:T(8,128)S(1)} collective-permute-done((f32[5,8,128]{2,1,0:T(8,128)S(1)}, f32[5,8,128]{2,1,0:T(8,128)S(1)}, u32[]{:S(2)}, u32[]{:S(2)}) %collective-permute-start) | collective-permute-done | bytes 20512 | tf_op jit(solution)/shard_map/ppermute | solution.py:477
  36.6 0.0 collective-permute-done.5.refs_8_
  36.6 0.0 collective-permute-done.2.refs_5_
  36.6 0.0 collective-permute-done.3.refs_6_
  36.6 0.0 copy-start.2
  36.6 0.0 copy-start.3
  36.6 0.0 copy-start.4
  36.6 0.0 copy-start.5
  36.6 6.5 %first_step.1 = (f32[5,32,16,128]{3,2,1,0:T(8,128)}, f32[8,56,128]{2,1,0:T(8,128)}, f32[5,32,128]{2,1,0:T(8,128)S(1)}, f32[5,32,128]{2,1,0:T(8,128)S(1)}, f32[5,...) custom-call(f32[5,32,16,128]{3,2,1,0:T(8,128)} %refs_0_.3, f32[32,16,128]{2,1,0:T(8,128)S(1)} %copy-done.1, ...), custom_call_target="tpu_custom_call" | custom-call | tf_op jit(solution)/shard_map/first_step/pallas_call | solution.py:530
  43.1 6.0 %all-to-all-start.1 = ((f32[8,56,128]{2,1,0:T(8,128)}), f32[8,56,128]{2,1,0:T(8,128)S(1)}, u32[]{:S(2)}, u32[]{:S(2)}) async-start(f32[8,56,128]{2,1,0:T(8,128)} %get-tuple-element.21), calls=%async_computation.1 | async-start | bytes 458752 | tf_op jit(solution)/shard_map/all_to_all | solution.py:543
  49.1 3.7 %collective-permute-start.6 = (f32[5,32,128]{2,1,0:T(8,128)S(1)}, f32[5,32,128]{2,1,0:T(8,128)S(1)}, u32[]{:S(2)}, u32[]{:S(2)}) collective-permute-start(f32[5,32,128]{2,1,0:T(8,128)S(1)} %get-tuple-element.22), channel_id=1, source_target_pairs={{0,4},{4,0},{8,12},{12,8},{16,20},{20,16},{24,28},{28,24},{32,36},... | collective-permute-start | bytes 245768 | tf_op jit(solution)/shard_map/ppermute | solution.py:477
  52.8 2.5 %collective-permute-start.7 = (f32[5,32,128]{2,1,0:T(8,128)S(1)}, f32[5,32,128]{2,1,0:T(8,128)S(1)}, u32[]{:S(2)}, u32[]{:S(2)}) collective-permute-start(f32[5,32,128]{2,1,0:T(8,128)S(1)} %get-tuple-element.23), channel_id=1, source_target_pairs={{4,8},{8,4},{12,16},{16,12},{20,24},{24,20},{28,32},{32,28},{36,40... | collective-permute-start | bytes 245768 | tf_op jit(solution)/shard_map/ppermute | solution.py:477
  55.4 5.3 %collective-permute-start.8 = (f32[5,16,128]{2,1,0:T(8,128)S(1)}, f32[5,16,128]{2,1,0:T(8,128)S(1)}, u32[]{:S(2)}, u32[]{:S(2)}) collective-permute-start(f32[5,16,128]{2,1,0:T(8,128)S(1)} %get-tuple-element.24), channel_id=1, source_target_pairs={{0,1},{1,0},{2,3},{3,2},{4,5},{5,4},{6,7},{7,6},{8,9},{9,8},{10,11... | collective-permute-start | bytes 122888 | tf_op jit(solution)/shard_map/ppermute | solution.py:477
  60.6 0.7 collective-permute-start.9
  61.3 0.7 collective-permute-done.8.refs_7_
  62.1 7.8 %second_step.1 = (f32[5,32,16,128]{3,2,1,0:T(8,128)}, f32[64,128]{1,0:T(8,128)S(1)}) custom-call(f32[5,32,16,128]{3,2,1,0:T(8,128)} %refs_0_.3, f32[32,16,128]{2,1,0:T(8,128)S(1)} %copy-done.1, f32[5,32,16,128]{3,2,1,0:T(8,128)} %get-tuple-element.20.refs_2_, f32[8,56,128]{2,1,0:T(8,128)S(1)} %all-to-all-done.1.refs_3_, ...), custom_call_target="tpu_custom_call" | custom-call | tf_op jit(solution)/shard_map/second_step/pallas_call | solution.py:549
  69.9 20.8 %all_to_all.25 = f32[64,1,128]{2,1,0:T(1,128)S(1)} all-to-all(f32[64,1,128]{2,1,0:T(1,128)S(1)} %bitcast.15), channel_id=1, replica_groups=mesh['stream'=8,'span'=16,'vert'=4] {'span','vert'}, dimensions={0} | all-to-all | bytes 65536 | tf_op jit(solution)/shard_map/all_to_all | solution.py:571
  90.7 0.1 reduce_sum.18
  90.8 13.2 %all_to_all.26 = f32[8,1,128]{2,1,0:T(1,128)S(1)} all-to-all(f32[8,1,128]{2,1,0:T(1,128)S(1)} %broadcast_in_dim.2), channel_id=1, replica_groups=mesh['stream'=8,'span'=16,'vert'=4] {'stream'}, dimensions={0} | all-to-all | bytes 8192 | tf_op jit(solution)/shard_map/all_to_all | solution.py:573
  104.1 0.5 reduce_sum.19
  (13 shorter events, 0.0 us)
Async XLA Ops:
  0.6 17.6 %copy-start = (f32[5,32,16,128]{3,2,1,0:T(8,128)S(1)}, f32[5,32,16,128]{3,2,1,0:T(8,128)}, u32[]{:S(2)}) copy-start(f32[5,32,16,128]{3,2,1,0:T(8,128)} %refs_0_.3) | copy-start | bytes 3932164
  3.2 33.3 %copy-start.1 = (f32[32,16,128]{2,1,0:T(8,128)S(1)}, f32[32,16,128]{2,1,0:T(8,128)}, u32[]{:S(2)}) copy-start(f32[32,16,128]{2,1,0:T(8,128)} %refs_1_.3) | copy-start | bytes 786436
  3.2 33.3 %all-to-all-start = ((f32[64,16,128]{2,1,0:T(8,128)}), f32[64,16,128]{2,1,0:T(8,128)S(1)}, u32[]{:S(2)}, u32[]{:S(2)}) async-start(f32[64,16,128]{2,1,0:T(8,128)} %bitcast.17), calls=%async_computation | async-start | bytes 1048576 | tf_op jit(solution)/shard_map/all_to_all | solution.py:505
  19.3 17.3 %collective-permute-start.2 = (f32[5,32,128]{2,1,0:T(8,128)S(1)}, f32[5,32,128]{2,1,0:T(8,128)S(1)}, u32[]{:S(2)}, u32[]{:S(2)}) collective-permute-start(f32[5,32,128]{2,1,0:T(8,128)S(1)} %get-tuple-element.16), channel_id=1, source_target_pairs={{0,4},{4,0},{8,12},{12,8},{16,20},{20,16},{24,28},{28,24},{32,36},... | collective-permute-start | bytes 245768 | tf_op jit(solution)/shard_map/ppermute | solution.py:477
  21.6 14.9 %collective-permute-start.3 = (f32[5,32,128]{2,1,0:T(8,128)S(1)}, f32[5,32,128]{2,1,0:T(8,128)S(1)}, u32[]{:S(2)}, u32[]{:S(2)}) collective-permute-start(f32[5,32,128]{2,1,0:T(8,128)S(1)} %get-tuple-element.17), channel_id=1, source_target_pairs={{4,8},{8,4},{12,16},{16,12},{20,24},{24,20},{28,32},{32,28},{36,40... | collective-permute-start | bytes 245768 | tf_op jit(solution)/shard_map/ppermute | solution.py:477
  24.9 4.4 %collective-permute-start.1 = (f32[5,8,128]{2,1,0:T(8,128)S(1)}, f32[5,8,128]{2,1,0:T(8,128)S(1)}, u32[]{:S(2)}, u32[]{:S(2)}) collective-permute-start(f32[5,8,128]{2,1,0:T(8,128)S(1)} %get-tuple-element.15), channel_id=1, source_target_pairs={{64,128},{128,64},{192,256},{256,192},{320,384},{384,320},{65,129}... | collective-permute-start | bytes 61448 | tf_op jit(solution)/shard_map/ppermute | solution.py:477
  25.6 11.0 %collective-permute-start.4 = (f32[5,16,128]{2,1,0:T(8,128)S(1)}, f32[5,16,128]{2,1,0:T(8,128)S(1)}, u32[]{:S(2)}, u32[]{:S(2)}) collective-permute-start(f32[5,16,128]{2,1,0:T(8,128)S(1)} %get-tuple-element.18), channel_id=1, source_target_pairs={{0,1},{1,0},{2,3},{3,2},{4,5},{5,4},{6,7},{7,6},{8,9},{9,8},{10,11... | collective-permute-start | bytes 122888 | tf_op jit(solution)/shard_map/ppermute | solution.py:477
  28.7 7.9 %collective-permute-start.5 = (f32[5,16,128]{2,1,0:T(8,128)S(1)}, f32[5,16,128]{2,1,0:T(8,128)S(1)}, u32[]{:S(2)}, u32[]{:S(2)}) collective-permute-start(f32[5,16,128]{2,1,0:T(8,128)S(1)} %get-tuple-element.19), channel_id=1, source_target_pairs={{1,2},{2,1},{5,6},{6,5},{9,10},{10,9},{13,14},{14,13},{17,18},{18,... | collective-permute-start | bytes 122888 | tf_op jit(solution)/shard_map/ppermute | solution.py:477
  29.3 7.2 %collective-permute-start = (f32[5,8,128]{2,1,0:T(8,128)S(1)}, f32[5,8,128]{2,1,0:T(8,128)S(1)}, u32[]{:S(2)}, u32[]{:S(2)}) collective-permute-start(f32[5,8,128]{2,1,0:T(8,128)S(1)} %get-tuple-element.15), channel_id=1, source_target_pairs={{0,64},{64,0},{128,192},{192,128},{256,320},{320,256},{384,448},{4... | collective-permute-start | bytes 61448 | tf_op jit(solution)/shard_map/ppermute | solution.py:477
  36.6 25.5 %copy-start.2 = (f32[1,16,1,3,2048]{4,2,3,1,0:T(1,128)S(1)}, f32[1,16,1,3,2048]{4,2,3,1,0:T(1,128)}, u32[]{:S(2)}) copy-start(f32[1,16,1,3,2048]{4,2,3,1,0:T(1,128)} %param.16) | copy-start | bytes 1179652
  36.6 25.5 %copy-start.3 = (s32[1,16,1,2048]{3,2,1,0:T(1,128)S(1)}, s32[1,16,1,2048]{3,2,1,0:T(1,128)}, u32[]{:S(2)}) copy-start(s32[1,16,1,2048]{3,2,1,0:T(1,128)} %refs_11_.1) | copy-start | bytes 393220
  36.6 25.5 %copy-start.4 = (f32[3,64,32]{1,2,0:T(8,128)S(1)}, f32[3,64,32]{1,2,0:T(8,128)}, u32[]{:S(2)}) copy-start(f32[3,64,32]{1,2,0:T(8,128)} %param.18) | copy-start | bytes 73732
  36.6 25.5 %copy-start.5 = (s32[1,1,1,2048]{3,2,1,0:T(1,128)S(1)}, s32[1,1,1,2048]{3,2,1,0:T(1,128)}, u32[]{:S(2)}) copy-start(s32[1,1,1,2048]{3,2,1,0:T(1,128)} %param.15) | copy-start | bytes 24580
  43.1 18.9 %all-to-all-start.1 = ((f32[8,56,128]{2,1,0:T(8,128)}), f32[8,56,128]{2,1,0:T(8,128)S(1)}, u32[]{:S(2)}, u32[]{:S(2)}) async-start(f32[8,56,128]{2,1,0:T(8,128)} %get-tuple-element.21), calls=%async_computation.1 | async-start | bytes 458752 | tf_op jit(solution)/shard_map/all_to_all | solution.py:543
  49.1 12.9 %collective-permute-start.6 = (f32[5,32,128]{2,1,0:T(8,128)S(1)}, f32[5,32,128]{2,1,0:T(8,128)S(1)}, u32[]{:S(2)}, u32[]{:S(2)}) collective-permute-start(f32[5,32,128]{2,1,0:T(8,128)S(1)} %get-tuple-element.22), channel_id=1, source_target_pairs={{0,4},{4,0},{8,12},{12,8},{16,20},{20,16},{24,28},{28,24},{32,36},... | collective-permute-start | bytes 245768 | tf_op jit(solution)/shard_map/ppermute | solution.py:477
  52.8 9.2 %collective-permute-start.7 = (f32[5,32,128]{2,1,0:T(8,128)S(1)}, f32[5,32,128]{2,1,0:T(8,128)S(1)}, u32[]{:S(2)}, u32[]{:S(2)}) collective-permute-start(f32[5,32,128]{2,1,0:T(8,128)S(1)} %get-tuple-element.23), channel_id=1, source_target_pairs={{4,8},{8,4},{12,16},{16,12},{20,24},{24,20},{28,32},{32,28},{36,40... | collective-permute-start | bytes 245768 | tf_op jit(solution)/shard_map/ppermute | solution.py:477
  55.4 6.6 %collective-permute-start.8 = (f32[5,16,128]{2,1,0:T(8,128)S(1)}, f32[5,16,128]{2,1,0:T(8,128)S(1)}, u32[]{:S(2)}, u32[]{:S(2)}) collective-permute-start(f32[5,16,128]{2,1,0:T(8,128)S(1)} %get-tuple-element.24), channel_id=1, source_target_pairs={{0,1},{1,0},{2,3},{3,2},{4,5},{5,4},{6,7},{7,6},{8,9},{9,8},{10,11... | collective-permute-start | bytes 122888 | tf_op jit(solution)/shard_map/ppermute | solution.py:477
  60.6 1.4 %collective-permute-start.9 = (f32[5,16,128]{2,1,0:T(8,128)S(1)}, f32[5,16,128]{2,1,0:T(8,128)S(1)}, u32[]{:S(2)}, u32[]{:S(2)}) collective-permute-start(f32[5,16,128]{2,1,0:T(8,128)S(1)} %get-tuple-element.25), channel_id=1, source_target_pairs={{1,2},{2,1},{5,6},{6,5},{9,10},{10,9},{13,14},{14,13},{17,18},{18,... | collective-permute-start | bytes 122888 | tf_op jit(solution)/shard_map/ppermute | solution.py:477

commit v5 on v4

--- a/solution.py
+++ b/solution.py
@@ -258,12 +258,10 @@
 
 def first_step(*refs):
     fields, solid = refs[:2]
-    arrived, base_out, sent = refs[2:9], refs[9], refs[10:15]
-    q, kept, leaving, base, sems, base_sems = refs[15], refs[16:23], refs[23:28], *refs[28:31]
-    got, xe, xo, ye, yo, ze, zo = kept
-    carry_out, ye1, yo1, ze1, zo1 = leaving
+    got, xe, xo, ye, yo, ze, zo = refs[2:9]
+    base_out, carry_out, ye1, yo1, ze1, zo1 = refs[9:15]
+    q, base, base_sems = refs[15:18]
     cz = fields.shape[1]
-    coming = fetch(arrived, kept, sems)
 
     def fill(z, carry):
         for f in range(NF):
@@ -271,7 +269,6 @@
         return carry
 
     lax.fori_loop(0, cz, fill, 0, unroll=4)
-    wait_all(coming[1:])
     fill_ghosts(q, ye, yo, ze, zo)
     x_low = face_choice("stream")
     xg = ghosts_x(
@@ -299,8 +296,6 @@
 
     accs = lax.fori_loop(0, cz // INNER, body, (zero,) * NF)
     store_faces(base, ye1, yo1, ze1, zo1)
-    going = fetch(leaving[1:], sent[1:], sems, 1)
-    coming[0].wait()
     total = got[0:ROWS]
     for i in range(1, got.shape[0] // ROWS):
         total = total + got[ROWS * i : ROWS * i + ROWS]
@@ -308,7 +303,6 @@
         carry_out[i, 0:ROWS] = total
         for f in range(NF):
             carry_out[i, ROWS + 8 * f : ROWS + 8 * f + 8] = accs[f]
-    wait_all(going + fetch(leaving[:1], sent[:1], sems))
     for g in range(cz // INNER):
         chunk = pl.ds(g * INNER, INNER)
         pltpu.make_async_copy(base.at[:, chunk], base_out.at[:, chunk], base_sems.at[g]).wait()
@@ -316,17 +310,17 @@
 
 def second_step(*refs):
     fields, solid, base = refs[:3]
-    arrived, late = refs[3:9], refs[9:13]
+    plane_h, late = refs[3], refs[9:13]
+    carried, ye, yo, ze, zo = refs[4:9]
     out_h, modal, q, target = refs[13:17]
-    kept, late_kept, out, sems, out_sems = refs[17:23], refs[23:27], *refs[27:30]
-    carried, plane_table, ye, yo, ze, zo = kept
+    plane_table, late_kept, out, sems, out_sems = refs[17], refs[18:22], *refs[22:25]
     cells, geom_v, strips_v, shapes = late_kept
     cz, cy, cx = fields.shape[1:]
     n_stream = carried.shape[0]
     span_pos = lax.axis_index("span")
     vert_pos = lax.axis_index("vert")
     stream_pos = lax.axis_index("stream")
-    coming = fetch(arrived, kept, sems)
+    coming = fetch((plane_h,), (plane_table,), sems)
     get_base = pltpu.make_async_copy(base, q.at[:, 1 : cz + 1, 8:24, :], out_sems.at[0])
     get_base.start()
     cells_h, geom_h, strips_h, shapes_h = late
@@ -337,7 +331,7 @@
         len(coming),
     )
 
-    wait_all(coming[:2])
+    wait_all(coming)
     low, high = carried[0, 0:8], carried[0, 8:16]
     for i in range(1, n_stream):
         low = low + carried[i, 0:8]
@@ -370,7 +364,6 @@
             jnp.where(vert_pos < lax.axis_size("vert") - 1, col[2 * cz + cy :], 0.0),
         )
 
-    wait_all(coming[2:])
     fill_ghosts(q, ye, yo, ze, zo, edge_push)
     get_base.wait()
 
@@ -530,39 +523,40 @@
     base, carry, *faces = pl.pallas_call(
         first_step,
         out_shape=(f32(NF, cz, cy, cx),) + leaving,
-        in_specs=[VM] * 2 + [HB] * 7,
-        out_specs=(HB,) * 6,
-        scratch_shapes=[scratch]
-        + buffers(arrived)
-        + buffers(leaving)
-        + [pltpu.VMEM((NF, cz, cy, cx), jnp.float32)]
-        + [pltpu.SemaphoreType.DMA((7,)), pltpu.SemaphoreType.DMA((cz // INNER,))],
+        in_specs=[VM] * 9,
+        out_specs=(HB,) + (VM,) * 5,
+        scratch_shapes=[
+            scratch,
+            pltpu.VMEM((NF, cz, cy, cx), jnp.float32),
+            pltpu.SemaphoreType.DMA((cz // INNER,)),
+        ],
         compiler_params=room(52),
         name="first_step",
     )(fields, solid_frac, *arrived)
     carried = lax.all_to_all(carry, "stream", 0, 0, tiled=True)
     ghosts = swap_yz(*faces)
     deck = deck_cells.shape[3]
-    arrived = (carried, jnp.asarray(plane)) + ghosts
+    plane = jnp.asarray(plane)
     cells = deck_cells.reshape(1, deck)
     shapes = mode_shapes.transpose(0, 2, 1)
     new_fields, modal = pl.pallas_call(
         second_step,
         out_shape=(f32(NF, cz, cy, cx), f32(tiles, 128)),
-        in_specs=[VM] * 2 + [HB] * 11,
+        in_specs=[VM] * 2 + [HB] * 2 + [VM] * 5 + [HB] * 4,
         out_specs=(HB, VM),
         scratch_shapes=[scratch, pltpu.VMEM((cz * cy, 8), jnp.float32)]
-        + buffers(arrived)
-        + buffers((cells, f32(3, 1, deck), strip_ids[0, 0], shapes))
+        + buffers((plane, cells, f32(3, 1, deck), strip_ids[0, 0], shapes))
         + [pltpu.VMEM((NF, cz, cy, cx), jnp.float32)]
-        + [pltpu.SemaphoreType.DMA((10,)), pltpu.SemaphoreType.DMA((cz // INNER + 1,))],
+        + [pltpu.SemaphoreType.DMA((5,)), pltpu.SemaphoreType.DMA((cz // INNER + 1,))],
         compiler_params=room(52),
         name="second_step",
     )(
         fields,
         solid_frac,
         base,
-        *arrived,
+        plane,
+        carried,
+        *ghosts,
         cells,
         deck_geom.transpose(0, 1, 3, 2, 4),
         strip_ids,

time: 105 us -> 104 us (level)
  no operation moved by 1% of the time
where the time goes in v5:
time: 104 us
  starting transfers between devices  48.9 us (47%)
  blocking collectives  34.1 us (33%)
  Pallas kernels  17 us (16%)
  waiting for transfers between devices  2.18 us (2%)
    ppermute x10, starting transfers between devices, swapped(): return lax.ppermute(block, axis, pairs)  27.9 us
    all_to_all x1, blocking collectives, on_device(): part = lax.all_to_all(modal, ('span', 'vert'), 0, 0, tiled=True)  20.8 us
    all_to_all x1, starting transfers between devices, on_device(): lax.all_to_all(sent.reshape(tiles, ROWS, 128), ('span', 'vert'), 0, 0, ti...  15 us
    all_to_all x1, blocking collectives, on_device(): part = lax.all_to_all(part, 'stream', 0, 0, tiled=True)  13.2 us
    pallas_call x1, Pallas kernels, on_device(): pl.pallas_call(second_step, out_shape=(f32(NF, cz, cy, cx), f32(tiles, 12...  7.34 us
    pallas_call x1, Pallas kernels, on_device(): pl.pallas_call(first_step, out_shape=(f32(NF, cz, cy, cx),) + leaving, in...  6.04 us
    all_to_all x1, starting transfers between devices, on_device(): carried = lax.all_to_all(carry, 'stream', 0, 0, tiled=True)  6.02 us
    pallas_call x1, Pallas kernels, on_device(): pl.pallas_call(sum_panels, out_shape=f32(tiles * ROWS, 128), in_specs=[HB...  2.59 us
  transfers between devices with their start and end apart: 12, of which 2 were waited for; matrix products, arithmetic and copies ran while one was open for 0% of the time, Pallas kernels for 1%

profile of v5, /device:TPU:1, one launch (start us, length us, event | category | flops | bytes accessed | tf_op | source)
XLA Modules:
  0.0 103.7 jit_solution(14406963975901715889)
XLA Ops:
  0.6 0.0 copy-start
  0.6 2.6 %panel_sums.1 = f32[1024,128]{1,0:T(8,128)} custom-call(f32[5,64,256]{2,1,0:T(8,128)} %bitcast.18, s32[1,64]{1,0:T(1,128)} %bitcast.20, f32[64,256]{1,0:T(8,128)} %constant.8.clone.turn_h, bf16[768,128]{1,0:T(8,128)(2,1)} %constant.9.clone.edge_h), custom_call_target="tpu_custom_call" | custom-call | tf_op jit(solution)/shard_map/panel_sums/pallas_call | solution.py:489
  3.2 0.0 copy-start.1
  3.2 15.0 %all-to-all-start = ((f32[64,16,128]{2,1,0:T(8,128)}), f32[64,16,128]{2,1,0:T(8,128)S(1)}, u32[]{:S(2)}, u32[]{:S(2)}) async-start(f32[64,16,128]{2,1,0:T(8,128)} %bitcast.17), calls=%async_computation | async-start | bytes 1048576 | tf_op jit(solution)/shard_map/all_to_all | solution.py:498
  18.2 1.0 pack_faces.1
  19.3 2.4 %collective-permute-start.2 = (f32[5,32,128]{2,1,0:T(8,128)S(1)}, f32[5,32,128]{2,1,0:T(8,128)S(1)}, u32[]{:S(2)}, u32[]{:S(2)}) collective-permute-start(f32[5,32,128]{2,1,0:T(8,128)S(1)} %get-tuple-element.16), channel_id=1, source_target_pairs={{0,4},{4,0},{8,12},{12,8},{16,20},{20,16},{24,28},{28,24},{32,36},... | collective-permute-start | bytes 245768 | tf_op jit(solution)/shard_map/ppermute | solution.py:470
  21.6 3.2 %collective-permute-start.3 = (f32[5,32,128]{2,1,0:T(8,128)S(1)}, f32[5,32,128]{2,1,0:T(8,128)S(1)}, u32[]{:S(2)}, u32[]{:S(2)}) collective-permute-start(f32[5,32,128]{2,1,0:T(8,128)S(1)} %get-tuple-element.17), channel_id=1, source_target_pairs={{4,8},{8,4},{12,16},{16,12},{20,24},{24,20},{28,32},{32,28},{36,40... | collective-permute-start | bytes 245768 | tf_op jit(solution)/shard_map/ppermute | solution.py:470
  24.9 0.7 collective-permute-start.1
  25.6 3.1 %collective-permute-start.4 = (f32[5,16,128]{2,1,0:T(8,128)S(1)}, f32[5,16,128]{2,1,0:T(8,128)S(1)}, u32[]{:S(2)}, u32[]{:S(2)}) collective-permute-start(f32[5,16,128]{2,1,0:T(8,128)S(1)} %get-tuple-element.18), channel_id=1, source_target_pairs={{0,1},{1,0},{2,3},{3,2},{4,5},{5,4},{6,7},{7,6},{8,9},{9,8},{10,11... | collective-permute-start | bytes 122888 | tf_op jit(solution)/shard_map/ppermute | solution.py:470
  28.7 0.7 collective-permute-start.5
  29.3 0.0 collective-permute-done.1.refs_4_
  29.3 5.7 %collective-permute-start = (f32[5,8,128]{2,1,0:T(8,128)S(1)}, f32[5,8,128]{2,1,0:T(8,128)S(1)}, u32[]{:S(2)}, u32[]{:S(2)}) collective-permute-start(f32[5,8,128]{2,1,0:T(8,128)S(1)} %get-tuple-element.15), channel_id=1, source_target_pairs={{0,64},{64,0},{128,192},{192,128},{256,320},{320,256},{384,448},{4... | collective-permute-start | bytes 61448 | tf_op jit(solution)/shard_map/ppermute | solution.py:470
  35.1 1.5 %collective-permute-done.refs_3_ = f32[5,8,128]{2,1,0:T(8,128)S(1)} collective-permute-done((f32[5,8,128]{2,1,0:T(8,128)S(1)}, f32[5,8,128]{2,1,0:T(8,128)S(1)}, u32[]{:S(2)}, u32[]{:S(2)}) %collective-permute-start) | collective-permute-done | bytes 20512 | tf_op jit(solution)/shard_map/ppermute | solution.py:470
  36.6 0.0 collective-permute-done.5.refs_8_
  36.6 0.0 collective-permute-done.2.refs_5_
  36.6 0.0 collective-permute-done.3.refs_6_
  36.6 0.0 copy-start.2
  36.6 0.0 copy-start.3
  36.6 0.0 copy-start.4
  36.6 0.0 copy-start.5
  36.6 6.0 %first_step.1 = (f32[5,32,16,128]{3,2,1,0:T(8,128)}, f32[8,56,128]{2,1,0:T(8,128)}, f32[5,32,128]{2,1,0:T(8,128)S(1)}, f32[5,32,128]{2,1,0:T(8,128)S(1)}, f32[5,...) custom-call(f32[5,32,16,128]{3,2,1,0:T(8,128)} %refs_0_.3, f32[32,16,128]{2,1,0:T(8,128)S(1)} %copy-done.1, ...), custom_call_target="tpu_custom_call" | custom-call | tf_op jit(solution)/shard_map/first_step/pallas_call | solution.py:523
  42.7 6.0 %all-to-all-start.1 = ((f32[8,56,128]{2,1,0:T(8,128)}), f32[8,56,128]{2,1,0:T(8,128)S(1)}, u32[]{:S(2)}, u32[]{:S(2)}) async-start(f32[8,56,128]{2,1,0:T(8,128)} %get-tuple-element.21), calls=%async_computation.1 | async-start | bytes 458752 | tf_op jit(solution)/shard_map/all_to_all | solution.py:536
  48.7 3.7 %collective-permute-start.6 = (f32[5,32,128]{2,1,0:T(8,128)S(1)}, f32[5,32,128]{2,1,0:T(8,128)S(1)}, u32[]{:S(2)}, u32[]{:S(2)}) collective-permute-start(f32[5,32,128]{2,1,0:T(8,128)S(1)} %get-tuple-element.22), channel_id=1, source_target_pairs={{0,4},{4,0},{8,12},{12,8},{16,20},{20,16},{24,28},{28,24},{32,36},... | collective-permute-start | bytes 245768 | tf_op jit(solution)/shard_map/ppermute | solution.py:470
  52.4 2.5 %collective-permute-start.7 = (f32[5,32,128]{2,1,0:T(8,128)S(1)}, f32[5,32,128]{2,1,0:T(8,128)S(1)}, u32[]{:S(2)}, u32[]{:S(2)}) collective-permute-start(f32[5,32,128]{2,1,0:T(8,128)S(1)} %get-tuple-element.23), channel_id=1, source_target_pairs={{4,8},{8,4},{12,16},{16,12},{20,24},{24,20},{28,32},{32,28},{36,40... | collective-permute-start | bytes 245768 | tf_op jit(solution)/shard_map/ppermute | solution.py:470
  55.0 5.3 %collective-permute-start.8 = (f32[5,16,128]{2,1,0:T(8,128)S(1)}, f32[5,16,128]{2,1,0:T(8,128)S(1)}, u32[]{:S(2)}, u32[]{:S(2)}) collective-permute-start(f32[5,16,128]{2,1,0:T(8,128)S(1)} %get-tuple-element.24), channel_id=1, source_target_pairs={{0,1},{1,0},{2,3},{3,2},{4,5},{5,4},{6,7},{7,6},{8,9},{9,8},{10,11... | collective-permute-start | bytes 122888 | tf_op jit(solution)/shard_map/ppermute | solution.py:470
  60.2 0.7 collective-permute-start.9
  60.9 0.7 collective-permute-done.8.refs_7_
  61.7 7.3 %second_step.1 = (f32[5,32,16,128]{3,2,1,0:T(8,128)}, f32[64,128]{1,0:T(8,128)S(1)}) custom-call(f32[5,32,16,128]{3,2,1,0:T(8,128)} %refs_0_.3, f32[32,16,128]{2,1,0:T(8,128)S(1)} %copy-done.1, f32[5,32,16,128]{3,2,1,0:T(8,128)} %get-tuple-element.20.refs_2_, bf16[512,768]{1,0:T(8,128)(2,1)} %constant.10.clone.refs_3_, ...), custom_call_target="tpu_custom_call" | custom-call | tf_op jit(solution)/shard_map/second_step/pallas_call | solution.py:542
  69.0 20.8 %all_to_all.25 = f32[64,1,128]{2,1,0:T(1,128)S(1)} all-to-all(f32[64,1,128]{2,1,0:T(1,128)S(1)} %bitcast.15), channel_id=1, replica_groups=mesh['stream'=8,'span'=16,'vert'=4] {'span','vert'}, dimensions={0} | all-to-all | bytes 65536 | tf_op jit(solution)/shard_map/all_to_all | solution.py:565
  89.9 0.1 reduce_sum.18
  89.9 13.2 %all_to_all.26 = f32[8,1,128]{2,1,0:T(1,128)S(1)} all-to-all(f32[8,1,128]{2,1,0:T(1,128)S(1)} %broadcast_in_dim.2), channel_id=1, replica_groups=mesh['stream'=8,'span'=16,'vert'=4] {'stream'}, dimensions={0} | all-to-all | bytes 8192 | tf_op jit(solution)/shard_map/all_to_all | solution.py:567
  103.2 0.5 reduce_sum.19
  (13 shorter events, 0.0 us)
Async XLA Ops:
  0.6 17.6 %copy-start = (f32[5,32,16,128]{3,2,1,0:T(8,128)S(1)}, f32[5,32,16,128]{3,2,1,0:T(8,128)}, u32[]{:S(2)}) copy-start(f32[5,32,16,128]{3,2,1,0:T(8,128)} %refs_0_.3) | copy-start | bytes 3932164
  3.2 33.3 %copy-start.1 = (f32[32,16,128]{2,1,0:T(8,128)S(1)}, f32[32,16,128]{2,1,0:T(8,128)}, u32[]{:S(2)}) copy-start(f32[32,16,128]{2,1,0:T(8,128)} %refs_1_.3) | copy-start | bytes 786436
  3.2 33.3 %all-to-all-start = ((f32[64,16,128]{2,1,0:T(8,128)}), f32[64,16,128]{2,1,0:T(8,128)S(1)}, u32[]{:S(2)}, u32[]{:S(2)}) async-start(f32[64,16,128]{2,1,0:T(8,128)} %bitcast.17), calls=%async_computation | async-start | bytes 1048576 | tf_op jit(solution)/shard_map/all_to_all | solution.py:498
  19.3 17.3 %collective-permute-start.2 = (f32[5,32,128]{2,1,0:T(8,128)S(1)}, f32[5,32,128]{2,1,0:T(8,128)S(1)}, u32[]{:S(2)}, u32[]{:S(2)}) collective-permute-start(f32[5,32,128]{2,1,0:T(8,128)S(1)} %get-tuple-element.16), channel_id=1, source_target_pairs={{0,4},{4,0},{8,12},{12,8},{16,20},{20,16},{24,28},{28,24},{32,36},... | collective-permute-start | bytes 245768 | tf_op jit(solution)/shard_map/ppermute | solution.py:470
  21.6 14.9 %collective-permute-start.3 = (f32[5,32,128]{2,1,0:T(8,128)S(1)}, f32[5,32,128]{2,1,0:T(8,128)S(1)}, u32[]{:S(2)}, u32[]{:S(2)}) collective-permute-start(f32[5,32,128]{2,1,0:T(8,128)S(1)} %get-tuple-element.17), channel_id=1, source_target_pairs={{4,8},{8,4},{12,16},{16,12},{20,24},{24,20},{28,32},{32,28},{36,40... | collective-permute-start | bytes 245768 | tf_op jit(solution)/shard_map/ppermute | solution.py:470
  24.9 4.4 %collective-permute-start.1 = (f32[5,8,128]{2,1,0:T(8,128)S(1)}, f32[5,8,128]{2,1,0:T(8,128)S(1)}, u32[]{:S(2)}, u32[]{:S(2)}) collective-permute-start(f32[5,8,128]{2,1,0:T(8,128)S(1)} %get-tuple-element.15), channel_id=1, source_target_pairs={{64,128},{128,64},{192,256},{256,192},{320,384},{384,320},{65,129}... | collective-permute-start | bytes 61448 | tf_op jit(solution)/shard_map/ppermute | solution.py:470
  25.6 11.0 %collective-permute-start.4 = (f32[5,16,128]{2,1,0:T(8,128)S(1)}, f32[5,16,128]{2,1,0:T(8,128)S(1)}, u32[]{:S(2)}, u32[]{:S(2)}) collective-permute-start(f32[5,16,128]{2,1,0:T(8,128)S(1)} %get-tuple-element.18), channel_id=1, source_target_pairs={{0,1},{1,0},{2,3},{3,2},{4,5},{5,4},{6,7},{7,6},{8,9},{9,8},{10,11... | collective-permute-start | bytes 122888 | tf_op jit(solution)/shard_map/ppermute | solution.py:470
  28.7 7.9 %collective-permute-start.5 = (f32[5,16,128]{2,1,0:T(8,128)S(1)}, f32[5,16,128]{2,1,0:T(8,128)S(1)}, u32[]{:S(2)}, u32[]{:S(2)}) collective-permute-start(f32[5,16,128]{2,1,0:T(8,128)S(1)} %get-tuple-element.19), channel_id=1, source_target_pairs={{1,2},{2,1},{5,6},{6,5},{9,10},{10,9},{13,14},{14,13},{17,18},{18,... | collective-permute-start | bytes 122888 | tf_op jit(solution)/shard_map/ppermute | solution.py:470
  29.3 7.2 %collective-permute-start = (f32[5,8,128]{2,1,0:T(8,128)S(1)}, f32[5,8,128]{2,1,0:T(8,128)S(1)}, u32[]{:S(2)}, u32[]{:S(2)}) collective-permute-start(f32[5,8,128]{2,1,0:T(8,128)S(1)} %get-tuple-element.15), channel_id=1, source_target_pairs={{0,64},{64,0},{128,192},{192,128},{256,320},{320,256},{384,448},{4... | collective-permute-start | bytes 61448 | tf_op jit(solution)/shard_map/ppermute | solution.py:470
  36.6 25.0 %copy-start.2 = (f32[1,16,1,3,2048]{4,2,3,1,0:T(1,128)S(1)}, f32[1,16,1,3,2048]{4,2,3,1,0:T(1,128)}, u32[]{:S(2)}) copy-start(f32[1,16,1,3,2048]{4,2,3,1,0:T(1,128)} %param.16) | copy-start | bytes 1179652
  36.6 25.0 %copy-start.3 = (s32[1,16,1,2048]{3,2,1,0:T(1,128)S(1)}, s32[1,16,1,2048]{3,2,1,0:T(1,128)}, u32[]{:S(2)}) copy-start(s32[1,16,1,2048]{3,2,1,0:T(1,128)} %refs_11_.1) | copy-start | bytes 393220
  36.6 25.0 %copy-start.4 = (f32[3,64,32]{1,2,0:T(8,128)S(1)}, f32[3,64,32]{1,2,0:T(8,128)}, u32[]{:S(2)}) copy-start(f32[3,64,32]{1,2,0:T(8,128)} %param.18) | copy-start | bytes 73732
  36.6 25.0 %copy-start.5 = (s32[1,1,1,2048]{3,2,1,0:T(1,128)S(1)}, s32[1,1,1,2048]{3,2,1,0:T(1,128)}, u32[]{:S(2)}) copy-start(s32[1,1,1,2048]{3,2,1,0:T(1,128)} %param.15) | copy-start | bytes 24580
  42.7 18.9 %all-to-all-start.1 = ((f32[8,56,128]{2,1,0:T(8,128)}), f32[8,56,128]{2,1,0:T(8,128)S(1)}, u32[]{:S(2)}, u32[]{:S(2)}) async-start(f32[8,56,128]{2,1,0:T(8,128)} %get-tuple-element.21), calls=%async_computation.1 | async-start | bytes 458752 | tf_op jit(solution)/shard_map/all_to_all | solution.py:536
  48.7 12.9 %collective-permute-start.6 = (f32[5,32,128]{2,1,0:T(8,128)S(1)}, f32[5,32,128]{2,1,0:T(8,128)S(1)}, u32[]{:S(2)}, u32[]{:S(2)}) collective-permute-start(f32[5,32,128]{2,1,0:T(8,128)S(1)} %get-tuple-element.22), channel_id=1, source_target_pairs={{0,4},{4,0},{8,12},{12,8},{16,20},{20,16},{24,28},{28,24},{32,36},... | collective-permute-start | bytes 245768 | tf_op jit(solution)/shard_map/ppermute | solution.py:470
  52.4 9.2 %collective-permute-start.7 = (f32[5,32,128]{2,1,0:T(8,128)S(1)}, f32[5,32,128]{2,1,0:T(8,128)S(1)}, u32[]{:S(2)}, u32[]{:S(2)}) collective-permute-start(f32[5,32,128]{2,1,0:T(8,128)S(1)} %get-tuple-element.23), channel_id=1, source_target_pairs={{4,8},{8,4},{12,16},{16,12},{20,24},{24,20},{28,32},{32,28},{36,40... | collective-permute-start | bytes 245768 | tf_op jit(solution)/shard_map/ppermute | solution.py:470
  55.0 6.6 %collective-permute-start.8 = (f32[5,16,128]{2,1,0:T(8,128)S(1)}, f32[5,16,128]{2,1,0:T(8,128)S(1)}, u32[]{:S(2)}, u32[]{:S(2)}) collective-permute-start(f32[5,16,128]{2,1,0:T(8,128)S(1)} %get-tuple-element.24), channel_id=1, source_target_pairs={{0,1},{1,0},{2,3},{3,2},{4,5},{5,4},{6,7},{7,6},{8,9},{9,8},{10,11... | collective-permute-start | bytes 122888 | tf_op jit(solution)/shard_map/ppermute | solution.py:470
  60.2 1.4 %collective-permute-start.9 = (f32[5,16,128]{2,1,0:T(8,128)S(1)}, f32[5,16,128]{2,1,0:T(8,128)S(1)}, u32[]{:S(2)}, u32[]{:S(2)}) collective-permute-start(f32[5,16,128]{2,1,0:T(8,128)S(1)} %get-tuple-element.25), channel_id=1, source_target_pairs={{1,2},{2,1},{5,6},{6,5},{9,10},{10,9},{13,14},{14,13},{17,18},{18,... | collective-permute-start | bytes 122888 | tf_op jit(solution)/shard_map/ppermute | solution.py:470

commit v6 on v5

--- a/solution.py
+++ b/solution.py
@@ -92,9 +92,12 @@
 
 
 def sum_panels(panels_h, owner_h, turn_h, edge_h, out, panels, owner, turn, edge_table, sems):
-    wait_all(
-        fetch((panels_h, owner_h, turn_h, edge_h), (panels, owner, turn, edge_table), sems)
-    )
+    first = fetch((owner_h, turn_h), (owner, turn), sems)
+    fields_in = fetch(
+        [panels_h.at[f] for f in range(NF)], [panels.at[f] for f in range(NF)], sems, 2
+    )
+    last = fetch((edge_h,), (edge_table,), sems, 2 + NF)
+    wait_all(first)
     n_vert = lax.axis_size("vert")
     tiles = turn.shape[0]
     spec = turn.shape[1] // 2
@@ -106,6 +109,7 @@
     cos_t, sin_t = turn[:, :spec], turn[:, spec:]
     turned = []
     for f in range(NF):
+        fields_in[f].wait()
         total = bdot(named, jnp.concatenate(split(panels[f]), axis=0), ((1,), (0,)))
         c, s = total[:, :spec], total[:, spec:]
         c2 = c * cos_t + s * sin_t
@@ -113,6 +117,7 @@
         out[pl.ds(f, tiles, stride=ROWS), :] = c2
         out[pl.ds(8 + f, tiles, stride=ROWS), :] = s2
         turned.append(jnp.concatenate([c2, s2], axis=1))
+    wait_all(last)
     hi, lo = split(jnp.concatenate(turned, axis=0))
     edge = bdot(jnp.concatenate([hi, hi, lo], axis=1), edge_table[...], ((1,), (0,)))
     lane = lax.broadcasted_iota(jnp.int32, (tiles, 128), 1)
@@ -260,8 +265,12 @@
     fields, solid = refs[:2]
     got, xe, xo, ye, yo, ze, zo = refs[2:9]
     base_out, carry_out, ye1, yo1, ze1, zo1 = refs[9:15]
-    q, base, base_sems = refs[15:18]
+    q, base, base_sems, carry, carry_sems = refs[15:20]
     cz = fields.shape[1]
+    total = got[0:ROWS]
+    for i in range(1, got.shape[0] // ROWS):
+        total = total + got[ROWS * i : ROWS * i + ROWS]
+    carry[0:ROWS] = total
 
     def fill(z, carry):
         for f in range(NF):
@@ -295,14 +304,12 @@
         return tuple(placed(accs[f], parts[f], g) for f in range(NF))
 
     accs = lax.fori_loop(0, cz // INNER, body, (zero,) * NF)
+    for f in range(NF):
+        carry[ROWS + 8 * f : ROWS + 8 * f + 8] = accs[f]
+    n_stream = carry_out.shape[0]
+    going = fetch([carry] * n_stream, [carry_out.at[i] for i in range(n_stream)], carry_sems)
     store_faces(base, ye1, yo1, ze1, zo1)
-    total = got[0:ROWS]
-    for i in range(1, got.shape[0] // ROWS):
-        total = total + got[ROWS * i : ROWS * i + ROWS]
-    for i in range(carry_out.shape[0]):
-        carry_out[i, 0:ROWS] = total
-        for f in range(NF):
-            carry_out[i, ROWS + 8 * f : ROWS + 8 * f + 8] = accs[f]
+    wait_all(going)
     for g in range(cz // INNER):
         chunk = pl.ds(g * INNER, INNER)
         pltpu.make_async_copy(base.at[:, chunk], base_out.at[:, chunk], base_sems.at[g]).wait()
@@ -310,28 +317,15 @@
 
 def second_step(*refs):
     fields, solid, base = refs[:3]
-    plane_h, late = refs[3], refs[9:13]
-    carried, ye, yo, ze, zo = refs[4:9]
-    out_h, modal, q, target = refs[13:17]
-    plane_table, late_kept, out, sems, out_sems = refs[17], refs[18:22], *refs[22:25]
-    cells, geom_v, strips_v, shapes = late_kept
+    plane_table, carried, ye, yo, ze, zo, cells, geom, strips, shapes = refs[3:13]
+    out_h, modal, q, target, out, out_sems = refs[13:19]
     cz, cy, cx = fields.shape[1:]
     n_stream = carried.shape[0]
     span_pos = lax.axis_index("span")
     vert_pos = lax.axis_index("vert")
     stream_pos = lax.axis_index("stream")
-    coming = fetch((plane_h,), (plane_table,), sems)
     get_base = pltpu.make_async_copy(base, q.at[:, 1 : cz + 1, 8:24, :], out_sems.at[0])
     get_base.start()
-    cells_h, geom_h, strips_h, shapes_h = late
-    rest = fetch(
-        (cells_h, geom_h.at[0, span_pos], strips_h.at[0, span_pos], shapes_h),
-        late_kept,
-        sems,
-        len(coming),
-    )
-
-    wait_all(coming)
     low, high = carried[0, 0:8], carried[0, 8:16]
     for i in range(1, n_stream):
         low = low + carried[i, 0:8]
@@ -405,10 +399,9 @@
     p_hi = pressure.astype(jnp.bfloat16)
     p_lo = (pressure - p_hi.astype(jnp.float32)).astype(jnp.bfloat16)
     parts = jnp.concatenate([p_hi, p_lo], axis=0)
-    wait_all(rest)
     count = cells.shape[1]
     step = 512
-    n_comp = geom_v.shape[0]
+    n_comp = geom.shape[2]
     own = shapes.shape[2] // lax.axis_size("span")
     sums = [jnp.zeros((8, 128), jnp.float32)] * own
     for at in range(0, count, step):
@@ -420,11 +413,11 @@
         lanes = lax.broadcasted_iota(jnp.int32, (cx, step), 0)
         sample = jnp.sum(jnp.where(lanes == (where & 127), picked, 0.0), axis=0, keepdims=True)
         traction = jnp.concatenate(
-            [sample * geom_v[c, :, at : at + step] for c in range(n_comp)]
+            [sample * geom[0, span_pos, c, :, at : at + step] for c in range(n_comp)]
             + [jnp.zeros((8 - n_comp, step), jnp.float32)],
             axis=0,
         )
-        strip = strips_v[:, at : at + step] - span_pos * own
+        strip = strips[0, span_pos, :, at : at + step] - span_pos * own
         for j in range(own):
             mine = jnp.where(strip == j, traction, 0.0)
             for k in range(0, step, 128):
@@ -491,7 +484,7 @@
         out_shape=f32(tiles * ROWS, 128),
         in_specs=[HB] * 4,
         out_specs=VM,
-        scratch_shapes=buffers(operands) + [pltpu.SemaphoreType.DMA((4,))],
+        scratch_shapes=buffers(operands) + [pltpu.SemaphoreType.DMA((NF + 3,))],
         compiler_params=room(60),
         name="panel_sums",
     )(*operands)
@@ -524,11 +517,13 @@
         first_step,
         out_shape=(f32(NF, cz, cy, cx),) + leaving,
         in_specs=[VM] * 9,
-        out_specs=(HB,) + (VM,) * 5,
+        out_specs=(HB, HB) + (VM,) * 4,
         scratch_shapes=[
             scratch,
             pltpu.VMEM((NF, cz, cy, cx), jnp.float32),
             pltpu.SemaphoreType.DMA((cz // INNER,)),
+            pltpu.VMEM((ROWS + 8 * NF, 128), jnp.float32),
+            pltpu.SemaphoreType.DMA((n_stream,)),
         ],
         compiler_params=room(52),
         name="first_step",
@@ -542,13 +537,12 @@
     new_fields, modal = pl.pallas_call(
         second_step,
         out_shape=(f32(NF, cz, cy, cx), f32(tiles, 128)),
-        in_specs=[VM] * 2 + [HB] * 2 + [VM] * 5 + [HB] * 4,
+        in_specs=[VM] * 2 + [HB] + [VM] * 10,
         out_specs=(HB, VM),
         scratch_shapes=[scratch, pltpu.VMEM((cz * cy, 8), jnp.float32)]
-        + buffers((plane, cells, f32(3, 1, deck), strip_ids[0, 0], shapes))
         + [pltpu.VMEM((NF, cz, cy, cx), jnp.float32)]
-        + [pltpu.SemaphoreType.DMA((5,)), pltpu.SemaphoreType.DMA((cz // INNER + 1,))],
-        compiler_params=room(52),
+        + [pltpu.SemaphoreType.DMA((cz // INNER + 1,))],
+        compiler_params=room(51),
         name="second_step",
     )(
         fields,

time: 104 us -> 104 us (level)
  no operation moved by 1% of the time
where the time goes in v6:
time: 104 us; the launch traced here: 103 us
  starting transfers between devices  48.9 us (47%)
  blocking collectives  34.1 us (33%)
  Pallas kernels  16.6 us (16%)
  waiting for transfers between devices  2.18 us (2%)
    ppermute x10, starting transfers between devices, swapped(): return lax.ppermute(block, axis, pairs)  27.9 us
    all_to_all x1, blocking collectives, on_device(): part = lax.all_to_all(modal, ('span', 'vert'), 0, 0, tiled=True)  20.8 us
    all_to_all x1, starting transfers between devices, on_device(): lax.all_to_all(sent.reshape(tiles, ROWS, 128), ('span', 'vert'), 0, 0, ti...  15 us
    all_to_all x1, blocking collectives, on_device(): part = lax.all_to_all(part, 'stream', 0, 0, tiled=True)  13.3 us
    pallas_call x1, Pallas kernels, on_device(): pl.pallas_call(second_step, out_shape=(f32(NF, cz, cy, cx), f32(tiles, 12...  6.88 us
    all_to_all x1, starting transfers between devices, on_device(): carried = lax.all_to_all(carry, 'stream', 0, 0, tiled=True)  6.02 us
    pallas_call x1, Pallas kernels, on_device(): pl.pallas_call(first_step, out_shape=(f32(NF, cz, cy, cx),) + leaving, in...  5.63 us
    pallas_call x1, Pallas kernels, on_device(): pl.pallas_call(sum_panels, out_shape=f32(tiles * ROWS, 128), in_specs=[HB...  3.08 us
  transfers between devices with their start and end apart: 12, of which 2 were waited for; matrix products, arithmetic and copies ran while one was open for 0% of the time, Pallas kernels for 1%

profile of v6, /device:TPU:1, one launch (start us, length us, event | category | flops | bytes accessed | tf_op | source)
XLA Modules:
  0.0 103.4 jit_solution(2136991853940999140)
XLA Ops:
  0.6 0.0 copy-start
  0.6 3.1 %panel_sums.1 = f32[1024,128]{1,0:T(8,128)} custom-call(f32[5,64,256]{2,1,0:T(8,128)} %bitcast.18, s32[1,64]{1,0:T(1,128)} %bitcast.20, f32[64,256]{1,0:T(8,128)} %constant.8.clone.turn_h, bf16[768,128]{1,0:T(8,128)(2,1)} %constant.9.clone.edge_h), custom_call_target="tpu_custom_call" | custom-call | tf_op jit(solution)/shard_map/panel_sums/pallas_call | solution.py:482
  3.7 0.0 copy-start.1
  3.7 15.0 %all-to-all-start = ((f32[64,16,128]{2,1,0:T(8,128)}), f32[64,16,128]{2,1,0:T(8,128)S(1)}, u32[]{:S(2)}, u32[]{:S(2)}) async-start(f32[64,16,128]{2,1,0:T(8,128)} %bitcast.17), calls=%async_computation | async-start | bytes 1048576 | tf_op jit(solution)/shard_map/all_to_all | solution.py:491
  18.7 1.0 pack_faces.1
  19.8 2.4 %collective-permute-start.2 = (f32[5,32,128]{2,1,0:T(8,128)S(1)}, f32[5,32,128]{2,1,0:T(8,128)S(1)}, u32[]{:S(2)}, u32[]{:S(2)}) collective-permute-start(f32[5,32,128]{2,1,0:T(8,128)S(1)} %get-tuple-element.16), channel_id=1, source_target_pairs={{0,4},{4,0},{8,12},{12,8},{16,20},{20,16},{24,28},{28,24},{32,36},... | collective-permute-start | bytes 245768 | tf_op jit(solution)/shard_map/ppermute | solution.py:463
  22.1 3.2 %collective-permute-start.3 = (f32[5,32,128]{2,1,0:T(8,128)S(1)}, f32[5,32,128]{2,1,0:T(8,128)S(1)}, u32[]{:S(2)}, u32[]{:S(2)}) collective-permute-start(f32[5,32,128]{2,1,0:T(8,128)S(1)} %get-tuple-element.17), channel_id=1, source_target_pairs={{4,8},{8,4},{12,16},{16,12},{20,24},{24,20},{28,32},{32,28},{36,40... | collective-permute-start | bytes 245768 | tf_op jit(solution)/shard_map/ppermute | solution.py:463
  25.4 0.7 collective-permute-start.1
  26.0 3.1 %collective-permute-start.4 = (f32[5,16,128]{2,1,0:T(8,128)S(1)}, f32[5,16,128]{2,1,0:T(8,128)S(1)}, u32[]{:S(2)}, u32[]{:S(2)}) collective-permute-start(f32[5,16,128]{2,1,0:T(8,128)S(1)} %get-tuple-element.18), channel_id=1, source_target_pairs={{0,1},{1,0},{2,3},{3,2},{4,5},{5,4},{6,7},{7,6},{8,9},{9,8},{10,11... | collective-permute-start | bytes 122888 | tf_op jit(solution)/shard_map/ppermute | solution.py:463
  29.1 0.7 collective-permute-start.5
  29.8 5.7 %collective-permute-start = (f32[5,8,128]{2,1,0:T(8,128)S(1)}, f32[5,8,128]{2,1,0:T(8,128)S(1)}, u32[]{:S(2)}, u32[]{:S(2)}) collective-permute-start(f32[5,8,128]{2,1,0:T(8,128)S(1)} %get-tuple-element.15), channel_id=1, source_target_pairs={{0,64},{64,0},{128,192},{192,128},{256,320},{320,256},{384,448},{4... | collective-permute-start | bytes 61448 | tf_op jit(solution)/shard_map/ppermute | solution.py:463
  35.6 1.5 %collective-permute-done.refs_3_ = f32[5,8,128]{2,1,0:T(8,128)S(1)} collective-permute-done((f32[5,8,128]{2,1,0:T(8,128)S(1)}, f32[5,8,128]{2,1,0:T(8,128)S(1)}, u32[]{:S(2)}, u32[]{:S(2)}) %collective-permute-start) | collective-permute-done | bytes 20512 | tf_op jit(solution)/shard_map/ppermute | solution.py:463
  37.0 0.0 collective-permute-done.4.refs_7_
  37.1 0.0 copy-start.2
  37.1 0.0 copy-start.3
  37.1 0.0 copy-start.4
  37.1 0.0 copy-start.5
  37.1 0.0 copy-start.6
  37.1 5.6 %first_step.1 = (f32[5,32,16,128]{3,2,1,0:T(8,128)}, f32[8,56,128]{2,1,0:T(8,128)}, f32[5,32,128]{2,1,0:T(8,128)S(1)}, f32[5,32,128]{2,1,0:T(8,128)S(1)}, f32[5,...) custom-call(f32[5,32,16,128]{3,2,1,0:T(8,128)} %refs_0_.3, f32[32,16,128]{2,1,0:T(8,128)S(1)} %copy-done.1, ...), custom_call_target="tpu_custom_call" | custom-call | tf_op jit(solution)/shard_map/first_step/pallas_call | solution.py:516
  42.8 6.0 %all-to-all-start.1 = ((f32[8,56,128]{2,1,0:T(8,128)}), f32[8,56,128]{2,1,0:T(8,128)S(1)}, u32[]{:S(2)}, u32[]{:S(2)}) async-start(f32[8,56,128]{2,1,0:T(8,128)} %get-tuple-element.21), calls=%async_computation.1 | async-start | bytes 458752 | tf_op jit(solution)/shard_map/all_to_all | solution.py:531
  48.8 3.7 %collective-permute-start.6 = (f32[5,32,128]{2,1,0:T(8,128)S(1)}, f32[5,32,128]{2,1,0:T(8,128)S(1)}, u32[]{:S(2)}, u32[]{:S(2)}) collective-permute-start(f32[5,32,128]{2,1,0:T(8,128)S(1)} %get-tuple-element.22), channel_id=1, source_target_pairs={{0,4},{4,0},{8,12},{12,8},{16,20},{20,16},{24,28},{28,24},{32,36},... | collective-permute-start | bytes 245768 | tf_op jit(solution)/shard_map/ppermute | solution.py:463
  52.5 2.5 %collective-permute-start.7 = (f32[5,32,128]{2,1,0:T(8,128)S(1)}, f32[5,32,128]{2,1,0:T(8,128)S(1)}, u32[]{:S(2)}, u32[]{:S(2)}) collective-permute-start(f32[5,32,128]{2,1,0:T(8,128)S(1)} %get-tuple-element.23), channel_id=1, source_target_pairs={{4,8},{8,4},{12,16},{16,12},{20,24},{24,20},{28,32},{32,28},{36,40... | collective-permute-start | bytes 245768 | tf_op jit(solution)/shard_map/ppermute | solution.py:463
  55.1 5.3 %collective-permute-start.8 = (f32[5,16,128]{2,1,0:T(8,128)S(1)}, f32[5,16,128]{2,1,0:T(8,128)S(1)}, u32[]{:S(2)}, u32[]{:S(2)}) collective-permute-start(f32[5,16,128]{2,1,0:T(8,128)S(1)} %get-tuple-element.24), channel_id=1, source_target_pairs={{0,1},{1,0},{2,3},{3,2},{4,5},{5,4},{6,7},{7,6},{8,9},{9,8},{10,11... | collective-permute-start | bytes 122888 | tf_op jit(solution)/shard_map/ppermute | solution.py:463
  60.3 0.7 collective-permute-start.9
  61.0 0.7 collective-permute-done.8.refs_7_
  61.7 0.0 collective-permute-done.9.refs_8_
  61.7 0.0 collective-permute-done.6.refs_5_
  61.8 6.9 %second_step.1 = (f32[5,32,16,128]{3,2,1,0:T(8,128)}, f32[64,128]{1,0:T(8,128)S(1)}) custom-call(f32[5,32,16,128]{3,2,1,0:T(8,128)} %refs_0_.3, f32[32,16,128]{2,1,0:T(8,128)S(1)} %copy-done.1, f32[5,32,16,128]{3,2,1,0:T(8,128)} %get-tuple-element.20.refs_2_, bf16[512,768]{1,0:T(8,128)(2,1)S(1)} %copy-done.2, f32[8,56,128]{2,1,0:T(8,128)S(1)} %all-to-all-done.1.refs_4_, ...), custom_call_target="tpu_custom_call" | custom-call | tf_op jit(solution)/shard_map/second_step/pallas_call | solution.py:537
  68.7 20.8 %all_to_all.25 = f32[64,1,128]{2,1,0:T(1,128)S(1)} all-to-all(f32[64,1,128]{2,1,0:T(1,128)S(1)} %bitcast.15), channel_id=1, replica_groups=mesh['stream'=8,'span'=16,'vert'=4] {'span','vert'}, dimensions={0} | all-to-all | bytes 65536 | tf_op jit(solution)/shard_map/all_to_all | solution.py:559
  89.5 0.1 reduce_sum.18
  89.6 13.3 %all_to_all.26 = f32[8,1,128]{2,1,0:T(1,128)S(1)} all-to-all(f32[8,1,128]{2,1,0:T(1,128)S(1)} %broadcast_in_dim.2), channel_id=1, replica_groups=mesh['stream'=8,'span'=16,'vert'=4] {'stream'}, dimensions={0} | all-to-all | bytes 8192 | tf_op jit(solution)/shard_map/all_to_all | solution.py:561
  102.8 0.5 reduce_sum.19
  (15 shorter events, 0.0 us)
Async XLA Ops:
  0.6 18.1 %copy-start = (f32[5,32,16,128]{3,2,1,0:T(8,128)S(1)}, f32[5,32,16,128]{3,2,1,0:T(8,128)}, u32[]{:S(2)}) copy-start(f32[5,32,16,128]{3,2,1,0:T(8,128)} %refs_0_.3) | copy-start | bytes 3932164
  3.7 33.3 %copy-start.1 = (f32[32,16,128]{2,1,0:T(8,128)S(1)}, f32[32,16,128]{2,1,0:T(8,128)}, u32[]{:S(2)}) copy-start(f32[32,16,128]{2,1,0:T(8,128)} %refs_1_.3) | copy-start | bytes 786436
  3.7 33.3 %all-to-all-start = ((f32[64,16,128]{2,1,0:T(8,128)}), f32[64,16,128]{2,1,0:T(8,128)S(1)}, u32[]{:S(2)}, u32[]{:S(2)}) async-start(f32[64,16,128]{2,1,0:T(8,128)} %bitcast.17), calls=%async_computation | async-start | bytes 1048576 | tf_op jit(solution)/shard_map/all_to_all | solution.py:491
  19.8 17.3 %collective-permute-start.2 = (f32[5,32,128]{2,1,0:T(8,128)S(1)}, f32[5,32,128]{2,1,0:T(8,128)S(1)}, u32[]{:S(2)}, u32[]{:S(2)}) collective-permute-start(f32[5,32,128]{2,1,0:T(8,128)S(1)} %get-tuple-element.16), channel_id=1, source_target_pairs={{0,4},{4,0},{8,12},{12,8},{16,20},{20,16},{24,28},{28,24},{32,36},... | collective-permute-start | bytes 245768 | tf_op jit(solution)/shard_map/ppermute | solution.py:463
  22.1 14.9 %collective-permute-start.3 = (f32[5,32,128]{2,1,0:T(8,128)S(1)}, f32[5,32,128]{2,1,0:T(8,128)S(1)}, u32[]{:S(2)}, u32[]{:S(2)}) collective-permute-start(f32[5,32,128]{2,1,0:T(8,128)S(1)} %get-tuple-element.17), channel_id=1, source_target_pairs={{4,8},{8,4},{12,16},{16,12},{20,24},{24,20},{28,32},{32,28},{36,40... | collective-permute-start | bytes 245768 | tf_op jit(solution)/shard_map/ppermute | solution.py:463
  25.4 4.4 %collective-permute-start.1 = (f32[5,8,128]{2,1,0:T(8,128)S(1)}, f32[5,8,128]{2,1,0:T(8,128)S(1)}, u32[]{:S(2)}, u32[]{:S(2)}) collective-permute-start(f32[5,8,128]{2,1,0:T(8,128)S(1)} %get-tuple-element.15), channel_id=1, source_target_pairs={{64,128},{128,64},{192,256},{256,192},{320,384},{384,320},{65,129}... | collective-permute-start | bytes 61448 | tf_op jit(solution)/shard_map/ppermute | solution.py:463
  26.0 11.0 %collective-permute-start.4 = (f32[5,16,128]{2,1,0:T(8,128)S(1)}, f32[5,16,128]{2,1,0:T(8,128)S(1)}, u32[]{:S(2)}, u32[]{:S(2)}) collective-permute-start(f32[5,16,128]{2,1,0:T(8,128)S(1)} %get-tuple-element.18), channel_id=1, source_target_pairs={{0,1},{1,0},{2,3},{3,2},{4,5},{5,4},{6,7},{7,6},{8,9},{9,8},{10,11... | collective-permute-start | bytes 122888 | tf_op jit(solution)/shard_map/ppermute | solution.py:463
  29.1 7.9 %collective-permute-start.5 = (f32[5,16,128]{2,1,0:T(8,128)S(1)}, f32[5,16,128]{2,1,0:T(8,128)S(1)}, u32[]{:S(2)}, u32[]{:S(2)}) collective-permute-start(f32[5,16,128]{2,1,0:T(8,128)S(1)} %get-tuple-element.19), channel_id=1, source_target_pairs={{1,2},{2,1},{5,6},{6,5},{9,10},{10,9},{13,14},{14,13},{17,18},{18,... | collective-permute-start | bytes 122888 | tf_op jit(solution)/shard_map/ppermute | solution.py:463
  29.8 7.2 %collective-permute-start = (f32[5,8,128]{2,1,0:T(8,128)S(1)}, f32[5,8,128]{2,1,0:T(8,128)S(1)}, u32[]{:S(2)}, u32[]{:S(2)}) collective-permute-start(f32[5,8,128]{2,1,0:T(8,128)S(1)} %get-tuple-element.15), channel_id=1, source_target_pairs={{0,64},{64,0},{128,192},{192,128},{256,320},{320,256},{384,448},{4... | collective-permute-start | bytes 61448 | tf_op jit(solution)/shard_map/ppermute | solution.py:463
  37.1 24.6 %copy-start.2 = (bf16[512,768]{1,0:T(8,128)(2,1)S(1)}, bf16[512,768]{1,0:T(8,128)(2,1)}, u32[]{:S(2)}) copy-start(bf16[512,768]{1,0:T(8,128)(2,1)} %constant.10.clone.refs_3_) | copy-start | bytes 2359300
  37.1 24.6 %copy-start.3 = (f32[1,16,1,3,2048]{4,2,3,1,0:T(1,128)S(1)}, f32[1,16,1,3,2048]{4,2,3,1,0:T(1,128)}, u32[]{:S(2)}) copy-start(f32[1,16,1,3,2048]{4,2,3,1,0:T(1,128)} %param.16) | copy-start | bytes 1179652
  37.1 24.6 %copy-start.4 = (s32[1,16,1,2048]{3,2,1,0:T(1,128)S(1)}, s32[1,16,1,2048]{3,2,1,0:T(1,128)}, u32[]{:S(2)}) copy-start(s32[1,16,1,2048]{3,2,1,0:T(1,128)} %refs_11_.1) | copy-start | bytes 393220
  37.1 24.6 %copy-start.5 = (f32[3,64,32]{1,2,0:T(8,128)S(1)}, f32[3,64,32]{1,2,0:T(8,128)}, u32[]{:S(2)}) copy-start(f32[3,64,32]{1,2,0:T(8,128)} %param.18) | copy-start | bytes 73732
  37.1 24.6 %copy-start.6 = (s32[1,1,1,2048]{3,2,1,0:T(1,128)S(1)}, s32[1,1,1,2048]{3,2,1,0:T(1,128)}, u32[]{:S(2)}) copy-start(s32[1,1,1,2048]{3,2,1,0:T(1,128)} %param.15) | copy-start | bytes 24580
  42.8 18.9 %all-to-all-start.1 = ((f32[8,56,128]{2,1,0:T(8,128)}), f32[8,56,128]{2,1,0:T(8,128)S(1)}, u32[]{:S(2)}, u32[]{:S(2)}) async-start(f32[8,56,128]{2,1,0:T(8,128)} %get-tuple-element.21), calls=%async_computation.1 | async-start | bytes 458752 | tf_op jit(solution)/shard_map/all_to_all | solution.py:531
  48.8 12.9 %collective-permute-start.6 = (f32[5,32,128]{2,1,0:T(8,128)S(1)}, f32[5,32,128]{2,1,0:T(8,128)S(1)}, u32[]{:S(2)}, u32[]{:S(2)}) collective-permute-start(f32[5,32,128]{2,1,0:T(8,128)S(1)} %get-tuple-element.22), channel_id=1, source_target_pairs={{0,4},{4,0},{8,12},{12,8},{16,20},{20,16},{24,28},{28,24},{32,36},... | collective-permute-start | bytes 245768 | tf_op jit(solution)/shard_map/ppermute | solution.py:463
  52.5 9.2 %collective-permute-start.7 = (f32[5,32,128]{2,1,0:T(8,128)S(1)}, f32[5,32,128]{2,1,0:T(8,128)S(1)}, u32[]{:S(2)}, u32[]{:S(2)}) collective-permute-start(f32[5,32,128]{2,1,0:T(8,128)S(1)} %get-tuple-element.23), channel_id=1, source_target_pairs={{4,8},{8,4},{12,16},{16,12},{20,24},{24,20},{28,32},{32,28},{36,40... | collective-permute-start | bytes 245768 | tf_op jit(solution)/shard_map/ppermute | solution.py:463
  55.1 6.6 %collective-permute-start.8 = (f32[5,16,128]{2,1,0:T(8,128)S(1)}, f32[5,16,128]{2,1,0:T(8,128)S(1)}, u32[]{:S(2)}, u32[]{:S(2)}) collective-permute-start(f32[5,16,128]{2,1,0:T(8,128)S(1)} %get-tuple-element.24), channel_id=1, source_target_pairs={{0,1},{1,0},{2,3},{3,2},{4,5},{5,4},{6,7},{7,6},{8,9},{9,8},{10,11... | collective-permute-start | bytes 122888 | tf_op jit(solution)/shard_map/ppermute | solution.py:463
  60.3 1.4 %collective-permute-start.9 = (f32[5,16,128]{2,1,0:T(8,128)S(1)}, f32[5,16,128]{2,1,0:T(8,128)S(1)}, u32[]{:S(2)}, u32[]{:S(2)}) collective-permute-start(f32[5,16,128]{2,1,0:T(8,128)S(1)} %get-tuple-element.25), channel_id=1, source_target_pairs={{1,2},{2,1},{5,6},{6,5},{9,10},{10,9},{13,14},{14,13},{17,18},{18,... | collective-permute-start | bytes 122888 | tf_op jit(solution)/shard_map/ppermute | solution.py:463

commit v7 on v6

--- a/solution.py
+++ b/solution.py
@@ -92,12 +92,9 @@
 
 
 def sum_panels(panels_h, owner_h, turn_h, edge_h, out, panels, owner, turn, edge_table, sems):
-    first = fetch((owner_h, turn_h), (owner, turn), sems)
-    fields_in = fetch(
-        [panels_h.at[f] for f in range(NF)], [panels.at[f] for f in range(NF)], sems, 2
-    )
-    last = fetch((edge_h,), (edge_table,), sems, 2 + NF)
-    wait_all(first)
+    wait_all(
+        fetch((panels_h, owner_h, turn_h, edge_h), (panels, owner, turn, edge_table), sems)
+    )
     n_vert = lax.axis_size("vert")
     tiles = turn.shape[0]
     spec = turn.shape[1] // 2
@@ -109,7 +106,6 @@
     cos_t, sin_t = turn[:, :spec], turn[:, spec:]
     turned = []
     for f in range(NF):
-        fields_in[f].wait()
         total = bdot(named, jnp.concatenate(split(panels[f]), axis=0), ((1,), (0,)))
         c, s = total[:, :spec], total[:, spec:]
         c2 = c * cos_t + s * sin_t
@@ -117,7 +113,6 @@
         out[pl.ds(f, tiles, stride=ROWS), :] = c2
         out[pl.ds(8 + f, tiles, stride=ROWS), :] = s2
         turned.append(jnp.concatenate([c2, s2], axis=1))
-    wait_all(last)
     hi, lo = split(jnp.concatenate(turned, axis=0))
     edge = bdot(jnp.concatenate([hi, hi, lo], axis=1), edge_table[...], ((1,), (0,)))
     lane = lax.broadcasted_iota(jnp.int32, (tiles, 128), 1)
@@ -484,7 +479,7 @@
         out_shape=f32(tiles * ROWS, 128),
         in_specs=[HB] * 4,
         out_specs=VM,
-        scratch_shapes=buffers(operands) + [pltpu.SemaphoreType.DMA((NF + 3,))],
+        scratch_shapes=buffers(operands) + [pltpu.SemaphoreType.DMA((4,))],
         compiler_params=room(60),
         name="panel_sums",
     )(*operands)
@@ -536,7 +531,7 @@
     shapes = mode_shapes.transpose(0, 2, 1)
     new_fields, modal = pl.pallas_call(
         second_step,
-        out_shape=(f32(NF, cz, cy, cx), f32(tiles, 128)),
+        out_shape=(f32(NF, cz, cy, cx), f32(n_span, 128)),
         in_specs=[VM] * 2 + [HB] + [VM] * 10,
         out_specs=(HB, VM),
         scratch_shapes=[scratch, pltpu.VMEM((cz * cy, 8), jnp.float32)]
@@ -556,9 +551,9 @@
         strip_ids,
         shapes,
     )
-    part = lax.all_to_all(modal, ("span", "vert"), 0, 0, tiled=True)
-    part = jnp.broadcast_to(jnp.sum(part, axis=0, keepdims=True), (n_stream, 128))
-    part = lax.all_to_all(part, "stream", 0, 0, tiled=True)
+    part = lax.all_to_all(modal, "span", 0, 0, tiled=True)
+    part = jnp.broadcast_to(jnp.sum(part, axis=0, keepdims=True), (n_stream * n_vert, 128))
+    part = lax.all_to_all(part, ("stream", "vert"), 0, 0, tiled=True)
     modal_force = jnp.sum(part, axis=0)[: mode_shapes.shape[2]]
     return (new_fields, modal_force)
 

time: 104 us -> 103 us (level)
  no operation moved by 1% of the time
where the time goes in v7:
time: 103 us
  starting transfers between devices  48.9 us (47%)
  blocking collectives  33.8 us (33%)
  Pallas kernels  16.1 us (16%)
  waiting for transfers between devices  2.18 us (2%)
    ppermute x10, starting transfers between devices, swapped(): return lax.ppermute(block, axis, pairs)  27.9 us
    all_to_all x1, blocking collectives, on_device(): part = lax.all_to_all(part, ('stream', 'vert'), 0, 0, tiled=True)  19.7 us
    all_to_all x1, starting transfers between devices, on_device(): lax.all_to_all(sent.reshape(tiles, ROWS, 128), ('span', 'vert'), 0, 0, ti...  15 us
    all_to_all x1, blocking collectives, on_device(): part = lax.all_to_all(modal, 'span', 0, 0, tiled=True)  14.1 us
    pallas_call x1, Pallas kernels, on_device(): pl.pallas_call(second_step, out_shape=(f32(NF, cz, cy, cx), f32(n_span, 1...  6.87 us
    all_to_all x1, starting transfers between devices, on_device(): carried = lax.all_to_all(carry, 'stream', 0, 0, tiled=True)  6.02 us
    pallas_call x1, Pallas kernels, on_device(): pl.pallas_call(first_step, out_shape=(f32(NF, cz, cy, cx),) + leaving, in...  5.63 us
    pallas_call x1, Pallas kernels, on_device(): pl.pallas_call(sum_panels, out_shape=f32(tiles * ROWS, 128), in_specs=[HB...  2.59 us
  transfers between devices with their start and end apart: 12, of which 2 were waited for; matrix products, arithmetic and copies ran while one was open for 0% of the time, Pallas kernels for 1%

profile of v7, /device:TPU:1, one launch (start us, length us, event | category | flops | bytes accessed | tf_op | source)
XLA Modules:
  0.0 102.6 jit_solution(6524237327700278143)
XLA Ops:
  0.6 0.0 copy-start
  0.6 2.6 %panel_sums.1 = f32[1024,128]{1,0:T(8,128)} custom-call(f32[5,64,256]{2,1,0:T(8,128)} %bitcast.18, s32[1,64]{1,0:T(1,128)} %bitcast.20, f32[64,256]{1,0:T(8,128)} %constant.8.clone.turn_h, bf16[768,128]{1,0:T(8,128)(2,1)} %constant.9.clone.edge_h), custom_call_target="tpu_custom_call" | custom-call | tf_op jit(solution)/shard_map/panel_sums/pallas_call | solution.py:477
  3.2 0.0 copy-start.1
  3.2 15.0 %all-to-all-start = ((f32[64,16,128]{2,1,0:T(8,128)}), f32[64,16,128]{2,1,0:T(8,128)S(1)}, u32[]{:S(2)}, u32[]{:S(2)}) async-start(f32[64,16,128]{2,1,0:T(8,128)} %bitcast.17), calls=%async_computation | async-start | bytes 1048576 | tf_op jit(solution)/shard_map/all_to_all | solution.py:486
  18.2 1.0 pack_faces.1
  19.3 2.4 %collective-permute-start.2 = (f32[5,32,128]{2,1,0:T(8,128)S(1)}, f32[5,32,128]{2,1,0:T(8,128)S(1)}, u32[]{:S(2)}, u32[]{:S(2)}) collective-permute-start(f32[5,32,128]{2,1,0:T(8,128)S(1)} %get-tuple-element.16), channel_id=1, source_target_pairs={{0,4},{4,0},{8,12},{12,8},{16,20},{20,16},{24,28},{28,24},{32,36},... | collective-permute-start | bytes 245768 | tf_op jit(solution)/shard_map/ppermute | solution.py:458
  21.6 3.2 %collective-permute-start.3 = (f32[5,32,128]{2,1,0:T(8,128)S(1)}, f32[5,32,128]{2,1,0:T(8,128)S(1)}, u32[]{:S(2)}, u32[]{:S(2)}) collective-permute-start(f32[5,32,128]{2,1,0:T(8,128)S(1)} %get-tuple-element.17), channel_id=1, source_target_pairs={{4,8},{8,4},{12,16},{16,12},{20,24},{24,20},{28,32},{32,28},{36,40... | collective-permute-start | bytes 245768 | tf_op jit(solution)/shard_map/ppermute | solution.py:458
  24.9 0.7 collective-permute-start.1
  25.6 3.1 %collective-permute-start.4 = (f32[5,16,128]{2,1,0:T(8,128)S(1)}, f32[5,16,128]{2,1,0:T(8,128)S(1)}, u32[]{:S(2)}, u32[]{:S(2)}) collective-permute-start(f32[5,16,128]{2,1,0:T(8,128)S(1)} %get-tuple-element.18), channel_id=1, source_target_pairs={{0,1},{1,0},{2,3},{3,2},{4,5},{5,4},{6,7},{7,6},{8,9},{9,8},{10,11... | collective-permute-start | bytes 122888 | tf_op jit(solution)/shard_map/ppermute | solution.py:458
  28.7 0.7 collective-permute-start.5
  29.3 0.0 collective-permute-done.1.refs_4_
  29.3 5.7 %collective-permute-start = (f32[5,8,128]{2,1,0:T(8,128)S(1)}, f32[5,8,128]{2,1,0:T(8,128)S(1)}, u32[]{:S(2)}, u32[]{:S(2)}) collective-permute-start(f32[5,8,128]{2,1,0:T(8,128)S(1)} %get-tuple-element.15), channel_id=1, source_target_pairs={{0,64},{64,0},{128,192},{192,128},{256,320},{320,256},{384,448},{4... | collective-permute-start | bytes 61448 | tf_op jit(solution)/shard_map/ppermute | solution.py:458
  35.1 1.5 %collective-permute-done.refs_3_ = f32[5,8,128]{2,1,0:T(8,128)S(1)} collective-permute-done((f32[5,8,128]{2,1,0:T(8,128)S(1)}, f32[5,8,128]{2,1,0:T(8,128)S(1)}, u32[]{:S(2)}, u32[]{:S(2)}) %collective-permute-start) | collective-permute-done | bytes 20512 | tf_op jit(solution)/shard_map/ppermute | solution.py:458
  36.5 0.0 collective-permute-done.4.refs_7_
  36.5 0.0 collective-permute-done.5.refs_8_
  36.6 0.0 all-to-all-done
  36.6 0.0 copy-start.2
  36.6 0.0 copy-start.3
  36.6 0.0 copy-start.4
  36.6 0.0 copy-start.5
  36.6 0.0 copy-start.6
  36.6 5.6 %first_step.1 = (f32[5,32,16,128]{3,2,1,0:T(8,128)}, f32[8,56,128]{2,1,0:T(8,128)}, f32[5,32,128]{2,1,0:T(8,128)S(1)}, f32[5,32,128]{2,1,0:T(8,128)S(1)}, f32[5,...) custom-call(f32[5,32,16,128]{3,2,1,0:T(8,128)} %refs_0_.3, f32[32,16,128]{2,1,0:T(8,128)S(1)} %copy-done.1, ...), custom_call_target="tpu_custom_call" | custom-call | tf_op jit(solution)/shard_map/first_step/pallas_call | solution.py:511
  42.3 6.0 %all-to-all-start.1 = ((f32[8,56,128]{2,1,0:T(8,128)}), f32[8,56,128]{2,1,0:T(8,128)S(1)}, u32[]{:S(2)}, u32[]{:S(2)}) async-start(f32[8,56,128]{2,1,0:T(8,128)} %get-tuple-element.21), calls=%async_computation.1 | async-start | bytes 458752 | tf_op jit(solution)/shard_map/all_to_all | solution.py:526
  48.3 3.7 %collective-permute-start.6 = (f32[5,32,128]{2,1,0:T(8,128)S(1)}, f32[5,32,128]{2,1,0:T(8,128)S(1)}, u32[]{:S(2)}, u32[]{:S(2)}) collective-permute-start(f32[5,32,128]{2,1,0:T(8,128)S(1)} %get-tuple-element.22), channel_id=1, source_target_pairs={{0,4},{4,0},{8,12},{12,8},{16,20},{20,16},{24,28},{28,24},{32,36},... | collective-permute-start | bytes 245768 | tf_op jit(solution)/shard_map/ppermute | solution.py:458
  52.0 2.5 %collective-permute-start.7 = (f32[5,32,128]{2,1,0:T(8,128)S(1)}, f32[5,32,128]{2,1,0:T(8,128)S(1)}, u32[]{:S(2)}, u32[]{:S(2)}) collective-permute-start(f32[5,32,128]{2,1,0:T(8,128)S(1)} %get-tuple-element.23), channel_id=1, source_target_pairs={{4,8},{8,4},{12,16},{16,12},{20,24},{24,20},{28,32},{32,28},{36,40... | collective-permute-start | bytes 245768 | tf_op jit(solution)/shard_map/ppermute | solution.py:458
  54.6 5.3 %collective-permute-start.8 = (f32[5,16,128]{2,1,0:T(8,128)S(1)}, f32[5,16,128]{2,1,0:T(8,128)S(1)}, u32[]{:S(2)}, u32[]{:S(2)}) collective-permute-start(f32[5,16,128]{2,1,0:T(8,128)S(1)} %get-tuple-element.24), channel_id=1, source_target_pairs={{0,1},{1,0},{2,3},{3,2},{4,5},{5,4},{6,7},{7,6},{8,9},{9,8},{10,11... | collective-permute-start | bytes 122888 | tf_op jit(solution)/shard_map/ppermute | solution.py:458
  59.8 0.7 collective-permute-start.9
  60.5 0.7 collective-permute-done.8.refs_7_
  61.3 6.9 %second_step.1 = (f32[5,32,16,128]{3,2,1,0:T(8,128)}, f32[16,128]{1,0:T(8,128)S(1)}) custom-call(f32[5,32,16,128]{3,2,1,0:T(8,128)} %refs_0_.3, f32[32,16,128]{2,1,0:T(8,128)S(1)} %copy-done.1, f32[5,32,16,128]{3,2,1,0:T(8,128)} %get-tuple-element.20.refs_2_, bf16[512,768]{1,0:T(8,128)(2,1)S(1)} %copy-done.2, f32[8,56,128]{2,1,0:T(8,128)S(1)} %all-to-all-done.1.refs_4_, ...), custom_call_target="tpu_custom_call" | custom-call | tf_op jit(solution)/shard_map/second_step/pallas_call | solution.py:532
  68.2 14.1 %all_to_all.25 = f32[16,1,128]{2,1,0:T(1,128)S(1)} all-to-all(f32[16,1,128]{2,1,0:T(1,128)S(1)} %bitcast.16), channel_id=1, replica_groups=mesh['stream'=8,'span'=16,'vert'=4] {'span'}, dimensions={0} | all-to-all | bytes 16384 | tf_op jit(solution)/shard_map/all_to_all | solution.py:554
  82.3 19.7 %all_to_all.26 = f32[32,1,128]{2,1,0:T(1,128)S(1)} all-to-all(f32[32,1,128]{2,1,0:T(1,128)S(1)} %broadcast_in_dim.2), channel_id=1, replica_groups=mesh['stream'=8,'span'=16,'vert'=4] {'stream','vert'}, dimensions={0} | all-to-all | bytes 32768 | tf_op jit(solution)/shard_map/all_to_all | solution.py:556
  102.0 0.5 reduce_sum.19
  (15 shorter events, 0.1 us)
Async XLA Ops:
  0.6 17.6 %copy-start = (f32[5,32,16,128]{3,2,1,0:T(8,128)S(1)}, f32[5,32,16,128]{3,2,1,0:T(8,128)}, u32[]{:S(2)}) copy-start(f32[5,32,16,128]{3,2,1,0:T(8,128)} %refs_0_.3) | copy-start | bytes 3932164
  3.2 33.3 %copy-start.1 = (f32[32,16,128]{2,1,0:T(8,128)S(1)}, f32[32,16,128]{2,1,0:T(8,128)}, u32[]{:S(2)}) copy-start(f32[32,16,128]{2,1,0:T(8,128)} %refs_1_.3) | copy-start | bytes 786436
  3.2 33.3 %all-to-all-start = ((f32[64,16,128]{2,1,0:T(8,128)}), f32[64,16,128]{2,1,0:T(8,128)S(1)}, u32[]{:S(2)}, u32[]{:S(2)}) async-start(f32[64,16,128]{2,1,0:T(8,128)} %bitcast.17), calls=%async_computation | async-start | bytes 1048576 | tf_op jit(solution)/shard_map/all_to_all | solution.py:486
  19.3 17.3 %collective-permute-start.2 = (f32[5,32,128]{2,1,0:T(8,128)S(1)}, f32[5,32,128]{2,1,0:T(8,128)S(1)}, u32[]{:S(2)}, u32[]{:S(2)}) collective-permute-start(f32[5,32,128]{2,1,0:T(8,128)S(1)} %get-tuple-element.16), channel_id=1, source_target_pairs={{0,4},{4,0},{8,12},{12,8},{16,20},{20,16},{24,28},{28,24},{32,36},... | collective-permute-start | bytes 245768 | tf_op jit(solution)/shard_map/ppermute | solution.py:458
  21.6 14.9 %collective-permute-start.3 = (f32[5,32,128]{2,1,0:T(8,128)S(1)}, f32[5,32,128]{2,1,0:T(8,128)S(1)}, u32[]{:S(2)}, u32[]{:S(2)}) collective-permute-start(f32[5,32,128]{2,1,0:T(8,128)S(1)} %get-tuple-element.17), channel_id=1, source_target_pairs={{4,8},{8,4},{12,16},{16,12},{20,24},{24,20},{28,32},{32,28},{36,40... | collective-permute-start | bytes 245768 | tf_op jit(solution)/shard_map/ppermute | solution.py:458
  24.9 4.4 %collective-permute-start.1 = (f32[5,8,128]{2,1,0:T(8,128)S(1)}, f32[5,8,128]{2,1,0:T(8,128)S(1)}, u32[]{:S(2)}, u32[]{:S(2)}) collective-permute-start(f32[5,8,128]{2,1,0:T(8,128)S(1)} %get-tuple-element.15), channel_id=1, source_target_pairs={{64,128},{128,64},{192,256},{256,192},{320,384},{384,320},{65,129}... | collective-permute-start | bytes 61448 | tf_op jit(solution)/shard_map/ppermute | solution.py:458
  25.6 11.0 %collective-permute-start.4 = (f32[5,16,128]{2,1,0:T(8,128)S(1)}, f32[5,16,128]{2,1,0:T(8,128)S(1)}, u32[]{:S(2)}, u32[]{:S(2)}) collective-permute-start(f32[5,16,128]{2,1,0:T(8,128)S(1)} %get-tuple-element.18), channel_id=1, source_target_pairs={{0,1},{1,0},{2,3},{3,2},{4,5},{5,4},{6,7},{7,6},{8,9},{9,8},{10,11... | collective-permute-start | bytes 122888 | tf_op jit(solution)/shard_map/ppermute | solution.py:458
  28.7 7.9 %collective-permute-start.5 = (f32[5,16,128]{2,1,0:T(8,128)S(1)}, f32[5,16,128]{2,1,0:T(8,128)S(1)}, u32[]{:S(2)}, u32[]{:S(2)}) collective-permute-start(f32[5,16,128]{2,1,0:T(8,128)S(1)} %get-tuple-element.19), channel_id=1, source_target_pairs={{1,2},{2,1},{5,6},{6,5},{9,10},{10,9},{13,14},{14,13},{17,18},{18,... | collective-permute-start | bytes 122888 | tf_op jit(solution)/shard_map/ppermute | solution.py:458
  29.3 7.2 %collective-permute-start = (f32[5,8,128]{2,1,0:T(8,128)S(1)}, f32[5,8,128]{2,1,0:T(8,128)S(1)}, u32[]{:S(2)}, u32[]{:S(2)}) collective-permute-start(f32[5,8,128]{2,1,0:T(8,128)S(1)} %get-tuple-element.15), channel_id=1, source_target_pairs={{0,64},{64,0},{128,192},{192,128},{256,320},{320,256},{384,448},{4... | collective-permute-start | bytes 61448 | tf_op jit(solution)/shard_map/ppermute | solution.py:458
  36.6 24.6 %copy-start.2 = (bf16[512,768]{1,0:T(8,128)(2,1)S(1)}, bf16[512,768]{1,0:T(8,128)(2,1)}, u32[]{:S(2)}) copy-start(bf16[512,768]{1,0:T(8,128)(2,1)} %constant.10.clone.refs_3_) | copy-start | bytes 2359300
  36.6 24.6 %copy-start.3 = (f32[1,16,1,3,2048]{4,2,3,1,0:T(1,128)S(1)}, f32[1,16,1,3,2048]{4,2,3,1,0:T(1,128)}, u32[]{:S(2)}) copy-start(f32[1,16,1,3,2048]{4,2,3,1,0:T(1,128)} %param.16) | copy-start | bytes 1179652
  36.6 24.6 %copy-start.4 = (s32[1,16,1,2048]{3,2,1,0:T(1,128)S(1)}, s32[1,16,1,2048]{3,2,1,0:T(1,128)}, u32[]{:S(2)}) copy-start(s32[1,16,1,2048]{3,2,1,0:T(1,128)} %refs_11_.1) | copy-start | bytes 393220
  36.6 24.6 %copy-start.5 = (f32[3,64,32]{1,2,0:T(8,128)S(1)}, f32[3,64,32]{1,2,0:T(8,128)}, u32[]{:S(2)}) copy-start(f32[3,64,32]{1,2,0:T(8,128)} %param.18) | copy-start | bytes 73732
  36.6 24.6 %copy-start.6 = (s32[1,1,1,2048]{3,2,1,0:T(1,128)S(1)}, s32[1,1,1,2048]{3,2,1,0:T(1,128)}, u32[]{:S(2)}) copy-start(s32[1,1,1,2048]{3,2,1,0:T(1,128)} %param.15) | copy-start | bytes 24580
  42.3 18.9 %all-to-all-start.1 = ((f32[8,56,128]{2,1,0:T(8,128)}), f32[8,56,128]{2,1,0:T(8,128)S(1)}, u32[]{:S(2)}, u32[]{:S(2)}) async-start(f32[8,56,128]{2,1,0:T(8,128)} %get-tuple-element.21), calls=%async_computation.1 | async-start | bytes 458752 | tf_op jit(solution)/shard_map/all_to_all | solution.py:526
  48.3 12.9 %collective-permute-start.6 = (f32[5,32,128]{2,1,0:T(8,128)S(1)}, f32[5,32,128]{2,1,0:T(8,128)S(1)}, u32[]{:S(2)}, u32[]{:S(2)}) collective-permute-start(f32[5,32,128]{2,1,0:T(8,128)S(1)} %get-tuple-element.22), channel_id=1, source_target_pairs={{0,4},{4,0},{8,12},{12,8},{16,20},{20,16},{24,28},{28,24},{32,36},... | collective-permute-start | bytes 245768 | tf_op jit(solution)/shard_map/ppermute | solution.py:458
  52.0 9.2 %collective-permute-start.7 = (f32[5,32,128]{2,1,0:T(8,128)S(1)}, f32[5,32,128]{2,1,0:T(8,128)S(1)}, u32[]{:S(2)}, u32[]{:S(2)}) collective-permute-start(f32[5,32,128]{2,1,0:T(8,128)S(1)} %get-tuple-element.23), channel_id=1, source_target_pairs={{4,8},{8,4},{12,16},{16,12},{20,24},{24,20},{28,32},{32,28},{36,40... | collective-permute-start | bytes 245768 | tf_op jit(solution)/shard_map/ppermute | solution.py:458
  54.6 6.6 %collective-permute-start.8 = (f32[5,16,128]{2,1,0:T(8,128)S(1)}, f32[5,16,128]{2,1,0:T(8,128)S(1)}, u32[]{:S(2)}, u32[]{:S(2)}) collective-permute-start(f32[5,16,128]{2,1,0:T(8,128)S(1)} %get-tuple-element.24), channel_id=1, source_target_pairs={{0,1},{1,0},{2,3},{3,2},{4,5},{5,4},{6,7},{7,6},{8,9},{9,8},{10,11... | collective-permute-start | bytes 122888 | tf_op jit(solution)/shard_map/ppermute | solution.py:458
  59.8 1.4 %collective-permute-start.9 = (f32[5,16,128]{2,1,0:T(8,128)S(1)}, f32[5,16,128]{2,1,0:T(8,128)S(1)}, u32[]{:S(2)}, u32[]{:S(2)}) collective-permute-start(f32[5,16,128]{2,1,0:T(8,128)S(1)} %get-tuple-element.25), channel_id=1, source_target_pairs={{1,2},{2,1},{5,6},{6,5},{9,10},{10,9},{13,14},{14,13},{17,18},{18,... | collective-permute-start | bytes 122888 | tf_op jit(solution)/shard_map/ppermute | solution.py:458

commit v8 on v7

--- a/solution.py
+++ b/solution.py
@@ -321,52 +321,68 @@
     stream_pos = lax.axis_index("stream")
     get_base = pltpu.make_async_copy(base, q.at[:, 1 : cz + 1, 8:24, :], out_sems.at[0])
     get_base.start()
-    low, high = carried[0, 0:8], carried[0, 8:16]
-    for i in range(1, n_stream):
-        low = low + carried[i, 0:8]
-        high = high + carried[i, 8:16]
-    one = jnp.where(lane_ids((1, 8)) == 0, 1.0, 0.0)
-    hi, lo = split(jnp.concatenate([low, high], axis=1))
-    target[...] = (
-        bdot(plane_table[...], jnp.concatenate([hi, hi, lo], axis=1), ((1,), (1,))) + one
-    )
-    n_edge = 2 * cz + 2 * cy
-    pick = (
-        lax.broadcasted_iota(jnp.int32, (n_edge, 128), 0) == lane_ids((n_edge, 128))
-    ).astype(jnp.bfloat16)
-    pick = jnp.concatenate([pick, pick], axis=1)
-    e_low = bdot(pick, jnp.concatenate(split(low), axis=1), ((1,), (1,)))
-    e_high = bdot(pick, jnp.concatenate(split(high), axis=1), ((1,), (1,)))
     relax = relax_weights(cx)
     decay = (6.0 * viscous + relax, 6.0 * heat_diff + relax)
-    push = time_step * relax
-
-    def edge_push(f):
-        col = e_low[:, 5 + f : 6 + f] if f < 3 else e_high[:, 2 + f : 3 + f]
-        if f == 0:
-            col = col + 1.0
-        col = col * push
-        return (
-            jnp.where(span_pos > 0, col[0:cz], 0.0),
-            jnp.where(span_pos < lax.axis_size("span") - 1, col[cz : 2 * cz], 0.0),
-            jnp.where(vert_pos > 0, col[2 * cz : 2 * cz + cy], 0.0),
-            jnp.where(vert_pos < lax.axis_size("vert") - 1, col[2 * cz + cy :], 0.0),
+
+    @pl.when(stream_pos == 0)
+    def _():
+        low, high = carried[0, 0:8], carried[0, 8:16]
+        for i in range(1, n_stream):
+            low = low + carried[i, 0:8]
+            high = high + carried[i, 8:16]
+        one = jnp.where(lane_ids((1, 8)) == 0, 1.0, 0.0)
+        hi, lo = split(jnp.concatenate([low, high], axis=1))
+        target[...] = (
+            bdot(plane_table[...], jnp.concatenate([hi, hi, lo], axis=1), ((1,), (1,))) + one
         )
-
-    fill_ghosts(q, ye, yo, ze, zo, edge_push)
-    get_base.wait()
-
-    def pushing(g, carry):
-        for i in range(4):
-            z = g * 4 + i
-            t = target[pl.ds(pl.multiple_of(z * cy, cy), cy), :]
+        n_edge = 2 * cz + 2 * cy
+        pick = (
+            lax.broadcasted_iota(jnp.int32, (n_edge, 128), 0) == lane_ids((n_edge, 128))
+        ).astype(jnp.bfloat16)
+        pick = jnp.concatenate([pick, pick], axis=1)
+        e_low = bdot(pick, jnp.concatenate(split(low), axis=1), ((1,), (1,)))
+        e_high = bdot(pick, jnp.concatenate(split(high), axis=1), ((1,), (1,)))
+        push = time_step * relax
+
+        def edge_push(f):
+            col = e_low[:, 5 + f : 6 + f] if f < 3 else e_high[:, 2 + f : 3 + f]
+            if f == 0:
+                col = col + 1.0
+            col = col * push
+            return (
+                jnp.where(span_pos > 0, col[0:cz], 0.0),
+                jnp.where(span_pos < lax.axis_size("span") - 1, col[cz : 2 * cz], 0.0),
+                jnp.where(vert_pos > 0, col[2 * cz : 2 * cz + cy], 0.0),
+                jnp.where(vert_pos < lax.axis_size("vert") - 1, col[2 * cz + cy :], 0.0),
+            )
+
+        fill_ghosts(q, ye, yo, ze, zo, edge_push)
+        get_base.wait()
+
+        def pushing(g, carry):
+            for i in range(4):
+                z = g * 4 + i
+                t = target[pl.ds(pl.multiple_of(z * cy, cy), cy), :]
+                for f in range(NF):
+                    pushed = push * t[:, f : f + 1]
+                    q[f, z + 1, 8:24, :] = q[f, z + 1, 8:24, :] + pushed
+                    out[f, z] = fields[f, z] + pushed
+            return carry
+
+        lax.fori_loop(0, cz // 4, pushing, 0)
+
+    @pl.when(stream_pos > 0)
+    def _():
+        fill_ghosts(q, ye, yo, ze, zo)
+
+        def keep(z, carry):
             for f in range(NF):
-                pushed = push * t[:, f : f + 1]
-                q[f, z + 1, 8:24, :] = q[f, z + 1, 8:24, :] + pushed
-                out[f, z] = fields[f, z] + pushed
-        return carry
-
-    lax.fori_loop(0, cz // 4, pushing, 0)
+                out[f, z] = fields[f, z]
+            return carry
+
+        lax.fori_loop(0, cz, keep, 0, unroll=4)
+        get_base.wait()
+
     west_at = jnp.maximum(stream_pos - 1, 0)
     east_at = jnp.minimum(stream_pos + 1, n_stream - 1)
     west, east = [], []

time: 103 us -> 102 us (level)
    all_to_all x1, blocking collectives: 19.7 us -> 18.7 us  [on_device(): part = lax.all_to_all(part, ('stream', 'vert'), 0, 0, tiled=True)]
where the time goes in v8:
time: 102 us; the launch traced here: 101 us
  starting transfers between devices  48.9 us (48%)
  blocking collectives  32.8 us (32%)
  Pallas kernels  16 us (16%)
  waiting for transfers between devices  2.18 us (2%)
    ppermute x10, starting transfers between devices, swapped(): return lax.ppermute(block, axis, pairs)  27.9 us
    all_to_all x1, blocking collectives, on_device(): part = lax.all_to_all(part, ('stream', 'vert'), 0, 0, tiled=True)  18.7 us
    all_to_all x1, starting transfers between devices, on_device(): lax.all_to_all(sent.reshape(tiles, ROWS, 128), ('span', 'vert'), 0, 0, ti...  15 us
    all_to_all x1, blocking collectives, on_device(): part = lax.all_to_all(modal, 'span', 0, 0, tiled=True)  14.1 us
    pallas_call x1, Pallas kernels, on_device(): pl.pallas_call(second_step, out_shape=(f32(NF, cz, cy, cx), f32(n_span, 1...  6.73 us
    all_to_all x1, starting transfers between devices, on_device(): carried = lax.all_to_all(carry, 'stream', 0, 0, tiled=True)  6.02 us
    pallas_call x1, Pallas kernels, on_device(): pl.pallas_call(first_step, out_shape=(f32(NF, cz, cy, cx),) + leaving, in...  5.63 us
    pallas_call x1, Pallas kernels, on_device(): pl.pallas_call(sum_panels, out_shape=f32(tiles * ROWS, 128), in_specs=[HB...  2.59 us
  transfers between devices with their start and end apart: 12, of which 2 were waited for; matrix products, arithmetic and copies ran while one was open for 0% of the time, Pallas kernels for 1%

profile of v8, /device:TPU:1, one launch (start us, length us, event | category | flops | bytes accessed | tf_op | source)
XLA Modules:
  0.0 101.4 jit_solution(8982503552627034162)
XLA Ops:
  0.6 0.0 copy-start
  0.6 2.6 %panel_sums.1 = f32[1024,128]{1,0:T(8,128)} custom-call(f32[5,64,256]{2,1,0:T(8,128)} %bitcast.18, s32[1,64]{1,0:T(1,128)} %bitcast.20, f32[64,256]{1,0:T(8,128)} %constant.8.clone.turn_h, bf16[768,128]{1,0:T(8,128)(2,1)} %constant.9.clone.edge_h), custom_call_target="tpu_custom_call" | custom-call | tf_op jit(solution)/shard_map/panel_sums/pallas_call | solution.py:493
  3.2 0.0 copy-start.1
  3.2 15.0 %all-to-all-start = ((f32[64,16,128]{2,1,0:T(8,128)}), f32[64,16,128]{2,1,0:T(8,128)S(1)}, u32[]{:S(2)}, u32[]{:S(2)}) async-start(f32[64,16,128]{2,1,0:T(8,128)} %bitcast.17), calls=%async_computation | async-start | bytes 1048576 | tf_op jit(solution)/shard_map/all_to_all | solution.py:502
  18.2 1.0 pack_faces.1
  19.3 2.4 %collective-permute-start.2 = (f32[5,32,128]{2,1,0:T(8,128)S(1)}, f32[5,32,128]{2,1,0:T(8,128)S(1)}, u32[]{:S(2)}, u32[]{:S(2)}) collective-permute-start(f32[5,32,128]{2,1,0:T(8,128)S(1)} %get-tuple-element.16), channel_id=1, source_target_pairs={{0,4},{4,0},{8,12},{12,8},{16,20},{20,16},{24,28},{28,24},{32,36},... | collective-permute-start | bytes 245768 | tf_op jit(solution)/shard_map/ppermute | solution.py:474
  21.6 3.2 %collective-permute-start.3 = (f32[5,32,128]{2,1,0:T(8,128)S(1)}, f32[5,32,128]{2,1,0:T(8,128)S(1)}, u32[]{:S(2)}, u32[]{:S(2)}) collective-permute-start(f32[5,32,128]{2,1,0:T(8,128)S(1)} %get-tuple-element.17), channel_id=1, source_target_pairs={{4,8},{8,4},{12,16},{16,12},{20,24},{24,20},{28,32},{32,28},{36,40... | collective-permute-start | bytes 245768 | tf_op jit(solution)/shard_map/ppermute | solution.py:474
  24.9 0.7 collective-permute-start.1
  25.6 3.1 %collective-permute-start.4 = (f32[5,16,128]{2,1,0:T(8,128)S(1)}, f32[5,16,128]{2,1,0:T(8,128)S(1)}, u32[]{:S(2)}, u32[]{:S(2)}) collective-permute-start(f32[5,16,128]{2,1,0:T(8,128)S(1)} %get-tuple-element.18), channel_id=1, source_target_pairs={{0,1},{1,0},{2,3},{3,2},{4,5},{5,4},{6,7},{7,6},{8,9},{9,8},{10,11... | collective-permute-start | bytes 122888 | tf_op jit(solution)/shard_map/ppermute | solution.py:474
  28.7 0.7 collective-permute-start.5
  29.3 0.0 collective-permute-done.1.refs_4_
  29.3 5.7 %collective-permute-start = (f32[5,8,128]{2,1,0:T(8,128)S(1)}, f32[5,8,128]{2,1,0:T(8,128)S(1)}, u32[]{:S(2)}, u32[]{:S(2)}) collective-permute-start(f32[5,8,128]{2,1,0:T(8,128)S(1)} %get-tuple-element.15), channel_id=1, source_target_pairs={{0,64},{64,0},{128,192},{192,128},{256,320},{320,256},{384,448},{4... | collective-permute-start | bytes 61448 | tf_op jit(solution)/shard_map/ppermute | solution.py:474
  35.1 1.5 %collective-permute-done.refs_3_ = f32[5,8,128]{2,1,0:T(8,128)S(1)} collective-permute-done((f32[5,8,128]{2,1,0:T(8,128)S(1)}, f32[5,8,128]{2,1,0:T(8,128)S(1)}, u32[]{:S(2)}, u32[]{:S(2)}) %collective-permute-start) | collective-permute-done | bytes 20512 | tf_op jit(solution)/shard_map/ppermute | solution.py:474
  36.5 0.0 collective-permute-done.4.refs_7_
  36.5 0.0 collective-permute-done.5.refs_8_
  36.6 0.0 all-to-all-done
  36.6 0.0 copy-start.2
  36.6 0.0 copy-start.3
  36.6 0.0 copy-start.4
  36.6 0.0 copy-start.5
  36.6 0.0 copy-start.6
  36.6 5.6 %first_step.1 = (f32[5,32,16,128]{3,2,1,0:T(8,128)}, f32[8,56,128]{2,1,0:T(8,128)}, f32[5,32,128]{2,1,0:T(8,128)S(1)}, f32[5,32,128]{2,1,0:T(8,128)S(1)}, f32[5,...) custom-call(f32[5,32,16,128]{3,2,1,0:T(8,128)} %refs_0_.3, f32[32,16,128]{2,1,0:T(8,128)S(1)} %copy-done.1, ...), custom_call_target="tpu_custom_call" | custom-call | tf_op jit(solution)/shard_map/first_step/pallas_call | solution.py:527
  42.3 6.0 %all-to-all-start.1 = ((f32[8,56,128]{2,1,0:T(8,128)}), f32[8,56,128]{2,1,0:T(8,128)S(1)}, u32[]{:S(2)}, u32[]{:S(2)}) async-start(f32[8,56,128]{2,1,0:T(8,128)} %get-tuple-element.21), calls=%async_computation.1 | async-start | bytes 458752 | tf_op jit(solution)/shard_map/all_to_all | solution.py:542
  48.3 3.7 %collective-permute-start.6 = (f32[5,32,128]{2,1,0:T(8,128)S(1)}, f32[5,32,128]{2,1,0:T(8,128)S(1)}, u32[]{:S(2)}, u32[]{:S(2)}) collective-permute-start(f32[5,32,128]{2,1,0:T(8,128)S(1)} %get-tuple-element.22), channel_id=1, source_target_pairs={{0,4},{4,0},{8,12},{12,8},{16,20},{20,16},{24,28},{28,24},{32,36},... | collective-permute-start | bytes 245768 | tf_op jit(solution)/shard_map/ppermute | solution.py:474
  52.0 2.5 %collective-permute-start.7 = (f32[5,32,128]{2,1,0:T(8,128)S(1)}, f32[5,32,128]{2,1,0:T(8,128)S(1)}, u32[]{:S(2)}, u32[]{:S(2)}) collective-permute-start(f32[5,32,128]{2,1,0:T(8,128)S(1)} %get-tuple-element.23), channel_id=1, source_target_pairs={{4,8},{8,4},{12,16},{16,12},{20,24},{24,20},{28,32},{32,28},{36,40... | collective-permute-start | bytes 245768 | tf_op jit(solution)/shard_map/ppermute | solution.py:474
  54.6 5.3 %collective-permute-start.8 = (f32[5,16,128]{2,1,0:T(8,128)S(1)}, f32[5,16,128]{2,1,0:T(8,128)S(1)}, u32[]{:S(2)}, u32[]{:S(2)}) collective-permute-start(f32[5,16,128]{2,1,0:T(8,128)S(1)} %get-tuple-element.24), channel_id=1, source_target_pairs={{0,1},{1,0},{2,3},{3,2},{4,5},{5,4},{6,7},{7,6},{8,9},{9,8},{10,11... | collective-permute-start | bytes 122888 | tf_op jit(solution)/shard_map/ppermute | solution.py:474
  59.8 0.7 collective-permute-start.9
  60.5 0.7 collective-permute-done.8.refs_7_
  61.3 6.7 %second_step.1 = (f32[5,32,16,128]{3,2,1,0:T(8,128)}, f32[16,128]{1,0:T(8,128)S(1)}) custom-call(f32[5,32,16,128]{3,2,1,0:T(8,128)} %refs_0_.3, f32[32,16,128]{2,1,0:T(8,128)S(1)} %copy-done.1, f32[5,32,16,128]{3,2,1,0:T(8,128)} %get-tuple-element.20.refs_2_, bf16[512,768]{1,0:T(8,128)(2,1)S(1)} %copy-done.2, f32[8,56,128]{2,1,0:T(8,128)S(1)} %all-to-all-done.1.refs_4_, ...), custom_call_target="tpu_custom_call" | custom-call | tf_op jit(solution)/shard_map/second_step/pallas_call | solution.py:548
  68.0 14.1 %all_to_all.25 = f32[16,1,128]{2,1,0:T(1,128)S(1)} all-to-all(f32[16,1,128]{2,1,0:T(1,128)S(1)} %bitcast.16), channel_id=1, replica_groups=mesh['stream'=8,'span'=16,'vert'=4] {'span'}, dimensions={0} | all-to-all | bytes 16384 | tf_op jit(solution)/shard_map/all_to_all | solution.py:570
  82.2 18.7 %all_to_all.26 = f32[32,1,128]{2,1,0:T(1,128)S(1)} all-to-all(f32[32,1,128]{2,1,0:T(1,128)S(1)} %broadcast_in_dim.2), channel_id=1, replica_groups=mesh['stream'=8,'span'=16,'vert'=4] {'stream','vert'}, dimensions={0} | all-to-all | bytes 32768 | tf_op jit(solution)/shard_map/all_to_all | solution.py:572
  100.8 0.5 reduce_sum.19
  (15 shorter events, 0.1 us)
Async XLA Ops:
  0.6 17.6 %copy-start = (f32[5,32,16,128]{3,2,1,0:T(8,128)S(1)}, f32[5,32,16,128]{3,2,1,0:T(8,128)}, u32[]{:S(2)}) copy-start(f32[5,32,16,128]{3,2,1,0:T(8,128)} %refs_0_.3) | copy-start | bytes 3932164
  3.2 33.3 %copy-start.1 = (f32[32,16,128]{2,1,0:T(8,128)S(1)}, f32[32,16,128]{2,1,0:T(8,128)}, u32[]{:S(2)}) copy-start(f32[32,16,128]{2,1,0:T(8,128)} %refs_1_.3) | copy-start | bytes 786436
  3.2 33.3 %all-to-all-start = ((f32[64,16,128]{2,1,0:T(8,128)}), f32[64,16,128]{2,1,0:T(8,128)S(1)}, u32[]{:S(2)}, u32[]{:S(2)}) async-start(f32[64,16,128]{2,1,0:T(8,128)} %bitcast.17), calls=%async_computation | async-start | bytes 1048576 | tf_op jit(solution)/shard_map/all_to_all | solution.py:502
  19.3 17.3 %collective-permute-start.2 = (f32[5,32,128]{2,1,0:T(8,128)S(1)}, f32[5,32,128]{2,1,0:T(8,128)S(1)}, u32[]{:S(2)}, u32[]{:S(2)}) collective-permute-start(f32[5,32,128]{2,1,0:T(8,128)S(1)} %get-tuple-element.16), channel_id=1, source_target_pairs={{0,4},{4,0},{8,12},{12,8},{16,20},{20,16},{24,28},{28,24},{32,36},... | collective-permute-start | bytes 245768 | tf_op jit(solution)/shard_map/ppermute | solution.py:474
  21.6 14.9 %collective-permute-start.3 = (f32[5,32,128]{2,1,0:T(8,128)S(1)}, f32[5,32,128]{2,1,0:T(8,128)S(1)}, u32[]{:S(2)}, u32[]{:S(2)}) collective-permute-start(f32[5,32,128]{2,1,0:T(8,128)S(1)} %get-tuple-element.17), channel_id=1, source_target_pairs={{4,8},{8,4},{12,16},{16,12},{20,24},{24,20},{28,32},{32,28},{36,40... | collective-permute-start | bytes 245768 | tf_op jit(solution)/shard_map/ppermute | solution.py:474
  24.9 4.4 %collective-permute-start.1 = (f32[5,8,128]{2,1,0:T(8,128)S(1)}, f32[5,8,128]{2,1,0:T(8,128)S(1)}, u32[]{:S(2)}, u32[]{:S(2)}) collective-permute-start(f32[5,8,128]{2,1,0:T(8,128)S(1)} %get-tuple-element.15), channel_id=1, source_target_pairs={{64,128},{128,64},{192,256},{256,192},{320,384},{384,320},{65,129}... | collective-permute-start | bytes 61448 | tf_op jit(solution)/shard_map/ppermute | solution.py:474
  25.6 11.0 %collective-permute-start.4 = (f32[5,16,128]{2,1,0:T(8,128)S(1)}, f32[5,16,128]{2,1,0:T(8,128)S(1)}, u32[]{:S(2)}, u32[]{:S(2)}) collective-permute-start(f32[5,16,128]{2,1,0:T(8,128)S(1)} %get-tuple-element.18), channel_id=1, source_target_pairs={{0,1},{1,0},{2,3},{3,2},{4,5},{5,4},{6,7},{7,6},{8,9},{9,8},{10,11... | collective-permute-start | bytes 122888 | tf_op jit(solution)/shard_map/ppermute | solution.py:474
  28.7 7.9 %collective-permute-start.5 = (f32[5,16,128]{2,1,0:T(8,128)S(1)}, f32[5,16,128]{2,1,0:T(8,128)S(1)}, u32[]{:S(2)}, u32[]{:S(2)}) collective-permute-start(f32[5,16,128]{2,1,0:T(8,128)S(1)} %get-tuple-element.19), channel_id=1, source_target_pairs={{1,2},{2,1},{5,6},{6,5},{9,10},{10,9},{13,14},{14,13},{17,18},{18,... | collective-permute-start | bytes 122888 | tf_op jit(solution)/shard_map/ppermute | solution.py:474
  29.3 7.2 %collective-permute-start = (f32[5,8,128]{2,1,0:T(8,128)S(1)}, f32[5,8,128]{2,1,0:T(8,128)S(1)}, u32[]{:S(2)}, u32[]{:S(2)}) collective-permute-start(f32[5,8,128]{2,1,0:T(8,128)S(1)} %get-tuple-element.15), channel_id=1, source_target_pairs={{0,64},{64,0},{128,192},{192,128},{256,320},{320,256},{384,448},{4... | collective-permute-start | bytes 61448 | tf_op jit(solution)/shard_map/ppermute | solution.py:474
  36.6 24.6 %copy-start.2 = (bf16[512,768]{1,0:T(8,128)(2,1)S(1)}, bf16[512,768]{1,0:T(8,128)(2,1)}, u32[]{:S(2)}) copy-start(bf16[512,768]{1,0:T(8,128)(2,1)} %constant.10.clone.refs_3_) | copy-start | bytes 2359300
  36.6 24.6 %copy-start.3 = (f32[1,16,1,3,2048]{4,2,3,1,0:T(1,128)S(1)}, f32[1,16,1,3,2048]{4,2,3,1,0:T(1,128)}, u32[]{:S(2)}) copy-start(f32[1,16,1,3,2048]{4,2,3,1,0:T(1,128)} %param.16) | copy-start | bytes 1179652
  36.6 24.6 %copy-start.4 = (s32[1,16,1,2048]{3,2,1,0:T(1,128)S(1)}, s32[1,16,1,2048]{3,2,1,0:T(1,128)}, u32[]{:S(2)}) copy-start(s32[1,16,1,2048]{3,2,1,0:T(1,128)} %refs_11_.1) | copy-start | bytes 393220
  36.6 24.6 %copy-start.5 = (f32[3,64,32]{1,2,0:T(8,128)S(1)}, f32[3,64,32]{1,2,0:T(8,128)}, u32[]{:S(2)}) copy-start(f32[3,64,32]{1,2,0:T(8,128)} %param.18) | copy-start | bytes 73732
  36.6 24.6 %copy-start.6 = (s32[1,1,1,2048]{3,2,1,0:T(1,128)S(1)}, s32[1,1,1,2048]{3,2,1,0:T(1,128)}, u32[]{:S(2)}) copy-start(s32[1,1,1,2048]{3,2,1,0:T(1,128)} %param.15) | copy-start | bytes 24580
  42.3 18.9 %all-to-all-start.1 = ((f32[8,56,128]{2,1,0:T(8,128)}), f32[8,56,128]{2,1,0:T(8,128)S(1)}, u32[]{:S(2)}, u32[]{:S(2)}) async-start(f32[8,56,128]{2,1,0:T(8,128)} %get-tuple-element.21), calls=%async_computation.1 | async-start | bytes 458752 | tf_op jit(solution)/shard_map/all_to_all | solution.py:542
  48.3 12.9 %collective-permute-start.6 = (f32[5,32,128]{2,1,0:T(8,128)S(1)}, f32[5,32,128]{2,1,0:T(8,128)S(1)}, u32[]{:S(2)}, u32[]{:S(2)}) collective-permute-start(f32[5,32,128]{2,1,0:T(8,128)S(1)} %get-tuple-element.22), channel_id=1, source_target_pairs={{0,4},{4,0},{8,12},{12,8},{16,20},{20,16},{24,28},{28,24},{32,36},... | collective-permute-start | bytes 245768 | tf_op jit(solution)/shard_map/ppermute | solution.py:474
  52.0 9.2 %collective-permute-start.7 = (f32[5,32,128]{2,1,0:T(8,128)S(1)}, f32[5,32,128]{2,1,0:T(8,128)S(1)}, u32[]{:S(2)}, u32[]{:S(2)}) collective-permute-start(f32[5,32,128]{2,1,0:T(8,128)S(1)} %get-tuple-element.23), channel_id=1, source_target_pairs={{4,8},{8,4},{12,16},{16,12},{20,24},{24,20},{28,32},{32,28},{36,40... | collective-permute-start | bytes 245768 | tf_op jit(solution)/shard_map/ppermute | solution.py:474
  54.6 6.6 %collective-permute-start.8 = (f32[5,16,128]{2,1,0:T(8,128)S(1)}, f32[5,16,128]{2,1,0:T(8,128)S(1)}, u32[]{:S(2)}, u32[]{:S(2)}) collective-permute-start(f32[5,16,128]{2,1,0:T(8,128)S(1)} %get-tuple-element.24), channel_id=1, source_target_pairs={{0,1},{1,0},{2,3},{3,2},{4,5},{5,4},{6,7},{7,6},{8,9},{9,8},{10,11... | collective-permute-start | bytes 122888 | tf_op jit(solution)/shard_map/ppermute | solution.py:474
  59.8 1.4 %collective-permute-start.9 = (f32[5,16,128]{2,1,0:T(8,128)S(1)}, f32[5,16,128]{2,1,0:T(8,128)S(1)}, u32[]{:S(2)}, u32[]{:S(2)}) collective-permute-start(f32[5,16,128]{2,1,0:T(8,128)S(1)} %get-tuple-element.25), channel_id=1, source_target_pairs={{1,2},{2,1},{5,6},{6,5},{9,10},{10,9},{13,14},{14,13},{17,18},{18,... | collective-permute-start | bytes 122888 | tf_op jit(solution)/shard_map/ppermute | solution.py:474

commit v9 on v8

--- a/solution.py
+++ b/solution.py
@@ -137,6 +137,7 @@
 
 
 INNER = 8
+WIDE = 16
 
 
 def packed_x(acc, v, zi):
@@ -147,8 +148,8 @@
     return acc
 
 
-def placed(whole, part, zo):
-    width = 4 * INNER
+def placed(whole, part, zo, inner):
+    width = 4 * inner
     lane = lane_ids((8, 128))
     return jnp.where(lane // width == zo, pltpu.roll(part, zo * width, 1), whole)
 
@@ -177,12 +178,12 @@
         new = []
         for f in range(NF):
             part = zero
-            for i in range(INNER):
-                part = packed_x(part, fields[f, g * INNER + i], i)
-            new.append(placed(accs[f], part, g))
+            for i in range(WIDE):
+                part = packed_x(part, fields[f, g * WIDE + i], i)
+            new.append(placed(accs[f], part, g, WIDE))
         return tuple(new)
 
-    accs = lax.fori_loop(0, cz // INNER, body, (zero,) * NF)
+    accs = lax.fori_loop(0, cz // WIDE, body, (zero,) * NF)
     for f in range(NF):
         xf[f] = accs[f]
     store_faces(fields, ye, yo, ze, zo)
@@ -296,7 +297,7 @@
                 parts[f] = packed_x(parts[f], b, i)
         chunk = pl.ds(pl.multiple_of(g * INNER, INNER), INNER)
         pltpu.make_async_copy(base.at[:, chunk], base_out.at[:, chunk], base_sems.at[g]).start()
-        return tuple(placed(accs[f], parts[f], g) for f in range(NF))
+        return tuple(placed(accs[f], parts[f], g, INNER) for f in range(NF))
 
     accs = lax.fori_loop(0, cz // INNER, body, (zero,) * NF)
     for f in range(NF):
@@ -393,18 +394,18 @@
     xg = ghosts_x(west, east)
 
     def body(g, carry):
-        turned = [pltpu.roll(xg[f], (128 - 4 * INNER * g) & 127, 1) for f in range(NF)]
-        for i in range(INNER):
-            z = g * INNER + i
+        turned = [pltpu.roll(xg[f], (128 - 4 * WIDE * g) & 127, 1) for f in range(NF)]
+        for i in range(WIDE):
+            z = g * WIDE + i
             damp2 = solid[z] * (2.0 / penalty)
             cs, rs = slab_rates(q, turned, damp2, decay, z, i)
             for f in range(NF):
                 out[f, z] = 0.5 * (out[f, z] + cs[f] + time_step * rs[f])
-        chunk = pl.ds(pl.multiple_of(g * INNER, INNER), INNER)
+        chunk = pl.ds(pl.multiple_of(g * WIDE, WIDE), WIDE)
         pltpu.make_async_copy(out.at[:, chunk], out_h.at[:, chunk], out_sems.at[g + 1]).start()
         return carry
 
-    lax.fori_loop(0, cz // INNER, body, 0)
+    lax.fori_loop(0, cz // WIDE, body, 0)
 
     pressure = jnp.transpose(jnp.reshape(out[3], (cz * cy, cx)))
     p_hi = pressure.astype(jnp.bfloat16)
@@ -446,8 +447,8 @@
         [total, jnp.zeros((1, 128 - shapes.shape[1]), jnp.float32)], axis=1
     )
     modal[...] = jnp.broadcast_to(total, modal.shape)
-    for g in range(cz // INNER):
-        chunk = pl.ds(g * INNER, INNER)
+    for g in range(cz // WIDE):
+        chunk = pl.ds(g * WIDE, WIDE)
         pltpu.make_async_copy(out.at[:, chunk], out_h.at[:, chunk], out_sems.at[g + 1]).wait()
 
 

time: 102 us -> 102 us (level)
  no operation moved by 1% of the time
where the time goes in v9:
time: 102 us; the launch traced here: 101 us
  starting transfers between devices  48.9 us (48%)
  blocking collectives  32.8 us (32%)
  Pallas kernels  15.6 us (15%)
  waiting for transfers between devices  2.18 us (2%)
    ppermute x10, starting transfers between devices, swapped(): return lax.ppermute(block, axis, pairs)  27.9 us
    all_to_all x1, blocking collectives, on_device(): part = lax.all_to_all(part, ('stream', 'vert'), 0, 0, tiled=True)  18.7 us
    all_to_all x1, starting transfers between devices, on_device(): lax.all_to_all(sent.reshape(tiles, ROWS, 128), ('span', 'vert'), 0, 0, ti...  15 us
    all_to_all x1, blocking collectives, on_device(): part = lax.all_to_all(modal, 'span', 0, 0, tiled=True)  14.1 us
    pallas_call x1, Pallas kernels, on_device(): pl.pallas_call(second_step, out_shape=(f32(NF, cz, cy, cx), f32(n_span, 1...  6.55 us
    all_to_all x1, starting transfers between devices, on_device(): carried = lax.all_to_all(carry, 'stream', 0, 0, tiled=True)  6.02 us
    pallas_call x1, Pallas kernels, on_device(): pl.pallas_call(first_step, out_shape=(f32(NF, cz, cy, cx),) + leaving, in...  5.63 us
    pallas_call x1, Pallas kernels, on_device(): pl.pallas_call(sum_panels, out_shape=f32(tiles * ROWS, 128), in_specs=[HB...  2.59 us
  transfers between devices with their start and end apart: 12, of which 2 were waited for; matrix products, arithmetic and copies ran while one was open for 0% of the time, Pallas kernels for 1%

profile of v9, /device:TPU:1, one launch (start us, length us, event | category | flops | bytes accessed | tf_op | source)
XLA Modules:
  0.0 101.0 jit_solution(14208366674815490389)
XLA Ops:
  0.6 0.0 copy-start
  0.6 2.6 %panel_sums.1 = f32[1024,128]{1,0:T(8,128)} custom-call(f32[5,64,256]{2,1,0:T(8,128)} %bitcast.18, s32[1,64]{1,0:T(1,128)} %bitcast.20, f32[64,256]{1,0:T(8,128)} %constant.8.clone.turn_h, bf16[768,128]{1,0:T(8,128)(2,1)} %constant.9.clone.edge_h), custom_call_target="tpu_custom_call" | custom-call | tf_op jit(solution)/shard_map/panel_sums/pallas_call | solution.py:494
  3.2 0.0 copy-start.1
  3.2 15.0 %all-to-all-start = ((f32[64,16,128]{2,1,0:T(8,128)}), f32[64,16,128]{2,1,0:T(8,128)S(1)}, u32[]{:S(2)}, u32[]{:S(2)}) async-start(f32[64,16,128]{2,1,0:T(8,128)} %bitcast.17), calls=%async_computation | async-start | bytes 1048576 | tf_op jit(solution)/shard_map/all_to_all | solution.py:503
  18.2 0.8 pack_faces.1
  19.1 2.4 %collective-permute-start.2 = (f32[5,32,128]{2,1,0:T(8,128)S(1)}, f32[5,32,128]{2,1,0:T(8,128)S(1)}, u32[]{:S(2)}, u32[]{:S(2)}) collective-permute-start(f32[5,32,128]{2,1,0:T(8,128)S(1)} %get-tuple-element.16), channel_id=1, source_target_pairs={{0,4},{4,0},{8,12},{12,8},{16,20},{20,16},{24,28},{28,24},{32,36},... | collective-permute-start | bytes 245768 | tf_op jit(solution)/shard_map/ppermute | solution.py:475
  21.5 3.2 %collective-permute-start.3 = (f32[5,32,128]{2,1,0:T(8,128)S(1)}, f32[5,32,128]{2,1,0:T(8,128)S(1)}, u32[]{:S(2)}, u32[]{:S(2)}) collective-permute-start(f32[5,32,128]{2,1,0:T(8,128)S(1)} %get-tuple-element.17), channel_id=1, source_target_pairs={{4,8},{8,4},{12,16},{16,12},{20,24},{24,20},{28,32},{32,28},{36,40... | collective-permute-start | bytes 245768 | tf_op jit(solution)/shard_map/ppermute | solution.py:475
  24.7 0.7 collective-permute-start.1
  25.4 3.1 %collective-permute-start.4 = (f32[5,16,128]{2,1,0:T(8,128)S(1)}, f32[5,16,128]{2,1,0:T(8,128)S(1)}, u32[]{:S(2)}, u32[]{:S(2)}) collective-permute-start(f32[5,16,128]{2,1,0:T(8,128)S(1)} %get-tuple-element.18), channel_id=1, source_target_pairs={{0,1},{1,0},{2,3},{3,2},{4,5},{5,4},{6,7},{7,6},{8,9},{9,8},{10,11... | collective-permute-start | bytes 122888 | tf_op jit(solution)/shard_map/ppermute | solution.py:475
  28.5 0.7 collective-permute-start.5
  29.2 0.0 collective-permute-done.1.refs_4_
  29.2 5.7 %collective-permute-start = (f32[5,8,128]{2,1,0:T(8,128)S(1)}, f32[5,8,128]{2,1,0:T(8,128)S(1)}, u32[]{:S(2)}, u32[]{:S(2)}) collective-permute-start(f32[5,8,128]{2,1,0:T(8,128)S(1)} %get-tuple-element.15), channel_id=1, source_target_pairs={{0,64},{64,0},{128,192},{192,128},{256,320},{320,256},{384,448},{4... | collective-permute-start | bytes 61448 | tf_op jit(solution)/shard_map/ppermute | solution.py:475
  34.9 1.5 %collective-permute-done.refs_3_ = f32[5,8,128]{2,1,0:T(8,128)S(1)} collective-permute-done((f32[5,8,128]{2,1,0:T(8,128)S(1)}, f32[5,8,128]{2,1,0:T(8,128)S(1)}, u32[]{:S(2)}, u32[]{:S(2)}) %collective-permute-start) | collective-permute-done | bytes 20512 | tf_op jit(solution)/shard_map/ppermute | solution.py:475
  36.4 0.0 collective-permute-done.4.refs_7_
  36.4 0.0 collective-permute-done.5.refs_8_
  36.4 0.0 collective-permute-done.2.refs_5_
  36.4 0.0 copy-start.2
  36.4 0.0 copy-start.3
  36.4 0.0 copy-start.4
  36.5 0.0 copy-start.5
  36.5 0.0 copy-start.6
  36.5 5.6 %first_step.1 = (f32[5,32,16,128]{3,2,1,0:T(8,128)}, f32[8,56,128]{2,1,0:T(8,128)}, f32[5,32,128]{2,1,0:T(8,128)S(1)}, f32[5,32,128]{2,1,0:T(8,128)S(1)}, f32[5,...) custom-call(f32[5,32,16,128]{3,2,1,0:T(8,128)} %refs_0_.3, f32[32,16,128]{2,1,0:T(8,128)S(1)} %copy-done.1, ...), custom_call_target="tpu_custom_call" | custom-call | tf_op jit(solution)/shard_map/first_step/pallas_call | solution.py:528
  42.1 6.0 %all-to-all-start.1 = ((f32[8,56,128]{2,1,0:T(8,128)}), f32[8,56,128]{2,1,0:T(8,128)S(1)}, u32[]{:S(2)}, u32[]{:S(2)}) async-start(f32[8,56,128]{2,1,0:T(8,128)} %get-tuple-element.21), calls=%async_computation.1 | async-start | bytes 458752 | tf_op jit(solution)/shard_map/all_to_all | solution.py:543
  48.1 3.9 %collective-permute-start.6 = (f32[5,32,128]{2,1,0:T(8,128)S(1)}, f32[5,32,128]{2,1,0:T(8,128)S(1)}, u32[]{:S(2)}, u32[]{:S(2)}) collective-permute-start(f32[5,32,128]{2,1,0:T(8,128)S(1)} %get-tuple-element.22), channel_id=1, source_target_pairs={{0,4},{4,0},{8,12},{12,8},{16,20},{20,16},{24,28},{28,24},{32,36},... | collective-permute-start | bytes 245768 | tf_op jit(solution)/shard_map/ppermute | solution.py:475
  52.0 2.4 %collective-permute-start.7 = (f32[5,32,128]{2,1,0:T(8,128)S(1)}, f32[5,32,128]{2,1,0:T(8,128)S(1)}, u32[]{:S(2)}, u32[]{:S(2)}) collective-permute-start(f32[5,32,128]{2,1,0:T(8,128)S(1)} %get-tuple-element.23), channel_id=1, source_target_pairs={{4,8},{8,4},{12,16},{16,12},{20,24},{24,20},{28,32},{32,28},{36,40... | collective-permute-start | bytes 245768 | tf_op jit(solution)/shard_map/ppermute | solution.py:475
  54.4 5.3 %collective-permute-start.8 = (f32[5,16,128]{2,1,0:T(8,128)S(1)}, f32[5,16,128]{2,1,0:T(8,128)S(1)}, u32[]{:S(2)}, u32[]{:S(2)}) collective-permute-start(f32[5,16,128]{2,1,0:T(8,128)S(1)} %get-tuple-element.24), channel_id=1, source_target_pairs={{0,1},{1,0},{2,3},{3,2},{4,5},{5,4},{6,7},{7,6},{8,9},{9,8},{10,11... | collective-permute-start | bytes 122888 | tf_op jit(solution)/shard_map/ppermute | solution.py:475
  59.7 0.7 collective-permute-start.9
  60.3 0.7 collective-permute-done.8.refs_7_
  61.1 6.5 %second_step.1 = (f32[5,32,16,128]{3,2,1,0:T(8,128)}, f32[16,128]{1,0:T(8,128)S(1)}) custom-call(f32[5,32,16,128]{3,2,1,0:T(8,128)} %refs_0_.3, f32[32,16,128]{2,1,0:T(8,128)S(1)} %copy-done.1, f32[5,32,16,128]{3,2,1,0:T(8,128)} %get-tuple-element.20.refs_2_, bf16[512,768]{1,0:T(8,128)(2,1)S(1)} %copy-done.2, f32[8,56,128]{2,1,0:T(8,128)S(1)} %all-to-all-done.1.refs_4_, ...), custom_call_target="tpu_custom_call" | custom-call | tf_op jit(solution)/shard_map/second_step/pallas_call | solution.py:549
  67.7 14.1 %all_to_all.25 = f32[16,1,128]{2,1,0:T(1,128)S(1)} all-to-all(f32[16,1,128]{2,1,0:T(1,128)S(1)} %bitcast.16), channel_id=1, replica_groups=mesh['stream'=8,'span'=16,'vert'=4] {'span'}, dimensions={0} | all-to-all | bytes 16384 | tf_op jit(solution)/shard_map/all_to_all | solution.py:571
  81.8 18.7 %all_to_all.26 = f32[32,1,128]{2,1,0:T(1,128)S(1)} all-to-all(f32[32,1,128]{2,1,0:T(1,128)S(1)} %broadcast_in_dim.2), channel_id=1, replica_groups=mesh['stream'=8,'span'=16,'vert'=4] {'stream','vert'}, dimensions={0} | all-to-all | bytes 32768 | tf_op jit(solution)/shard_map/all_to_all | solution.py:573
  100.5 0.5 reduce_sum.19
  (15 shorter events, 0.1 us)
Async XLA Ops:
  0.6 17.6 %copy-start = (f32[5,32,16,128]{3,2,1,0:T(8,128)S(1)}, f32[5,32,16,128]{3,2,1,0:T(8,128)}, u32[]{:S(2)}) copy-start(f32[5,32,16,128]{3,2,1,0:T(8,128)} %refs_0_.3) | copy-start | bytes 3932164
  3.2 33.2 %copy-start.1 = (f32[32,16,128]{2,1,0:T(8,128)S(1)}, f32[32,16,128]{2,1,0:T(8,128)}, u32[]{:S(2)}) copy-start(f32[32,16,128]{2,1,0:T(8,128)} %refs_1_.3) | copy-start | bytes 786436
  3.2 33.1 %all-to-all-start = ((f32[64,16,128]{2,1,0:T(8,128)}), f32[64,16,128]{2,1,0:T(8,128)S(1)}, u32[]{:S(2)}, u32[]{:S(2)}) async-start(f32[64,16,128]{2,1,0:T(8,128)} %bitcast.17), calls=%async_computation | async-start | bytes 1048576 | tf_op jit(solution)/shard_map/all_to_all | solution.py:503
  19.1 17.3 %collective-permute-start.2 = (f32[5,32,128]{2,1,0:T(8,128)S(1)}, f32[5,32,128]{2,1,0:T(8,128)S(1)}, u32[]{:S(2)}, u32[]{:S(2)}) collective-permute-start(f32[5,32,128]{2,1,0:T(8,128)S(1)} %get-tuple-element.16), channel_id=1, source_target_pairs={{0,4},{4,0},{8,12},{12,8},{16,20},{20,16},{24,28},{28,24},{32,36},... | collective-permute-start | bytes 245768 | tf_op jit(solution)/shard_map/ppermute | solution.py:475
  21.5 14.9 %collective-permute-start.3 = (f32[5,32,128]{2,1,0:T(8,128)S(1)}, f32[5,32,128]{2,1,0:T(8,128)S(1)}, u32[]{:S(2)}, u32[]{:S(2)}) collective-permute-start(f32[5,32,128]{2,1,0:T(8,128)S(1)} %get-tuple-element.17), channel_id=1, source_target_pairs={{4,8},{8,4},{12,16},{16,12},{20,24},{24,20},{28,32},{32,28},{36,40... | collective-permute-start | bytes 245768 | tf_op jit(solution)/shard_map/ppermute | solution.py:475
  24.7 4.4 %collective-permute-start.1 = (f32[5,8,128]{2,1,0:T(8,128)S(1)}, f32[5,8,128]{2,1,0:T(8,128)S(1)}, u32[]{:S(2)}, u32[]{:S(2)}) collective-permute-start(f32[5,8,128]{2,1,0:T(8,128)S(1)} %get-tuple-element.15), channel_id=1, source_target_pairs={{64,128},{128,64},{192,256},{256,192},{320,384},{384,320},{65,129}... | collective-permute-start | bytes 61448 | tf_op jit(solution)/shard_map/ppermute | solution.py:475
  25.4 11.0 %collective-permute-start.4 = (f32[5,16,128]{2,1,0:T(8,128)S(1)}, f32[5,16,128]{2,1,0:T(8,128)S(1)}, u32[]{:S(2)}, u32[]{:S(2)}) collective-permute-start(f32[5,16,128]{2,1,0:T(8,128)S(1)} %get-tuple-element.18), channel_id=1, source_target_pairs={{0,1},{1,0},{2,3},{3,2},{4,5},{5,4},{6,7},{7,6},{8,9},{9,8},{10,11... | collective-permute-start | bytes 122888 | tf_op jit(solution)/shard_map/ppermute | solution.py:475
  28.5 7.9 %collective-permute-start.5 = (f32[5,16,128]{2,1,0:T(8,128)S(1)}, f32[5,16,128]{2,1,0:T(8,128)S(1)}, u32[]{:S(2)}, u32[]{:S(2)}) collective-permute-start(f32[5,16,128]{2,1,0:T(8,128)S(1)} %get-tuple-element.19), channel_id=1, source_target_pairs={{1,2},{2,1},{5,6},{6,5},{9,10},{10,9},{13,14},{14,13},{17,18},{18,... | collective-permute-start | bytes 122888 | tf_op jit(solution)/shard_map/ppermute | solution.py:475
  29.2 7.2 %collective-permute-start = (f32[5,8,128]{2,1,0:T(8,128)S(1)}, f32[5,8,128]{2,1,0:T(8,128)S(1)}, u32[]{:S(2)}, u32[]{:S(2)}) collective-permute-start(f32[5,8,128]{2,1,0:T(8,128)S(1)} %get-tuple-element.15), channel_id=1, source_target_pairs={{0,64},{64,0},{128,192},{192,128},{256,320},{320,256},{384,448},{4... | collective-permute-start | bytes 61448 | tf_op jit(solution)/shard_map/ppermute | solution.py:475
  36.4 24.6 %copy-start.2 = (bf16[512,768]{1,0:T(8,128)(2,1)S(1)}, bf16[512,768]{1,0:T(8,128)(2,1)}, u32[]{:S(2)}) copy-start(bf16[512,768]{1,0:T(8,128)(2,1)} %constant.10.clone.refs_3_) | copy-start | bytes 2359300
  36.4 24.6 %copy-start.3 = (f32[1,16,1,3,2048]{4,2,3,1,0:T(1,128)S(1)}, f32[1,16,1,3,2048]{4,2,3,1,0:T(1,128)}, u32[]{:S(2)}) copy-start(f32[1,16,1,3,2048]{4,2,3,1,0:T(1,128)} %param.16) | copy-start | bytes 1179652
  36.4 24.6 %copy-start.4 = (s32[1,16,1,2048]{3,2,1,0:T(1,128)S(1)}, s32[1,16,1,2048]{3,2,1,0:T(1,128)}, u32[]{:S(2)}) copy-start(s32[1,16,1,2048]{3,2,1,0:T(1,128)} %refs_11_.1) | copy-start | bytes 393220
  36.5 24.6 %copy-start.5 = (f32[3,64,32]{1,2,0:T(8,128)S(1)}, f32[3,64,32]{1,2,0:T(8,128)}, u32[]{:S(2)}) copy-start(f32[3,64,32]{1,2,0:T(8,128)} %param.18) | copy-start | bytes 73732
  36.5 24.6 %copy-start.6 = (s32[1,1,1,2048]{3,2,1,0:T(1,128)S(1)}, s32[1,1,1,2048]{3,2,1,0:T(1,128)}, u32[]{:S(2)}) copy-start(s32[1,1,1,2048]{3,2,1,0:T(1,128)} %param.15) | copy-start | bytes 24580
  42.1 18.9 %all-to-all-start.1 = ((f32[8,56,128]{2,1,0:T(8,128)}), f32[8,56,128]{2,1,0:T(8,128)S(1)}, u32[]{:S(2)}, u32[]{:S(2)}) async-start(f32[8,56,128]{2,1,0:T(8,128)} %get-tuple-element.21), calls=%async_computation.1 | async-start | bytes 458752 | tf_op jit(solution)/shard_map/all_to_all | solution.py:543
  48.1 12.9 %collective-permute-start.6 = (f32[5,32,128]{2,1,0:T(8,128)S(1)}, f32[5,32,128]{2,1,0:T(8,128)S(1)}, u32[]{:S(2)}, u32[]{:S(2)}) collective-permute-start(f32[5,32,128]{2,1,0:T(8,128)S(1)} %get-tuple-element.22), channel_id=1, source_target_pairs={{0,4},{4,0},{8,12},{12,8},{16,20},{20,16},{24,28},{28,24},{32,36},... | collective-permute-start | bytes 245768 | tf_op jit(solution)/shard_map/ppermute | solution.py:475
  52.0 9.0 %collective-permute-start.7 = (f32[5,32,128]{2,1,0:T(8,128)S(1)}, f32[5,32,128]{2,1,0:T(8,128)S(1)}, u32[]{:S(2)}, u32[]{:S(2)}) collective-permute-start(f32[5,32,128]{2,1,0:T(8,128)S(1)} %get-tuple-element.23), channel_id=1, source_target_pairs={{4,8},{8,4},{12,16},{16,12},{20,24},{24,20},{28,32},{32,28},{36,40... | collective-permute-start | bytes 245768 | tf_op jit(solution)/shard_map/ppermute | solution.py:475
  54.4 6.6 %collective-permute-start.8 = (f32[5,16,128]{2,1,0:T(8,128)S(1)}, f32[5,16,128]{2,1,0:T(8,128)S(1)}, u32[]{:S(2)}, u32[]{:S(2)}) collective-permute-start(f32[5,16,128]{2,1,0:T(8,128)S(1)} %get-tuple-element.24), channel_id=1, source_target_pairs={{0,1},{1,0},{2,3},{3,2},{4,5},{5,4},{6,7},{7,6},{8,9},{9,8},{10,11... | collective-permute-start | bytes 122888 | tf_op jit(solution)/shard_map/ppermute | solution.py:475
  59.7 1.4 %collective-permute-start.9 = (f32[5,16,128]{2,1,0:T(8,128)S(1)}, f32[5,16,128]{2,1,0:T(8,128)S(1)}, u32[]{:S(2)}, u32[]{:S(2)}) collective-permute-start(f32[5,16,128]{2,1,0:T(8,128)S(1)} %get-tuple-element.25), channel_id=1, source_target_pairs={{1,2},{2,1},{5,6},{6,5},{9,10},{10,9},{13,14},{14,13},{17,18},{18,... | collective-permute-start | bytes 122888 | tf_op jit(solution)/shard_map/ppermute | solution.py:475
